TPU v7x, 128 devices: a whole 4x4x4 slice. The times are simulated.
128 devices in a mesh: blk: 16 (over x_lo, y, core), grp: 8 (over z, x_hi).
Axes of the slice: x: 4 (x_hi: 2, x_lo: 2; x = x_hi * 2 + x_lo), y: 4, z: 4, core: 2. Of those that a mesh axis runs over, the one named last changes fastest.
Arguments:
- inverse: bfloat16 [2, 16, 1024, 1024], P(None, 'blk', 'grp'), may hold values from -0.0034375 to 0.1734375
- excite: bfloat16 [2, 16, 1024, 128], P(None, 'blk'), may hold values from -0.125 to 0.125
- coordinates: int32 [3, 16, 1024], replicated, may hold values from 0 to 31, as said below
- block_of_slot: int32 [16], replicated, may hold values from 0 to 15, each once
- panel_order: int32 [16], replicated, may hold values from 0 to 15, each once
Outputs:
- reduced: float32 [2, 2048, 2048], P(None, 'blk', 'grp')
- schur: float32 [2, 2048, 2048], P(None, 'blk', 'grp')
Inputs may be any that keep to these rules, and one draw needn't show every extreme that they name: `coordinates`: components 0 and 1 lie in 0 to 31, component 2 in 0 to 31. No two unknowns of any blocks share a lattice point. `block_of_slot`: slot s is the (s mod 1)-th block of index s // 1 of blk; every block number appears once. `panel_order`: every block number appears once; the first 2 are eliminated in that order, without pivoting.
All inputs are finite; a program needn't handle non-finite values.
Results may differ from a plain program's by a relative error of at most 0.0055.
Values may be sent and summed in bfloat16 or wider, within the bound.
No kernel may reach another device: no remote copies, remote signals or barrier semaphores. Data moves between devices by JAX's collectives and lax.ppermute only.
A program may use at most 64 MiB of HBM per device.

v0:
```python
import jax
import jax.numpy as jnp
from jax import lax
from jax.sharding import PartitionSpec as P

PANELS = 2


SELF_REAL = 12.0
SELF_IMAG = -3.0
COUPLE = 2.0
WAVE = 1.3


def sent_to_all(x, axis):
    copies = jnp.broadcast_to(x, (lax.axis_size(axis), *x.shape))
    return lax.all_to_all(copies, axis, split_axis=0, concat_axis=0, tiled=True)


def joined_along(tiles, dim):
    tiles = jnp.moveaxis(tiles, 0, dim)
    lengths = tiles.shape
    return tiles.reshape(*lengths[:dim], lengths[dim] * lengths[dim + 1], *lengths[dim + 2 :])


def collect(x, axis, dim):
    tiles = sent_to_all(x, axis)
    return joined_along(tiles, dim)


def from_root(x, axis, root):
    return lax.dynamic_index_in_dim(lax.all_gather(x, axis), root, 0, keepdims=False)


def green_tile(test_pos, basis_pos):
    squared = jnp.zeros((test_pos.shape[1], basis_pos.shape[1]), jnp.int32)
    for which in range(3):
        spacing = test_pos[which][:, None] - basis_pos[which][None, :]
        squared = squared + spacing * spacing
    coincide = squared == 0
    distance = jnp.sqrt(jnp.maximum(squared, 1).astype(jnp.float32))
    scaled = COUPLE / distance
    angle_term = WAVE * distance
    real_part = jnp.where(coincide, jnp.float32(SELF_REAL), scaled * jnp.cos(angle_term))
    imag_part = jnp.where(coincide, jnp.float32(SELF_IMAG), -scaled * jnp.sin(angle_term))
    return (real_part.astype(jnp.bfloat16), imag_part.astype(jnp.bfloat16))


def solve_pivot(pivot, right):
    upper_bound = lax.Precision.HIGHEST
    funcs = pivot.shape[1]
    top = jnp.concatenate([pivot[0], -pivot[1]], axis=1)
    lower = jnp.concatenate([pivot[1], pivot[0]], axis=1)
    real_form = jnp.concatenate([top, lower], axis=0)
    stacked = jnp.concatenate([right[0], right[1]], axis=0)
    normal = jnp.dot(real_form.T, real_form, precision=upper_bound)
    factor = jnp.linalg.cholesky(normal)
    answer = jax.scipy.linalg.cho_solve(
        (factor, True), jnp.dot(real_form.T, stacked, precision=upper_bound)
    )
    misfit = stacked - jnp.dot(real_form, answer, precision=upper_bound)
    answer = answer + jax.scipy.linalg.cho_solve(
        (factor, True), jnp.dot(real_form.T, misfit, precision=upper_bound)
    )
    return (answer[:funcs], answer[funcs:])


def on_device(inverse, excite, coordinates, block_of_slot, panel_order):
    upper_bound = lax.Precision.HIGHEST
    per_dev = inverse.shape[1]
    funcs = excite.shape[3]
    blocks = block_of_slot.shape[0]
    block_number = lax.axis_index("blk")
    grp_index = lax.axis_index("grp")
    own_slots = block_number * per_dev + jnp.arange(per_dev, dtype=jnp.int32)
    own_ids = jnp.take(block_of_slot, own_slots)
    rows_real = jnp.einsum(
        "sur,src->suc", inverse[0], excite[0], preferred_element_type=jnp.float32
    ) - jnp.einsum("sur,src->suc", inverse[1], excite[1], preferred_element_type=jnp.float32)
    rows_imag = jnp.einsum(
        "sur,src->suc", inverse[0], excite[1], preferred_element_type=jnp.float32
    ) + jnp.einsum("sur,src->suc", inverse[1], excite[0], preferred_element_type=jnp.float32)
    basis_rows = jnp.stack([rows_real, rows_imag]).astype(jnp.bfloat16)
    own_full = collect(basis_rows, "grp", 2)
    own_pos = jnp.take(coordinates, own_ids, axis=1)
    sliced = collect(basis_rows, "blk", 1)
    slot_list = jnp.arange(blocks, dtype=jnp.int32)
    matches = block_of_slot[None, :] == slot_list[:, None]
    slot_of_block = jnp.sum(jnp.where(matches, slot_list[None, :], 0), axis=1)
    grouped_per_block = jnp.take(sliced, slot_of_block, axis=1)
    slab = lax.all_to_all(grouped_per_block, "grp", split_axis=1, concat_axis=2, tiled=True)
    slab_count = slab.shape[1]
    own_test = own_full.astype(jnp.float32)
    start_table = jnp.zeros((2, per_dev * funcs, slab_count * funcs), jnp.float32)

    def one_pair(index, carried):
        test_slot = index // slab_count
        slab_slot = index % slab_count
        test_pos = lax.dynamic_index_in_dim(own_pos, test_slot, 1, keepdims=False)
        basis_pos = lax.dynamic_index_in_dim(
            coordinates, grp_index * slab_count + slab_slot, 1, keepdims=False
        )
        greens_function_real, greens_function_imaginary = green_tile(test_pos, basis_pos)
        basis = lax.dynamic_index_in_dim(slab, slab_slot, 1, keepdims=False)
        product_real = jnp.dot(
            greens_function_real, basis[0], preferred_element_type=jnp.float32
        ) - jnp.dot(greens_function_imaginary, basis[1], preferred_element_type=jnp.float32)
        product_imaginary = jnp.dot(
            greens_function_real, basis[1], preferred_element_type=jnp.float32
        ) + jnp.dot(greens_function_imaginary, basis[0], preferred_element_type=jnp.float32)
        tested = lax.dynamic_index_in_dim(own_test, test_slot, 1, keepdims=False)
        coupled_real = jnp.dot(tested[0].T, product_real, precision=upper_bound) + jnp.dot(
            tested[1].T, product_imaginary, precision=upper_bound
        )
        coupled_imag = jnp.dot(tested[0].T, product_imaginary, precision=upper_bound) - jnp.dot(
            tested[1].T, product_real, precision=upper_bound
        )
        placed = jnp.stack([coupled_real, coupled_imag])
        return lax.dynamic_update_slice(carried, placed, (0, test_slot * funcs, slab_slot * funcs))

    reduced = lax.fori_loop(0, per_dev * slab_count, one_pair, start_table)
    col_blocks = reduced.shape[2] // funcs
    slot_numbers = jnp.arange(blocks, dtype=jnp.int32)
    system_matrix = reduced
    for step in range(PANELS):
        pivot_id = panel_order[step]
        slot_pos = jnp.sum(jnp.where(block_of_slot == pivot_id, slot_numbers, 0))
        owner = slot_pos // per_dev
        local_row = slot_pos % per_dev
        col_owner = pivot_id // col_blocks
        local_col = pivot_id % col_blocks
        upper = system_matrix
        upper = from_root(upper, "blk", owner)
        column = lax.dynamic_slice_in_dim(system_matrix, local_col * funcs, funcs, 2)
        pivot = lax.dynamic_slice_in_dim(upper, local_col * funcs, funcs, 2)
        column, pivot = (from_root(column, "grp", col_owner), from_root(pivot, "grp", col_owner))
        sol_real, sol_imag = solve_pivot(pivot, upper)
        upd_real = jnp.dot(column[0], sol_real, precision=upper_bound) - jnp.dot(
            column[1], sol_imag, precision=upper_bound
        )
        upd_imag = jnp.dot(column[0], sol_imag, precision=upper_bound) + jnp.dot(
            column[1], sol_real, precision=upper_bound
        )
        system_matrix = system_matrix - jnp.stack([upd_real, upd_imag])
    return (reduced, system_matrix)


def solution(mesh):
    placed = (P(None, "blk", "grp", None), P(None, "blk", None, None), P(), P(), P())
    return jax.shard_map(
        on_device,
        mesh=mesh,
        in_specs=placed,
        out_specs=(P(None, "blk", "grp"), P(None, "blk", "grp")),
        check_vma=False,
    )
```

profile of v0, /device:TPU:0, one launch (start us, length us, event | category | flops | bytes accessed | tf_op | source)
XLA Modules:
  0.0 565.9 jit_solution(489426940338771536)
XLA Ops:
  7.2 1.2 fusion.30
  8.4 1.2 fusion.36
  9.7 1.2 fusion.26
  10.9 1.2 fusion.27
  12.2 1.2 broadcast_in_dim.83
  13.4 5.6 all-to-all-start
  19.2 16.4 %all-to-all-done = bf16[16,2,1,128,128]{4,3,1,2,0:T(8,128)(2,1)S(1)} async-done(((bf16[16,2,1,128,128]{4,3,1,2,0:T(8,128)(2,1)}), bf16[16,2,1,128,128]{4,3,1,2,0:T(8,128)(2,1)S(1)}, u32[]{:S(2)}, u32[]{:S(2)}) %all-to-all-start) | async-done | bytes 1048608 | tf_op jit(solution)/shard_map/all_to_all | solution.py:17
  36.5 7.5 %all-to-all-start.2 = ((bf16[8,2,1,128,128]{4,3,1,2,0:T(8,128)(2,1)}), bf16[8,2,1,128,128]{4,3,1,2,0:T(8,128)(2,1)S(1)}, u32[]{:S(2)}, u32[]{:S(2)}) async-start(bf16[8,2,1,128,128]{4,3,1,2,0:T(8,128)(2,1)} %broadcast_in_dim.85), calls=%async_computation.2 | async-start | bytes 1048576 | tf_op jit(solution)/shard_map/all_to_all | solution.py:17
  44.8 1.1 select_bitcast_fusion
  46.0 9.3 %all-to-all-done.2 = bf16[8,2,1,128,128]{4,3,1,2,0:T(8,128)(2,1)S(1)} async-done(((bf16[8,2,1,128,128]{4,3,1,2,0:T(8,128)(2,1)}), bf16[8,2,1,128,128]{4,3,1,2,0:T(8,128)(2,1)S(1)}, u32[]{:S(2)}, u32[]{:S(2)}) %all-to-all-start.2) | async-done | bytes 524320 | tf_op jit(solution)/shard_map/all_to_all | solution.py:17
  55.3 3.6 all-to-all-start.1
  61.2 13.7 %all-to-all-done.1 = bf16[2,16,128,128]{3,2,0,1:T(8,128)(2,1)S(1)} async-done(((bf16[2,16,128,128]{3,2,0,1:T(8,128)(2,1)}), bf16[2,16,128,128]{3,2,0,1:T(8,128)(2,1)S(1)}, u32[]{:S(2)}, u32[]{:S(2)}) %all-to-all-start.1) | async-done | bytes 1048608 | tf_op jit(solution)/shard_map/all_to_all | solution.py:91
  75.0 168.6 %while.25 = (s32[]{:T(128)}, f32[2,128,256]{2,1,0:T(8,128)S(1)}, s32[3,1,1024]{2,1,0:T(1,128)S(1)}, s32[]{:T(128)}, s32[3,16,1024]{2,1,0:T(8,128)}, /*index=5*/b...) while((s32[]{:T(128)}, f32[2,128,256]{2,1,0:T(8,128)S(1)}, ...), condition=%wide.region_2.3_spmd, body=%wide.region_1.2_spmd.sunk | while | flops 1948581888 | bytes 9716109 | solution.py:121
  76.3 17.6 %fusion.179 = f32[1024,128]{1,0:T(8,128)S(1)} fusion(bf16[2,2,1024,128]{3,2,1,0:T(8,128)(2,1)S(1)} %get-tuple-element.479, s32[]{:T(128)S(6)} %add.377, s32[]{:T(128)S(6)} %select_n.264, s32[1024]{0:T(1024)S(1)} %bitcast.286, s32[1024]{0:T(1024)S(1)} %bitcast.294, s32[1024]{0:T(1024)S(1)} %bitcast.282, s32[1024]{0:T(1024)S(1)} %bitcast.290, ...), kind=kOutput, calls=%fused_computation.26.clone.1 | convolution fusion | flops 285212672 | bytes 811016 | tf_op jit(solution)/shard_map/while/body/eval_jaxpr/dot_general | solution.py:108
  93.9 17.9 %convolution_add_fusion.6 = f32[1024,128]{1,0:T(8,128)S(1)} fusion(f32[1024,128]{1,0:T(8,128)S(1)} %fusion.179, bf16[2,2,1024,128]{3,2,1,0:T(8,128)(2,1)S(1)} %get-tuple-element.479, s32[]{:T(128)S(6)} %select_n.264, s32[1024]{0:T(1024)S(1)} %bitcast.287, s32[1024]{0:T(1024)S(1)} %bitcast.295, s32[1024]{0:T(1024)S(1)} %bitcast.283, ...), kind=kOutput, calls=%fused_computation.7.clone.1 | convolution fusion | flops 286392320 | bytes 1335300 | tf_op jit(solution)/shard_map/while/body/eval_jaxpr/dot_general | solution.py:110
  112.9 17.6 %fusion.181 = f32[1024,128]{1,0:T(8,128)S(1)} fusion(bf16[2,2,1024,128]{3,2,1,0:T(8,128)(2,1)S(1)} %get-tuple-element.479, s32[]{:T(128)S(6)} %select_n.264, s32[1024]{0:T(1024)S(1)} %bitcast.288, s32[1024]{0:T(1024)S(1)} %bitcast.296, s32[1024]{0:T(1024)S(1)} %bitcast.284, s32[1024]{0:T(1024)S(1)} %bitcast.292, s32[1024]{0:T(1024)S(1)} %bitcast.280, ...), kind=kOutput, calls=%fused_computation.25.clone.1 | convolution fusion | flops 285212672 | bytes 811012 | tf_op jit(solution)/shard_map/while/body/eval_jaxpr/dot_general | solution.py:105
  130.5 18.2 %convolution_subtract_fusion.18 = f32[1024,128]{1,0:T(8,128)S(1)} fusion(f32[1024,128]{1,0:T(8,128)S(1)} %fusion.181, bf16[2,2,1024,128]{3,2,1,0:T(8,128)(2,1)S(1)} %get-tuple-element.479, s32[]{:T(128)S(6)} %add.377, s32[]{:T(128)S(6)} %select_n.264, s32[1024]{0:T(1024)S(1)} %bitcast.289, s32[1024]{0:T(1024)S(1)} %bitcast.297, ...), kind=kOutput, calls=%fused_computation.8.clone.1 | convolution fusion | flops 286392320 | bytes 1335304 | tf_op jit(solution)/shard_map/while/body/eval_jaxpr/dot_general | solution.py:107
  156.4 17.6 %fusion.179 = f32[1024,128]{1,0:T(8,128)S(1)} fusion(bf16[2,2,1024,128]{3,2,1,0:T(8,128)(2,1)S(1)} %get-tuple-element.479, s32[]{:T(128)S(6)} %add.377, s32[]{:T(128)S(6)} %select_n.264, s32[1024]{0:T(1024)S(1)} %bitcast.286, s32[1024]{0:T(1024)S(1)} %bitcast.294, s32[1024]{0:T(1024)S(1)} %bitcast.282, s32[1024]{0:T(1024)S(1)} %bitcast.290, ...), kind=kOutput, calls=%fused_computation.26.clone.1 | convolution fusion | flops 285212672 | bytes 811016 | tf_op jit(solution)/shard_map/while/body/eval_jaxpr/dot_general | solution.py:108
  174.0 17.9 %convolution_add_fusion.6 = f32[1024,128]{1,0:T(8,128)S(1)} fusion(f32[1024,128]{1,0:T(8,128)S(1)} %fusion.179, bf16[2,2,1024,128]{3,2,1,0:T(8,128)(2,1)S(1)} %get-tuple-element.479, s32[]{:T(128)S(6)} %select_n.264, s32[1024]{0:T(1024)S(1)} %bitcast.287, s32[1024]{0:T(1024)S(1)} %bitcast.295, s32[1024]{0:T(1024)S(1)} %bitcast.283, ...), kind=kOutput, calls=%fused_computation.7.clone.1 | convolution fusion | flops 286392320 | bytes 1335300 | tf_op jit(solution)/shard_map/while/body/eval_jaxpr/dot_general | solution.py:110
  192.9 17.6 %fusion.181 = f32[1024,128]{1,0:T(8,128)S(1)} fusion(bf16[2,2,1024,128]{3,2,1,0:T(8,128)(2,1)S(1)} %get-tuple-element.479, s32[]{:T(128)S(6)} %select_n.264, s32[1024]{0:T(1024)S(1)} %bitcast.288, s32[1024]{0:T(1024)S(1)} %bitcast.296, s32[1024]{0:T(1024)S(1)} %bitcast.284, s32[1024]{0:T(1024)S(1)} %bitcast.292, s32[1024]{0:T(1024)S(1)} %bitcast.280, ...), kind=kOutput, calls=%fused_computation.25.clone.1 | convolution fusion | flops 285212672 | bytes 811012 | tf_op jit(solution)/shard_map/while/body/eval_jaxpr/dot_general | solution.py:105
  210.6 18.1 %convolution_subtract_fusion.18 = f32[1024,128]{1,0:T(8,128)S(1)} fusion(f32[1024,128]{1,0:T(8,128)S(1)} %fusion.181, bf16[2,2,1024,128]{3,2,1,0:T(8,128)(2,1)S(1)} %get-tuple-element.479, s32[]{:T(128)S(6)} %add.377, s32[]{:T(128)S(6)} %select_n.264, s32[1024]{0:T(1024)S(1)} %bitcast.289, s32[1024]{0:T(1024)S(1)} %bitcast.297, ...), kind=kOutput, calls=%fused_computation.8.clone.1 | convolution fusion | flops 286392320 | bytes 1335304 | tf_op jit(solution)/shard_map/while/body/eval_jaxpr/dot_general | solution.py:107
  245.0 2.0 fusion.109
  251.0 27.5 %all-gather.17.cloned.1.call-done = f32[32,128,256]{2,1,0:T(8,128)} async-done(((f32[2,128,256]{2,1,0:T(8,128)}), f32[32,128,256]{2,1,0:T(8,128)}) %all-gather.17.cloned.1.call-update) | async-done | bytes 4194320 | tf_op jit(solution)/shard_map/all_gather | solution.py:32
  278.5 1.7 constant_dynamic-slice_fusion.7
  281.0 1.6 constant_dynamic-slice_fusion.8
  283.7 44.2 %all-gather.11.cloned.1.call-done = f32[8,2,128,128]{3,2,1,0:T(8,128)} async-done(((f32[1,2,128,128]{3,2,1,0:T(8,128)}), f32[8,2,128,128]{3,2,1,0:T(8,128)}) %all-gather.11.cloned.1.call-update) | async-done | bytes 1048592 | tf_op jit(solution)/shard_map/all_gather | solution.py:32
  330.3 11.7 %cholesky.130 = f32[128,128]{1,0:T(8,128)S(1)} custom-call(f32[128,128]{1,0:T(8,128)S(1)} %cholesky.194), custom_call_target="Cholesky" | custom-call | tf_op jit(solution)/shard_map/jit(cholesky)/cholesky | solution.py:57
  342.1 9.8 %custom-call.17 = f32[1,128,128]{1,2,0:T(8,128)S(1)} custom-call(f32[1,128,128]{2,1,0:T(8,128)S(1)} %get-tuple-element.322), custom_call_target="InvertDiagBlocksLowerTriangular" | custom-call | tf_op jit(solution)/shard_map/jit(cholesky)/cholesky | solution.py:57
  352.4 11.7 %cholesky.147 = f32[128,128]{1,0:T(8,128)S(1)} custom-call(f32[128,128]{1,0:T(8,128)S(1)} %convolution_subtract_fusion.15), custom_call_target="Cholesky" | custom-call | tf_op jit(solution)/shard_map/jit(cholesky)/cholesky | solution.py:57
  366.3 4.4 while.26
  367.3 1.4 bitcast_dynamic-update-slice_fusion.4
  369.3 1.4 bitcast_dynamic-update-slice_fusion.4
  370.7 19.7 %custom-call.18 = f32[2,128,128]{1,2,0:T(8,128)S(1)} custom-call(f32[2,128,128]{2,1,0:T(8,128)S(1)} %get-tuple-element.232), custom_call_target="InvertDiagBlocksLowerTriangular" | custom-call | tf_op jit(solution)/shard_map/jit(_cho_solve)/triangular_solve | solution.py:58
  396.7 1.1 fusion.68
  398.9 1.1 fusion.23
  404.4 32.4 %all-gather.21.cloned.1.call-done = f32[32,128,256]{2,1,0:T(8,128)} async-done(((f32[2,128,256]{2,1,0:T(8,128)}), f32[32,128,256]{2,1,0:T(8,128)}) %all-gather.21.cloned.1.call-update) | async-done | bytes 4194320 | tf_op jit(solution)/shard_map/all_gather | solution.py:32
  436.9 1.7 constant_dynamic-slice_fusion.5
  439.5 1.6 constant_dynamic-slice_fusion.6
  442.1 43.4 %all-gather.13.cloned.1.call-done = f32[8,2,128,128]{3,2,1,0:T(8,128)} async-done(((f32[1,2,128,128]{3,2,1,0:T(8,128)}), f32[8,2,128,128]{3,2,1,0:T(8,128)}) %all-gather.13.cloned.1.call-update) | async-done | bytes 1048592 | tf_op jit(solution)/shard_map/all_gather | solution.py:32
  488.0 11.7 %cholesky.164 = f32[128,128]{1,0:T(8,128)S(1)} custom-call(f32[128,128]{1,0:T(8,128)S(1)} %cholesky.197), custom_call_target="Cholesky" | custom-call | tf_op jit(solution)/shard_map/jit(cholesky)/cholesky | solution.py:57
  499.8 9.8 %custom-call.20 = f32[1,128,128]{1,2,0:T(8,128)S(1)} custom-call(f32[1,128,128]{2,1,0:T(8,128)S(1)} %get-tuple-element.318), custom_call_target="InvertDiagBlocksLowerTriangular" | custom-call | tf_op jit(solution)/shard_map/jit(cholesky)/cholesky | solution.py:57
  510.1 11.7 %cholesky.181 = f32[128,128]{1,0:T(8,128)S(1)} custom-call(f32[128,128]{1,0:T(8,128)S(1)} %convolution_subtract_fusion.14), custom_call_target="Cholesky" | custom-call | tf_op jit(solution)/shard_map/jit(cholesky)/cholesky | solution.py:57
  524.5 4.2 while.27
  525.3 1.4 bitcast_dynamic-update-slice_fusion.5
  527.3 1.4 bitcast_dynamic-update-slice_fusion.5
  528.7 19.7 %custom-call.21 = f32[2,128,128]{1,2,0:T(8,128)S(1)} custom-call(f32[2,128,128]{2,1,0:T(8,128)S(1)} %get-tuple-element.234), custom_call_target="InvertDiagBlocksLowerTriangular" | custom-call | tf_op jit(solution)/shard_map/jit(_cho_solve)/triangular_solve | solution.py:58
  553.6 1.1 fusion.58
  556.9 1.1 fusion.21
  (133 shorter events, 44.1 us)
Async XLA Ops:
  7.2 11.9 %copy-start.3 = (s32[16]{0:T(128)S(1)}, s32[16]{0:T(128)}, u32[]{:S(2)}) copy-start(s32[16]{0:T(128)} %param.13) | copy-start | bytes 196
  13.4 22.2 %all-to-all-start = ((bf16[16,2,1,128,128]{4,3,1,2,0:T(8,128)(2,1)}), bf16[16,2,1,128,128]{4,3,1,2,0:T(8,128)(2,1)S(1)}, u32[]{:S(2)}, u32[]{:S(2)}) async-start(bf16[16,2,1,128,128]{4,3,1,2,0:T(8,128)(2,1)} %broadcast_in_dim.83), calls=%async_computation | async-start | bytes 2097152 | tf_op jit(solution)/shard_map/all_to_all | solution.py:17
  36.5 18.8 %all-to-all-start.2 = ((bf16[8,2,1,128,128]{4,3,1,2,0:T(8,128)(2,1)}), bf16[8,2,1,128,128]{4,3,1,2,0:T(8,128)(2,1)S(1)}, u32[]{:S(2)}, u32[]{:S(2)}) async-start(bf16[8,2,1,128,128]{4,3,1,2,0:T(8,128)(2,1)} %broadcast_in_dim.85), calls=%async_computation.2 | async-start | bytes 1048576 | tf_op jit(solution)/shard_map/all_to_all | solution.py:17
  55.3 19.6 %all-to-all-start.1 = ((bf16[2,16,128,128]{3,2,0,1:T(8,128)(2,1)}), bf16[2,16,128,128]{3,2,0,1:T(8,128)(2,1)S(1)}, u32[]{:S(2)}, u32[]{:S(2)}) async-start(bf16[2,16,128,128]{3,2,0,1:T(8,128)(2,1)} %select_bitcast_fusion), calls=%async_computation.1 | async-start | bytes 2097152 | tf_op jit(solution)/shard_map/all_to_all | solution.py:91
  58.8 219.7 %all-gather.17.cloned.1.call-start = ((), (), s32[]{:S(2)}) async-start(), calls=%async_computation.6 | async-start | bytes 4456448 | tf_op jit(solution)/shard_map/all_gather | solution.py:32
  75.0 169.4 %copy-start.2 = (s32[16]{0:T(128)S(1)}, s32[16]{0:T(128)}, u32[]{:S(2)}) copy-start(s32[16]{0:T(128)} %param.14) | copy-start | bytes 196
  75.0 170.0 %copy-start.4 = (s32[16]{0:T(128)S(1)}, s32[16]{0:T(128)}, u32[]{:S(2)}) copy-start(s32[16]{0:T(128)} %param.13) | copy-start | bytes 196
  243.6 0.7 copy-start
  244.3 83.5 %all-gather.11.cloned.1.call-start = ((), (), s32[]{:S(2)}) async-start(), calls=%async_computation.3 | async-start | bytes 1179648 | tf_op jit(solution)/shard_map/all_gather | solution.py:32
  280.2 115.3 %all-gather.15.cloned.1.call-start = ((), (), s32[]{:S(2)}) async-start(), calls=%async_computation.5 | async-start | bytes 1179648 | tf_op jit(solution)/shard_map/all_gather | solution.py:32
  282.6 154.2 %all-gather.21.cloned.1.call-start = ((), (), s32[]{:S(2)}) async-start(), calls=%async_computation.8 | async-start | bytes 4456448 | tf_op jit(solution)/shard_map/all_gather | solution.py:32
  391.0 9.1 %copy-start.1 = (f32[2,128,256]{2,1,0:T(8,128)S(1)}, f32[2,128,256]{2,1,0:T(8,128)}, u32[]{:S(2)}) copy-start(f32[2,128,256]{2,1,0:T(8,128)} %copy-done) | copy-start | bytes 786436
  400.8 84.7 %all-gather.13.cloned.1.call-start = ((), (), s32[]{:S(2)}) async-start(), calls=%async_computation.4 | async-start | bytes 1179648 | tf_op jit(solution)/shard_map/all_gather | solution.py:32
  438.6 115.0 %all-gather.19.cloned.1.call-start = ((), (), s32[]{:S(2)}) async-start(), calls=%async_computation.7 | async-start | bytes 1179648 | tf_op jit(solution)/shard_map/all_gather | solution.py:32
Sparse Core Ops, SparseCore 0:
  244.5 34.0 all-gather.16
  281.4 46.3 all-gather.10
  330.2 45.3 all-gather.14
  400.9 35.8 all-gather.20
  439.1 46.4 all-gather.12
  487.7 45.2 all-gather.18
where the time goes:
time: 570 us; the launch traced here: 566 us
  waiting for transfers between devices  187 us (33%)
  matrix products  177 us (31%)
  other arithmetic  116 us (20%)
  between operations  27.2 us (5%)
  local copies, waits for them, and re-layouts  25.3 us (4%)
  starting transfers between devices  17.1 us (3%)
  loops' own time  16.8 us (3%)
    all_gather x6, waiting for transfers between devices, from_root(): lax.all_gather(x, axis)  148 us
    another operation x13, other arithmetic, solve_pivot(): factor = jnp.linalg.cholesky(normal)  68.7 us
    another operation x5, other arithmetic, solve_pivot(): jax.scipy.linalg.cho_solve((factor, True), jnp.dot(real_form.T, stacked,...  39.4 us
    dot_general x2, matrix products, one_pair(): jnp.dot(greens_function_imaginary, basis[1], preferred_element_type=jnp.f...  36.3 us
    dot_general x2, matrix products, one_pair(): jnp.dot(greens_function_imaginary, basis[0], preferred_element_type=jnp.f...  35.8 us
    dot_general x2, matrix products, one_pair(): jnp.dot(greens_function_real, basis[0], preferred_element_type=jnp.float32)  35.2 us
    dot_general x2, matrix products, one_pair(): jnp.dot(greens_function_real, basis[1], preferred_element_type=jnp.float32)  35.2 us
    all_to_all x2, waiting for transfers between devices, sent_to_all(): return lax.all_to_all(copies, axis, split_axis=0, concat_axis=0, tiled=True)  25.7 us
  transfers between devices with their start and end apart: 9, of which 7 were waited for; matrix products, arithmetic and copies ran while one was open for 25% of the time, Pallas kernels for 0%

commit v1 on v0

v1 whole, which is shorter than its diff:
```python
import functools

import jax
import jax.numpy as jnp
import numpy as np
from jax import lax
from jax.experimental import pallas as pl
from jax.experimental.pallas import tpu as pltpu
from jax.sharding import PartitionSpec as P

PANELS = 2
bf16 = jnp.bfloat16
f32 = jnp.float32
i32 = jnp.int32

SELF_REAL = 6.0
SELF_IMAG = -1.5
TURNS = 1.3 / (2 * np.pi)
SHIFT = float(1.5 * 2**23)
SIN = (4.44288283, -7.30824115, 3.60628896, -0.8457636, 0.10920575)
COS = (-1.4142135, 6.97885099, -5.73946117, 1.88356298, -0.31069819)
VMEM = pl.BlockSpec(memory_space=pltpu.VMEM)
SMEM = pl.BlockSpec(memory_space=pltpu.SMEM)
MB = 1 << 20


def horner(coefs, g):
    r = coefs[-1]
    for k in coefs[-2::-1]:
        r = r * g + k
    return r


def half_green(sq):
    inv_r = lax.rsqrt(sq)
    turns = (sq * inv_r) * TURNS
    f = turns - ((turns + SHIFT) - SHIFT)
    g = f * f
    s = horner(SIN, g) * f
    c = horner(COS, g)
    return inv_r - (s * s) * inv_r, (s * c) * inv_r


def basis_kernel(core_ref, inv_ref, exc_ref, own_ref, keep_ref, send_ref):
    er, ei = exc_ref[0, 0], exc_ref[1, 0]
    j = jnp.dot(inv_ref[0, 0], jnp.concatenate([er, ei], 1), preferred_element_type=f32)
    j += jnp.dot(inv_ref[1, 0], jnp.concatenate([-ei, er], 1), preferred_element_type=f32)
    rows, cols = j.shape[0], j.shape[1] // 2
    half = rows // 2
    jb = j.astype(bf16)
    for g in range(own_ref.shape[0]):
        own_ref[g, 0] = jb[:, :cols]
        own_ref[g, 1] = jb[:, cols:]
    mine = pl.multiple_of(core_ref[0] * half, half)
    other = pl.multiple_of((1 - core_ref[0]) * half, half)
    for part in range(2):
        keep_ref[part] = own_ref[0, part, pl.ds(mine, half), :]
        send_ref[part] = own_ref[0, part, pl.ds(other, half), :]


def basis_rows(core, inverse, excite, copies):
    rows, cols = inverse.shape[2], excite.shape[3]
    half = jax.ShapeDtypeStruct((2, rows // 2, cols), bf16)
    return pl.pallas_call(
        basis_kernel,
        out_shape=(jax.ShapeDtypeStruct((copies, 2, rows, cols), bf16), half, half),
        in_specs=[SMEM, VMEM, VMEM],
        out_specs=(VMEM, VMEM, VMEM),
        name="basis",
    )(core, inverse, excite)


def green_kernel(left_ids, right_ids, fl_ref, fr_ref, g_ref, sq_ref):
    rows, cols = sq_ref.shape
    sq_ref[...] = lax.dot_general(
        fl_ref[0], fr_ref[0], (((0,), (0,)), ((), ())), preferred_element_type=f32
    )

    def strip(i, _):
        r = pl.ds(pl.multiple_of(i * 8, 8), 8)
        re, im = half_green(sq_ref[r, :])
        g_ref[0, 0, r, :] = re.astype(bf16)
        g_ref[0, 1, r, :] = im.astype(bf16)
        return 0

    lax.fori_loop(0, rows // 8, strip, 0, unroll=4)
    tile, chunk = pl.program_id(0), pl.program_id(1)

    @pl.when(left_ids[tile] == right_ids[tile])
    def _():
        at = pl.ds(pl.multiple_of(chunk * rows, rows), rows)
        same = lax.broadcasted_iota(i32, (rows, rows), 0) == lax.broadcasted_iota(i32, (rows, rows), 1)
        for part, value in ((0, SELF_REAL), (1, SELF_IMAG)):
            block = g_ref[0, part, :, at].astype(f32)
            g_ref[0, part, :, at] = jnp.where(same, value, block).astype(bf16)


def green_tiles(left_ids, right_ids, feat_left, feat_right, name):
    tiles, unk = left_ids.shape[0], feat_left.shape[2]
    rows = 256
    depth = feat_left.shape[1]
    return pl.pallas_call(
        green_kernel,
        out_shape=jax.ShapeDtypeStruct((tiles, 2, unk, unk), bf16),
        grid_spec=pltpu.PrefetchScalarGridSpec(
            num_scalar_prefetch=2,
            grid=(tiles, unk // rows),
            in_specs=[
                pl.BlockSpec((1, depth, rows), lambda t, m, le, ri: (le[t], 0, m)),
                pl.BlockSpec((1, depth, unk), lambda t, m, le, ri: (ri[t], 0, 0)),
            ],
            out_specs=pl.BlockSpec((1, 2, rows, unk), lambda t, m, le, ri: (t, 0, m, 0)),
            scratch_shapes=[pltpu.VMEM((rows, unk), f32)],
        ),
        compiler_params=pltpu.CompilerParams(vmem_limit_bytes=16 * MB),
        cost_estimate=pl.CostEstimate(
            flops=tiles * unk * unk * 30, transcendentals=tiles * unk * unk, bytes_accessed=tiles * unk * unk * 4
        ),
        name=name,
    )(left_ids, right_ids, feat_left, feat_right)


def features(coordinates):
    pos = coordinates.astype(i32)
    norm = jnp.sum(pos * pos, axis=0)
    low = norm % 64
    high = norm - low
    one, zero = jnp.ones_like(norm), jnp.zeros_like(norm)
    x, y, z = pos[0], pos[1], pos[2]
    pad = [zero] * 9
    left = jnp.stack([-2 * x, -2 * y, -2 * z, high, low, one, one] + pad, axis=1)
    right = jnp.stack([x, y, z, one, one, high, low] + pad, axis=1)
    return left.astype(bf16), right.astype(bf16)


def coupling_kernel(first, left_at, core_ref, g_ref, *refs):
    if left_at is None:
        own_ref, mine_ref, other_ref, out_ref, copies_ref, lhs, top, bottom, acc = refs
    else:
        mine_ref, other_ref, out_ref, lhs, top, bottom, acc = refs
    tile, chunk = pl.program_id(0), pl.program_id(1)
    chunks = pl.num_programs(1)
    core = core_ref[0]
    groups, _, _, half, cols = mine_ref.shape
    rows = g_ref.shape[2]

    def rows_of(g, part):
        return pl.ds(pl.multiple_of(g * 2 * half + part * half, half), half)

    @pl.when((tile == 0) & (chunk == 0))
    def _():
        if left_at is None:
            for g in range(groups):
                r = pl.ds(g * 2 * half, 2 * half)
                lhs[r, :cols] = own_ref[g, 0]
                lhs[r, cols:] = own_ref[g, 1]
        else:
            for g in range(groups):
                for src, part in ((mine_ref, core), (other_ref, 1 - core)):
                    r = rows_of(g, part)
                    lhs[r, :cols] = src[g, left_at + core, 0]
                    lhs[r, cols:] = src[g, left_at + core, 1]

    @pl.when(chunk == 0)
    def _():
        acc[...] = jnp.zeros_like(acc)
        for g in range(groups):
            for src, part in ((mine_ref, core), (other_ref, 1 - core)):
                r = rows_of(g, part)
                jr, ji = src[g, first + tile, 0], src[g, first + tile, 1]
                top[r, :cols] = jr
                top[r, cols:] = ji
                bottom[r, :cols] = -ji
                bottom[r, cols:] = jr

    y = jnp.dot(g_ref[0, 0], top[...], preferred_element_type=f32)
    y += jnp.dot(g_ref[0, 1], bottom[...], preferred_element_type=f32)
    y_hi = y.astype(bf16)
    y_lo = (y - y_hi.astype(f32)).astype(bf16)
    left = lhs[pl.ds(pl.multiple_of(chunk * rows, rows), rows), :]
    over_rows = (((0,), (0,)), ((), ()))
    acc[...] += lax.dot_general(left, y_hi, over_rows, preferred_element_type=f32) + lax.dot_general(
        left, y_lo, over_rows, preferred_element_type=f32
    )

    @pl.when(chunk == chunks - 1)
    def _():
        re = 2.0 * (acc[:cols, :cols] + acc[cols:, cols:])
        im = 2.0 * (acc[:cols, cols:] - acc[cols:, :cols])
        out_ref[0] = re
        out_ref[1] = im
        if left_at is None:
            for k in range(copies_ref.shape[0]):
                copies_ref[k, 0] = re.astype(bf16)
                copies_ref[k, 1] = im.astype(bf16)


def couplings(core, green, own, mine, other, first, left_at, name):
    tiles, _, unk, _ = green.shape
    cols = mine.shape[4]
    rows = 256
    copies = 8
    whole = lambda x: pl.BlockSpec(x.shape, lambda t, m: (0,) * x.ndim)
    args = ([own] if left_at is None else []) + [mine, other]
    out_shape = [jax.ShapeDtypeStruct((2, cols, tiles * cols), f32)]
    out_specs = [pl.BlockSpec((2, cols, cols), lambda t, m: (0, 0, t))]
    if left_at is None:
        out_shape.append(jax.ShapeDtypeStruct((copies, 2, cols, tiles * cols), bf16))
        out_specs.append(pl.BlockSpec((copies, 2, cols, cols), lambda t, m: (0, 0, 0, t)))
    return pl.pallas_call(
        functools.partial(coupling_kernel, first, left_at),
        out_shape=out_shape,
        grid=(tiles, unk // rows),
        in_specs=[SMEM, pl.BlockSpec((1, 2, rows, unk), lambda t, m: (t, 0, m, 0))] + [whole(x) for x in args],
        out_specs=out_specs,
        scratch_shapes=[
            pltpu.VMEM((unk, 2 * cols), bf16),
            pltpu.VMEM((unk, 2 * cols), bf16),
            pltpu.VMEM((unk, 2 * cols), bf16),
            pltpu.VMEM((2 * cols, 2 * cols), f32),
        ],
        compiler_params=pltpu.CompilerParams(vmem_limit_bytes=24 * MB),
        cost_estimate=pl.CostEstimate(
            flops=tiles * unk * unk * 2048, transcendentals=0, bytes_accessed=tiles * unk * unk * 4
        ),
        name=name,
    )(core, green, *args)


SIZE = 64


def turned(x):
    lane = lax.broadcasted_iota(i32, x.shape, x.ndim - 1)
    rolled = pltpu.roll(x, SIZE, x.ndim - 1)
    return jnp.where(lane < SIZE, -rolled, rolled)


def small_inverse(block):
    tiles = [block[8 * t : 8 * t + 8] for t in range(SIZE // 8)]
    lane = lax.broadcasted_iota(i32, (8, 2 * SIZE), 1)
    sub = lax.broadcasted_iota(i32, (8, 2 * SIZE), 0)
    lane1 = lax.broadcasted_iota(i32, (1, 2 * SIZE), 1)
    for k in range(SIZE):
        t, s = divmod(k, 8)
        cr = [jnp.broadcast_to(x[:, k : k + 1], x.shape) for x in tiles]
        ci = [jnp.broadcast_to(x[:, SIZE + k : SIZE + k + 1], x.shape) for x in tiles]
        pr, pi = cr[t][s : s + 1], ci[t][s : s + 1]
        scale = 1.0 / (pr * pr + pi * pi)
        qr, qi = pr * scale, -(pi * scale)
        row = tiles[t][s : s + 1]
        row = jnp.where(lane1 == k, 1.0, jnp.where(lane1 == SIZE + k, 0.0, row))
        row_t = turned(row)
        new = row * qr + row_t * qi
        new_t = row_t * qr - row * qi
        new = jnp.broadcast_to(new, (8, 2 * SIZE))
        new_t = jnp.broadcast_to(new_t, (8, 2 * SIZE))
        gone = (lane == k) | (lane == SIZE + k)
        tiles = [jnp.where(gone, 0.0, x) - a * new - b * new_t for x, a, b in zip(tiles, cr, ci)]
        tiles[t] = jnp.where(sub == s, new, tiles[t])
    return jnp.concatenate(tiles, 0)


def inverse_kernel(core_ref, mine_ref, other_ref, out_ref, a_ref):
    core = core_ref[0]
    rows = mine_ref.shape[1]
    blocks = a_ref.shape[0]
    for src, part in ((mine_ref, core), (other_ref, 1 - core)):
        r = pl.ds(pl.multiple_of(part * rows, rows), rows)
        for j in range(blocks):
            c = slice(j * SIZE, (j + 1) * SIZE)
            a_ref[j, r, :] = jnp.concatenate([src[0][:, c], src[1][:, c]], 1)
    high = lax.Precision.HIGHEST

    def step(kb, _):
        r = pl.ds(pl.multiple_of(kb * SIZE, SIZE), SIZE)
        inv = small_inverse(a_ref[kb, r, :])
        col = a_ref[kb]
        a_ref[kb] = jnp.zeros_like(col)
        lane = lax.broadcasted_iota(i32, (SIZE, 2 * SIZE), 1)
        row = lax.broadcasted_iota(i32, (SIZE, 2 * SIZE), 0)
        a_ref[kb, r, :] = jnp.where(lane == row, 1.0, 0.0)
        panel = jnp.concatenate([a_ref[j, r, :] for j in range(blocks)], 1)
        flip = jnp.concatenate([turned(a_ref[j, r, :]) for j in range(blocks)], 1)
        prod = jnp.dot(inv, jnp.concatenate([panel, flip], 0), precision=high, preferred_element_type=f32)
        parts = [prod[:, 2 * SIZE * j : 2 * SIZE * (j + 1)] for j in range(blocks)]
        full = jnp.concatenate([prod, jnp.concatenate([turned(x) for x in parts], 1)], 0)
        upd = jnp.dot(col, full, precision=high, preferred_element_type=f32)
        for j in range(blocks):
            a_ref[j] = a_ref[j] - upd[:, 2 * SIZE * j : 2 * SIZE * (j + 1)]
            a_ref[j, r, :] = parts[j]
        return 0

    lax.fori_loop(0, blocks, step, 0)
    for part in range(2):
        out_ref[part] = jnp.concatenate(
            [a_ref[j][:, part * SIZE : (part + 1) * SIZE] for j in range(blocks)], 1
        )


def pivot_inverse(core, mine, other):
    order = 2 * mine.shape[1]
    return pl.pallas_call(
        inverse_kernel,
        out_shape=jax.ShapeDtypeStruct((2, order, order), f32),
        in_specs=[SMEM, VMEM, VMEM],
        out_specs=VMEM,
        scratch_shapes=[pltpu.VMEM((order // SIZE, order, 2 * SIZE), f32)],
        cost_estimate=pl.CostEstimate(flops=int(12e9), transcendentals=0, bytes_accessed=1 << 20),
        name="pivot_inverse",
    )(core, mine, other)


def split3(x):
    hi = x.astype(bf16)
    rest = x - hi.astype(f32)
    mid = rest.astype(bf16)
    low = (rest - mid.astype(f32)).astype(bf16)
    return hi, mid, low


def schur_kernel(info, inv_ref, mine_ref, other_ref, c0_ref, c1_ref, r_ref, out_ref):
    core = info[0]
    funcs = mine_ref.shape[2]
    b = []
    for p in range(PANELS):
        local = info[1 + p] == core
        b.append([jnp.where(local, mine_ref[p, k].astype(f32), other_ref[p, k].astype(f32)).astype(bf16) for k in range(2)])
    br = jnp.concatenate([b[p][0] for p in range(PANELS)], 0)
    bi = jnp.concatenate([b[p][1] for p in range(PANELS)], 0)
    right = jnp.concatenate([jnp.concatenate([br, bi], 1), jnp.concatenate([-bi, br], 1)], 0)
    w = jnp.zeros((PANELS * funcs, right.shape[1]), f32)
    for x in split3(jnp.concatenate([inv_ref[0], inv_ref[1]], 1)):
        w += jnp.dot(x, right, preferred_element_type=f32)
    cols = w.shape[1] // 2
    w_hi = w.astype(bf16)
    w_lo = (w - w_hi.astype(f32)).astype(bf16)
    cr = jnp.concatenate([c0_ref[0, 0], c1_ref[0, 0]], 1)
    ci = jnp.concatenate([c0_ref[0, 1], c1_ref[0, 1]], 1)
    left = jnp.concatenate([cr, ci], 0)
    prod = jnp.dot(left, w_hi, preferred_element_type=f32) + jnp.dot(left, w_lo, preferred_element_type=f32)
    rows = cr.shape[0]
    out_ref[0] = r_ref[0] - (prod[:rows, :cols] - prod[rows:, cols:])
    out_ref[1] = r_ref[1] - (prod[:rows, cols:] + prod[rows:, :cols])


def schur_tile(info, inv, mine, other, column, reduced):
    funcs = mine.shape[2]
    whole = lambda x: pl.BlockSpec(x.shape, lambda i, s: (0,) * x.ndim)

    def at(p):
        return lambda i, s: (s[3 + p], 0, 0, s[5 + p])

    return pl.pallas_call(
        schur_kernel,
        out_shape=jax.ShapeDtypeStruct(reduced.shape, f32),
        grid_spec=pltpu.PrefetchScalarGridSpec(
            num_scalar_prefetch=1,
            grid=(1,),
            in_specs=[
                whole(inv),
                whole(mine),
                whole(other),
                pl.BlockSpec((1, 2, funcs, funcs), at(0)),
                pl.BlockSpec((1, 2, funcs, funcs), at(1)),
                whole(reduced),
            ],
            out_specs=whole(reduced),
        ),
        name="schur",
    )(info, inv, mine, other, column, column, reduced)


def on_device(inverse, excite, coordinates, block_of_slot, panel_order):
    blk_size, grp_size = lax.axis_size("blk"), lax.axis_size("grp")
    blocks = block_of_slot.shape[0]
    slot, grp = lax.axis_index("blk"), lax.axis_index("grp")
    core = slot % 2
    slabs = blocks // grp_size
    swap = [(i, i ^ 1) for i in range(blk_size)]
    same_core = [list(range(c, blk_size, 2)) for c in range(2)]
    core1 = core.reshape(1)

    def spread(x, axis, groups=None):
        return lax.all_to_all(x, axis, split_axis=0, concat_axis=0, tiled=True, axis_index_groups=groups)

    order = jnp.arange(blocks, dtype=i32)
    slot_of = jnp.sum(jnp.where(block_of_slot[None, :] == order[:, None], order[None, :], 0), axis=1)
    own_id = jnp.sum(jnp.where(order == slot, block_of_slot, 0))
    pivots = panel_order[:PANELS]
    feat_left, feat_right = features(coordinates)

    own8, keep, send = basis_rows(core1, inverse, excite, grp_size)
    own_full = spread(own8, "grp")
    got = lax.ppermute(send, "blk", swap)
    pair = jnp.broadcast_to(jnp.stack([keep, got])[None], (blk_size // 2, 2, *keep.shape))
    sliced = spread(pair, "blk", same_core)
    sliced = sliced.reshape(blk_size, *keep.shape)

    green_main = green_tiles(
        jnp.broadcast_to(own_id, (slabs,)), grp * slabs + jnp.arange(slabs, dtype=i32), feat_left, feat_right, "green_main"
    )
    pivot_mine = jnp.sum(jnp.where(jnp.arange(PANELS) == core, pivots, 0))
    green_pivot = green_tiles(jnp.broadcast_to(pivot_mine, (PANELS,)), pivots, feat_left, feat_right, "green_pivot")

    wanted = jnp.concatenate(
        [order.reshape(grp_size, slabs), jnp.broadcast_to(pivots[None], (grp_size, PANELS))], axis=1
    )
    from_slot = jnp.sum(jnp.where(wanted[:, :, None] == order, slot_of, 0), axis=2)
    place = (from_slot // 2) * 2 + (from_slot % 2 + core) % 2
    mine = spread(jnp.take(sliced, place.reshape(-1), axis=0).reshape(*place.shape, *keep.shape), "grp")
    other = lax.ppermute(mine, "blk", swap)

    reduced, copies = couplings(core1, green_main, own_full, mine, other, 0, None, "main")
    (pivot_rows,) = couplings(core1, green_pivot, None, mine, other, slabs, slabs, "pivot")

    column = spread(copies, "grp")
    rows = spread(copies, "blk", same_core)
    pivot_slot = jnp.sum(jnp.where(pivots[:, None] == order, slot_of, 0), axis=1)
    row_mine = jnp.stack([lax.dynamic_index_in_dim(rows, pivot_slot[p] // 2, 0, keepdims=False) for p in range(PANELS)])
    row_other = lax.ppermute(row_mine, "blk", swap)
    inv = pivot_inverse(core1, pivot_rows, lax.ppermute(pivot_rows, "blk", swap))
    info = jnp.concatenate([core1, pivot_slot % 2, pivots // slabs, pivots % slabs]).astype(i32)
    schur = schur_tile(info, inv, row_mine, row_other, column, reduced)
    return (reduced, schur)


def solution(mesh):
    placed = (P(None, "blk", "grp", None), P(None, "blk", None, None), P(), P(), P())
    return jax.shard_map(
        on_device,
        mesh=mesh,
        in_specs=placed,
        out_specs=(P(None, "blk", "grp"), P(None, "blk", "grp")),
        check_vma=False,
    )
```

time: 570 us -> 173 us (0.30)
  waiting for transfers between devices: 187 us -> 9.87 us
  matrix products: 177 us -> 0 us
  other arithmetic: 116 us -> 5.21 us
  Pallas kernels: 0 us -> 82.6 us
  blocking collectives: 0 us -> 23.3 us
  between operations: 27.2 us -> 6.04 us
  loops' own time: 16.8 us -> 0 us
    dot_general x36 -> x0, matrix products: 169 us -> none  [the longest x2 36.3 us: one_pair(): jnp.dot(greens_function_imaginary, basis[1], preferred_element_type=jnp.f...]
    all_gather x6 -> x0, waiting for transfers between devices: 148 us -> none  [from_root(): lax.all_gather(x, axis)]
    another operation x21 -> x4, other arithmetic: 108 us -> 1.11 us  [the longest x1 0.77 us: on_device(): jnp.stack([keep, got])[None]]
    pallas_call x0 -> x7, Pallas kernels: none -> 82.6 us  [the longest x1 31.8 us: pivot_inverse(): pl.pallas_call(inverse_kernel, out_shape=jax.ShapeDtypeStruct((2, order,...]
    all_to_all x3 -> x4, waiting for transfers between devices: 39.4 us -> 9.86 us  [spread(): lax.all_to_all(x, axis, split_axis=0, concat_axis=0, tiled=True, axis_ind...]
    all_to_all x0 -> x1, blocking collectives: none -> 23.3 us  [spread(): lax.all_to_all(x, axis, split_axis=0, concat_axis=0, tiled=True, axis_ind...]
    another operation x3 -> x0, loops' own time: 16.8 us -> none  [the longest x1 16 us: on_device(): reduced = lax.fori_loop(0, per_dev * slab_count, one_pair, start_table)]
    unnamed x10 -> x22, local copies, waits for them, and re-layouts: 0.72 us -> 14.9 us
  transfers between devices with their start and end apart: 9 -> 8, of which waited for: 7 -> 1; matrix products, arithmetic and copies ran while one was open for 25% -> 6% of each run, Pallas kernels for 0% -> 39%
where the time goes in v1:
time: 173 us; the launch traced here: 170 us
  Pallas kernels  82.6 us (48%)
  blocking collectives  23.3 us (13%)
  local copies, waits for them, and re-layouts  21.9 us (13%)
  starting transfers between devices  21.6 us (12%)
  waiting for transfers between devices  9.87 us (6%)
  between operations  6.04 us (3%)
  other arithmetic  5.21 us (3%)
    pallas_call x1, Pallas kernels, pivot_inverse(): pl.pallas_call(inverse_kernel, out_shape=jax.ShapeDtypeStruct((2, order,...  31.8 us
    pallas_call x2, Pallas kernels, green_tiles(): pl.pallas_call(green_kernel, out_shape=jax.ShapeDtypeStruct((tiles, 2, un...  26.5 us
    all_to_all x1, blocking collectives, spread(): lax.all_to_all(x, axis, split_axis=0, concat_axis=0, tiled=True, axis_ind...  23.3 us
    all_to_all x4, starting transfers between devices, spread(): lax.all_to_all(x, axis, split_axis=0, concat_axis=0, tiled=True, axis_ind...  20.5 us
    pallas_call x2, Pallas kernels, couplings(): pl.pallas_call(functools.partial(coupling_kernel, first, left_at), out_sh...  18.2 us
    unnamed x22, local copies, waits for them, and re-layouts  14.9 us
    all_to_all x4, waiting for transfers between devices, spread(): lax.all_to_all(x, axis, split_axis=0, concat_axis=0, tiled=True, axis_ind...  9.86 us
    pallas_call x1, Pallas kernels, schur_tile(): pl.pallas_call(schur_kernel, out_shape=jax.ShapeDtypeStruct(reduced.shape...  3.71 us
  transfers between devices with their start and end apart: 8, of which 1 were waited for; matrix products, arithmetic and copies ran while one was open for 6% of the time, Pallas kernels for 39%

profile of v1, /device:TPU:0, one launch (start us, length us, event | category | flops | bytes accessed | tf_op | source)
XLA Modules:
  0.0 170.5 jit_solution(7966666951363787190)
XLA Ops:
  0.7 2.4 %basis.1 = (bf16[8,2,128,128]{3,2,1,0:T(8,128)(2,1)}, bf16[2,64,128]{2,1,0:T(8,128)(2,1)}, bf16[2,64,128]{2,1,0:T(8,128)(2,1)}) custom-call(s32[1]{0:T(128)} %bitcast.core_ref, bf16[2,1,128,1024]{3,2,1,0:T(8,128)(2,1)} %inv_ref.1, bf16[2,1,1024,128]{3,2,1,0:T(8,128)(2,1)} %exc_ref.1), custom_call_target="tpu_custom_call" | custom-call | tf_op jit(solution)/shard_map/basis/pallas_call | solution.py:64
  3.1 0.8 select_reduce_fusion.1
  3.8 1.4 and_select_fusion.2
  5.2 0.1 pad.9.clone
  5.3 0.1 pad_add_fusion
  5.3 0.2 select_reduce_fusion
  5.6 0.1 copy.50
  5.6 0.8 pad_maximum_fusion.1
  6.4 0.9 broadcast_in_dim.77
  7.3 5.5 %all-to-all-start.1 = ((bf16[8,2,2,64,128]{4,3,2,1,0:T(8,128)(2,1)}), bf16[8,2,2,64,128]{4,3,2,1,0:T(8,128)(2,1)S(1)}, u32[]{:S(2)}, u32[]{:S(2)}) async-start(bf16[8,2,2,64,128]{4,3,2,1,0:T(8,128)(2,1)} %broadcast_in_dim.77), calls=%async_computation.1 | async-start | bytes 1048576 | tf_op jit(solution)/shard_map/all_to_all | solution.py:385
  12.9 0.1 copy.49
  13.0 0.1 reduce_sum.63
  13.1 9.9 %all-to-all-done.1 = bf16[8,2,2,64,128]{4,3,2,1,0:T(8,128)(2,1)S(1)} async-done(((bf16[8,2,2,64,128]{4,3,2,1,0:T(8,128)(2,1)}), bf16[8,2,2,64,128]{4,3,2,1,0:T(8,128)(2,1)S(1)}, u32[]{:S(2)}, u32[]{:S(2)}) %all-to-all-start.1) | async-done | bytes 524320 | tf_op jit(solution)/shard_map/all_to_all | solution.py:385
  22.9 0.7 gather_fusion
  23.7 0.2 broadcast_select_fusion
  23.9 23.3 %all_to_all.25.refs_1_.refs_0_ = bf16[8,4,2,64,128]{4,3,2,1,0:T(8,128)(2,1)S(1)} all-to-all(bf16[8,4,2,64,128]{4,3,2,1,0:T(8,128)(2,1)S(1)} %broadcast_select_fusion), channel_id=1, replica_groups=mesh['blk'=16,'grp'=8] {'grp'}, dimensions={0} | all-to-all | bytes 2097152 | tf_op jit(solution)/shard_map/all_to_all | solution.py:385
  47.2 3.5 %all-to-all-start = ((bf16[8,2,128,128]{3,2,1,0:T(8,128)(2,1)}), bf16[8,2,128,128]{3,2,1,0:T(8,128)(2,1)S(1)}, u32[]{:S(2)}, u32[]{:S(2)}) async-start(bf16[8,2,128,128]{3,2,1,0:T(8,128)(2,1)} %get-tuple-element.7), calls=%async_computation | async-start | bytes 1048576 | tf_op jit(solution)/shard_map/all_to_all | solution.py:385
  50.7 0.1 copy.48
  50.8 0.1 copy.43
  50.9 0.1 copy.44
  50.9 0.1 copy.45
  51.1 0.3 fusion.7
  51.5 0.8 stack.30.fr_ref
  52.4 0.8 stack.14.fl_ref
  53.2 0.7 broadcast_in_dim.81.left_ids
  53.9 13.3 %green_pivot.1.g_ref = bf16[2,2,1024,1024]{3,2,1,0:T(8,128)(2,1)S(1)} custom-call(s32[2]{0:T(128)S(1)} %broadcast_in_dim.81.left_ids, s32[2]{0:T(128)S(1)} %get-tuple-element.27.right_ids, bf16[16,16,1024]{2,1,0:T(8,128)(2,1)S(1)} %stack.14.fl_ref, bf16[16,16,1024]{2,1,0:T(8,128)(2,1)S(1)} %stack.30.fr_ref), custom_call_target="tpu_custom_call" | custom-call | flops 62914560 | bytes 8388608 | tf_op jit(solution)/shard_map/green_pivot/pallas_call | solution.py:102
  67.2 3.2 %copy-done = bf16[2,2,1024,1024]{3,2,1,0:T(8,128)(2,1)} copy-done((bf16[2,2,1024,1024]{3,2,1,0:T(8,128)(2,1)}, bf16[2,2,1024,1024]{3,2,1,0:T(8,128)(2,1)S(1)}, u32[]{:S(2)}) %copy-start) | copy-done | bytes 8388632
  70.4 0.6 fusion.16
  71.1 0.6 broadcast_in_dim.70.left_ids
  71.7 13.1 %green_main.1.g_ref = bf16[2,2,1024,1024]{3,2,1,0:T(8,128)(2,1)S(1)} custom-call(s32[2]{0:T(128)S(1)} %broadcast_in_dim.70.left_ids, s32[2]{0:T(128)S(1)} %iota_add_fusion.right_ids, bf16[16,16,1024]{2,1,0:T(8,128)(2,1)S(1)} %stack.14.fl_ref, bf16[16,16,1024]{2,1,0:T(8,128)(2,1)S(1)} %stack.30.fr_ref), custom_call_target="tpu_custom_call" | custom-call | flops 62914560 | bytes 8388608 | tf_op jit(solution)/shard_map/green_main/pallas_call | solution.py:102
  84.9 3.2 %copy-done.2 = bf16[2,2,1024,1024]{3,2,1,0:T(8,128)(2,1)} copy-done((bf16[2,2,1024,1024]{3,2,1,0:T(8,128)(2,1)}, bf16[2,2,1024,1024]{3,2,1,0:T(8,128)(2,1)S(1)}, u32[]{:S(2)}) %copy-start.2) | copy-done | bytes 8388632
  88.1 3.4 %copy-done.3 = bf16[2,2,1024,1024]{3,2,1,0:T(8,128)(2,1)S(1)} copy-done((bf16[2,2,1024,1024]{3,2,1,0:T(8,128)(2,1)S(1)}, bf16[2,2,1024,1024]{3,2,1,0:T(8,128)(2,1)}, u32[]{:S(2)}) %copy-start.3) | copy-done | bytes 8388632
  91.5 9.6 %main.1 = (f32[2,128,256]{2,1,0:T(8,128)}, bf16[8,2,128,256]{3,2,1,0:T(8,128)(2,1)}) custom-call(s32[1]{0:T(128)} %bitcast.core_ref, bf16[2,2,1024,1024]{3,2,1,0:T(8,128)(2,1)S(1)} %copy-done.3, bf16[8,2,128,128]{3,2,1,0:T(8,128)(2,1)S(1)} %all-to-all-done.refs_0_, bf16[8,4,2,64,128]{4,3,2,1,0:T(8,128)(2,1)S(1)} %all_to_all.25.refs_1_.refs_0_, ...), custom_call_target="tpu_custom_call" | custom-call | flops 4294967296 | bytes 8388608 | tf_op jit(solution)/shard_map/main/pallas_call | solution.py:210
  101.1 4.2 %all-to-all-start.3 = ((bf16[8,2,128,256]{3,2,1,0:T(8,128)(2,1)}), bf16[8,2,128,256]{3,2,1,0:T(8,128)(2,1)}, u32[]{:S(2)}, u32[]{:S(2)}) async-start(bf16[8,2,128,256]{3,2,1,0:T(8,128)(2,1)} %get-tuple-element.11), calls=%async_computation.3 | async-start | bytes 2097152 | tf_op jit(solution)/shard_map/all_to_all | solution.py:385
  105.4 0.2 fusion.14
  105.5 0.6 fusion.22
  106.2 3.4 %copy-done.1 = bf16[2,2,1024,1024]{3,2,1,0:T(8,128)(2,1)S(1)} copy-done((bf16[2,2,1024,1024]{3,2,1,0:T(8,128)(2,1)S(1)}, bf16[2,2,1024,1024]{3,2,1,0:T(8,128)(2,1)}, u32[]{:S(2)}) %copy-start.1) | copy-done | bytes 8388632
  109.5 8.6 %pivot.1.mine_ref = f32[2,128,256]{2,1,0:T(8,128)S(1)} custom-call(s32[1]{0:T(128)} %bitcast.core_ref, bf16[2,2,1024,1024]{3,2,1,0:T(8,128)(2,1)S(1)} %copy-done.1, bf16[8,4,2,64,128]{4,3,2,1,0:T(8,128)(2,1)S(1)} %all_to_all.25.refs_1_.refs_0_, bf16[8,4,2,64,128]{4,3,2,1,0:T(8,128)(2,1)} %collective-permute-done.1.refs_2_.refs_1_), custom_call_target="tpu_custom_call" | custom-call | flops 4294967296 | bytes 8388608 | tf_op jit(solution)/shard_map/pivot/pallas_call | solution.py:210
  118.2 0.6 collective-permute-start.2
  118.8 0.6 pad_add_fusion.1.info
  124.5 7.2 %all-to-all-start.4 = ((bf16[8,2,128,256]{3,2,1,0:T(8,128)(2,1)}), bf16[8,2,128,256]{3,2,1,0:T(8,128)(2,1)S(1)}, u32[]{:S(2)}, u32[]{:S(2)}) async-start(bf16[8,2,128,256]{3,2,1,0:T(8,128)(2,1)} %get-tuple-element.11), calls=%async_computation.4 | async-start | bytes 2097152 | tf_op jit(solution)/shard_map/all_to_all | solution.py:385
  131.7 1.0 constant_dynamic-slice_fusion.1
  132.7 0.5 collective-permute-start.3
  133.2 0.7 copy-done.9
  133.9 31.8 %pivot_inverse.1.inv_ref = f32[2,256,256]{2,1,0:T(8,128)} custom-call(s32[1]{0:T(128)} %bitcast.core_ref, f32[2,128,256]{2,1,0:T(8,128)} %copy-done.4, f32[2,128,256]{2,1,0:T(8,128)} %copy-done.9), custom_call_target="tpu_custom_call" | custom-call | flops 12000000000 | bytes 1048576 | tf_op jit(solution)/shard_map/pivot_inverse/pallas_call | solution.py:303
  165.7 0.9 copy-done.5
  166.7 0.1 copy-done.8
  166.7 3.7 %schur.1 = f32[2,128,256]{2,1,0:T(8,128)} custom-call(s32[7]{0:T(128)} %pad_add_fusion.1.info, f32[2,256,256]{2,1,0:T(8,128)} %pivot_inverse.1.inv_ref, bf16[2,2,128,256]{3,2,1,0:T(8,128)(2,1)} %copy-done.6, bf16[2,2,128,256]{3,2,1,0:T(8,128)(2,1)} %copy-done.8, bf16[8,2,128,256]{3,2,1,0:T(8,128)(2,1)} %copy-done.5, bf16[8,2,128,256]{3,2,1,0:T(8,128)(2,1)} %copy-done.5, ...), custom_call_target="tpu_custom_call" | custom-call | tf_op jit(solution)/shard_map/schur/pallas_call | solution.py:354
  (38 shorter events, 0.4 us)
Async XLA Ops:
  0.6 50.1 %copy-start.7 = (s32[3,16,1024]{2,1,0:T(8,128)S(1)}, s32[3,16,1024]{2,1,0:T(8,128)}, u32[]{:S(2)}) copy-start(s32[3,16,1024]{2,1,0:T(8,128)} %param.7) | copy-start | bytes 589828
  3.1 2.6 %collective-permute-start = (bf16[2,64,128]{2,1,0:T(8,128)(2,1)}, bf16[2,64,128]{2,1,0:T(8,128)(2,1)S(1)}, u32[]{:S(2)}, u32[]{:S(2)}) collective-permute-start(bf16[2,64,128]{2,1,0:T(8,128)(2,1)} %get-tuple-element.9), channel_id=1, source_target_pairs={{0,8},{8,0},{16,24},{24,16},{32,40},{40,32},{48,56},{56,48},{64,72... | collective-permute-start | bytes 98312 | tf_op jit(solution)/shard_map/ppermute | solution.py:395
  7.3 15.6 %all-to-all-start.1 = ((bf16[8,2,2,64,128]{4,3,2,1,0:T(8,128)(2,1)}), bf16[8,2,2,64,128]{4,3,2,1,0:T(8,128)(2,1)S(1)}, u32[]{:S(2)}, u32[]{:S(2)}) async-start(bf16[8,2,2,64,128]{4,3,2,1,0:T(8,128)(2,1)} %broadcast_in_dim.77), calls=%async_computation.1 | async-start | bytes 1048576 | tf_op jit(solution)/shard_map/all_to_all | solution.py:385
  23.9 46.6 %copy-start.10 = (s32[16]{0:T(128)S(1)}, s32[16]{0:T(128)}, u32[]{:S(2)}) copy-start(s32[16]{0:T(128)} %param.8) | copy-start | bytes 196
  47.2 40.9 %collective-permute-start.1 = (bf16[8,4,2,64,128]{4,3,2,1,0:T(8,128)(2,1)S(1)}, bf16[8,4,2,64,128]{4,3,2,1,0:T(8,128)(2,1)}, u32[]{:S(2)}, u32[]{:S(2)}) collective-permute-start(bf16[8,4,2,64,128]{4,3,2,1,0:T(8,128)(2,1)S(1)} %all_to_all.25.refs_1_.refs_0_), channel_id=1, source_target_pairs={{0,8},{8,0},{16,24},{24,16},{32,40},{40,32},{48,56},{56,48},{64,72... | collective-permute-start | bytes 3145736 | tf_op jit(solution)/shard_map/ppermute | solution.py:412
  47.2 40.9 %all-to-all-start = ((bf16[8,2,128,128]{3,2,1,0:T(8,128)(2,1)}), bf16[8,2,128,128]{3,2,1,0:T(8,128)(2,1)S(1)}, u32[]{:S(2)}, u32[]{:S(2)}) async-start(bf16[8,2,128,128]{3,2,1,0:T(8,128)(2,1)} %get-tuple-element.7), calls=%async_computation | async-start | bytes 1048576 | tf_op jit(solution)/shard_map/all_to_all | solution.py:385
  67.2 3.2 %copy-start = (bf16[2,2,1024,1024]{3,2,1,0:T(8,128)(2,1)}, bf16[2,2,1024,1024]{3,2,1,0:T(8,128)(2,1)S(1)}, u32[]{:S(2)}) copy-start(bf16[2,2,1024,1024]{3,2,1,0:T(8,128)(2,1)S(1)} %green_pivot.1.g_ref) | copy-start | bytes 25165828
  84.9 3.2 %copy-start.2 = (bf16[2,2,1024,1024]{3,2,1,0:T(8,128)(2,1)}, bf16[2,2,1024,1024]{3,2,1,0:T(8,128)(2,1)S(1)}, u32[]{:S(2)}) copy-start(bf16[2,2,1024,1024]{3,2,1,0:T(8,128)(2,1)S(1)} %green_main.1.g_ref) | copy-start | bytes 25165828
  88.1 3.4 %copy-start.3 = (bf16[2,2,1024,1024]{3,2,1,0:T(8,128)(2,1)S(1)}, bf16[2,2,1024,1024]{3,2,1,0:T(8,128)(2,1)}, u32[]{:S(2)}) copy-start(bf16[2,2,1024,1024]{3,2,1,0:T(8,128)(2,1)} %copy-done.2) | copy-start | bytes 25165828
  101.1 23.3 %all-to-all-start.3 = ((bf16[8,2,128,256]{3,2,1,0:T(8,128)(2,1)}), bf16[8,2,128,256]{3,2,1,0:T(8,128)(2,1)}, u32[]{:S(2)}, u32[]{:S(2)}) async-start(bf16[8,2,128,256]{3,2,1,0:T(8,128)(2,1)} %get-tuple-element.11), calls=%async_computation.3 | async-start | bytes 2097152 | tf_op jit(solution)/shard_map/all_to_all | solution.py:385
  106.2 3.4 %copy-start.1 = (bf16[2,2,1024,1024]{3,2,1,0:T(8,128)(2,1)S(1)}, bf16[2,2,1024,1024]{3,2,1,0:T(8,128)(2,1)}, u32[]{:S(2)}) copy-start(bf16[2,2,1024,1024]{3,2,1,0:T(8,128)(2,1)} %copy-done) | copy-start | bytes 25165828
  118.2 15.0 %copy-start.4 = (f32[2,128,256]{2,1,0:T(8,128)}, f32[2,128,256]{2,1,0:T(8,128)S(1)}, u32[]{:S(2)}) copy-start(f32[2,128,256]{2,1,0:T(8,128)S(1)} %pivot.1.mine_ref) | copy-start | bytes 786436
  118.2 15.0 %collective-permute-start.2 = (f32[2,128,256]{2,1,0:T(8,128)S(1)}, f32[2,128,256]{2,1,0:T(8,128)S(1)}, u32[]{:S(2)}, u32[]{:S(2)}) collective-permute-start(f32[2,128,256]{2,1,0:T(8,128)S(1)} %pivot.1.mine_ref), channel_id=1, source_target_pairs={{0,8},{8,0},{16,24},{24,16},{32,40},{40,32},{48,56},{56,48},{64,72... | collective-permute-start | bytes 786440 | tf_op jit(solution)/shard_map/ppermute | solution.py:422
  124.5 41.2 %all-to-all-start.4 = ((bf16[8,2,128,256]{3,2,1,0:T(8,128)(2,1)}), bf16[8,2,128,256]{3,2,1,0:T(8,128)(2,1)S(1)}, u32[]{:S(2)}, u32[]{:S(2)}) async-start(bf16[8,2,128,256]{3,2,1,0:T(8,128)(2,1)} %get-tuple-element.11), calls=%async_computation.4 | async-start | bytes 2097152 | tf_op jit(solution)/shard_map/all_to_all | solution.py:385
  132.7 33.0 %copy-start.6 = (bf16[2,2,128,256]{3,2,1,0:T(8,128)(2,1)}, bf16[2,2,128,256]{3,2,1,0:T(8,128)(2,1)S(1)}, u32[]{:S(2)}) copy-start(bf16[2,2,128,256]{3,2,1,0:T(8,128)(2,1)S(1)} %pad_maximum_fusion.mine_ref) | copy-start | bytes 786436
  132.7 33.0 %collective-permute-start.3 = (bf16[2,2,128,256]{3,2,1,0:T(8,128)(2,1)S(1)}, bf16[2,2,128,256]{3,2,1,0:T(8,128)(2,1)S(1)}, u32[]{:S(2)}, u32[]{:S(2)}) collective-permute-start(bf16[2,2,128,256]{3,2,1,0:T(8,128)(2,1)S(1)} %pad_maximum_fusion.mine_ref), channel_id=1, source_target_pairs={{0,8},{8,0},{16,24},{24,16},{32,40},{40,32},{48,56},{56,48},{64,72... | collective-permute-start | bytes 786440 | tf_op jit(solution)/shard_map/ppermute | solution.py:421
  133.2 0.7 copy-start.9
  165.7 1.0 copy-start.5
  165.7 1.0 copy-start.8

commit v2 on v1

--- a/solution.py
+++ b/solution.py
@@ -7,6 +7,7 @@
 from jax.experimental import pallas as pl
 from jax.experimental.pallas import tpu as pltpu
 from jax.sharding import PartitionSpec as P
+
 
 PANELS = 2
 bf16 = jnp.bfloat16
@@ -41,37 +42,36 @@
     return inv_r - (s * s) * inv_r, (s * c) * inv_r
 
 
-def basis_kernel(core_ref, inv_ref, exc_ref, own_ref, keep_ref, send_ref):
+def basis_kernel(core_ref, inv_ref, exc_ref, keep_ref, send_ref, both):
     er, ei = exc_ref[0, 0], exc_ref[1, 0]
     j = jnp.dot(inv_ref[0, 0], jnp.concatenate([er, ei], 1), preferred_element_type=f32)
     j += jnp.dot(inv_ref[1, 0], jnp.concatenate([-ei, er], 1), preferred_element_type=f32)
     rows, cols = j.shape[0], j.shape[1] // 2
     half = rows // 2
-    jb = j.astype(bf16)
-    for g in range(own_ref.shape[0]):
-        own_ref[g, 0] = jb[:, :cols]
-        own_ref[g, 1] = jb[:, cols:]
+    both[...] = j.astype(bf16)
     mine = pl.multiple_of(core_ref[0] * half, half)
     other = pl.multiple_of((1 - core_ref[0]) * half, half)
     for part in range(2):
-        keep_ref[part] = own_ref[0, part, pl.ds(mine, half), :]
-        send_ref[part] = own_ref[0, part, pl.ds(other, half), :]
-
-
-def basis_rows(core, inverse, excite, copies):
+        keep_ref[part] = both[pl.ds(mine, half), part * cols : (part + 1) * cols]
+        send_ref[part] = both[pl.ds(other, half), part * cols : (part + 1) * cols]
+
+
+def basis_rows(core, inverse, excite):
     rows, cols = inverse.shape[2], excite.shape[3]
     half = jax.ShapeDtypeStruct((2, rows // 2, cols), bf16)
     return pl.pallas_call(
         basis_kernel,
-        out_shape=(jax.ShapeDtypeStruct((copies, 2, rows, cols), bf16), half, half),
+        out_shape=(half, half),
         in_specs=[SMEM, VMEM, VMEM],
-        out_specs=(VMEM, VMEM, VMEM),
+        out_specs=(VMEM, VMEM),
+        scratch_shapes=[pltpu.VMEM((rows, 2 * cols), bf16)],
+        compiler_params=pltpu.CompilerParams(vmem_limit_bytes=8 * MB),
         name="basis",
     )(core, inverse, excite)
 
 
 def green_kernel(left_ids, right_ids, fl_ref, fr_ref, g_ref, sq_ref):
-    rows, cols = sq_ref.shape
+    rows, _ = sq_ref.shape
     sq_ref[...] = lax.dot_general(
         fl_ref[0], fr_ref[0], (((0,), (0,)), ((), ())), preferred_element_type=f32
     )
@@ -95,13 +95,13 @@
             g_ref[0, part, :, at] = jnp.where(same, value, block).astype(bf16)
 
 
-def green_tiles(left_ids, right_ids, feat_left, feat_right, name):
+def green_tiles(left_ids, right_ids, feat_left, feat_right):
     tiles, unk = left_ids.shape[0], feat_left.shape[2]
     rows = 256
     depth = feat_left.shape[1]
     return pl.pallas_call(
         green_kernel,
-        out_shape=jax.ShapeDtypeStruct((tiles, 2, unk, unk), bf16),
+        out_shape=pltpu.HBM((tiles, 2, unk, unk), bf16),
         grid_spec=pltpu.PrefetchScalarGridSpec(
             num_scalar_prefetch=2,
             grid=(tiles, unk // rows),
@@ -112,11 +112,10 @@
             out_specs=pl.BlockSpec((1, 2, rows, unk), lambda t, m, le, ri: (t, 0, m, 0)),
             scratch_shapes=[pltpu.VMEM((rows, unk), f32)],
         ),
-        compiler_params=pltpu.CompilerParams(vmem_limit_bytes=16 * MB),
+        compiler_params=pltpu.CompilerParams(vmem_limit_bytes=10 * MB),
         cost_estimate=pl.CostEstimate(
             flops=tiles * unk * unk * 30, transcendentals=tiles * unk * unk, bytes_accessed=tiles * unk * unk * 4
         ),
-        name=name,
     )(left_ids, right_ids, feat_left, feat_right)
 
 
@@ -135,7 +134,7 @@
 
 def coupling_kernel(first, left_at, core_ref, g_ref, *refs):
     if left_at is None:
-        own_ref, mine_ref, other_ref, out_ref, copies_ref, lhs, top, bottom, acc = refs
+        mine_ref, other_ref, out_ref, copies_ref, lhs, top, bottom, acc = refs
     else:
         mine_ref, other_ref, out_ref, lhs, top, bottom, acc = refs
     tile, chunk = pl.program_id(0), pl.program_id(1)
@@ -149,17 +148,12 @@
 
     @pl.when((tile == 0) & (chunk == 0))
     def _():
-        if left_at is None:
-            for g in range(groups):
-                r = pl.ds(g * 2 * half, 2 * half)
-                lhs[r, :cols] = own_ref[g, 0]
-                lhs[r, cols:] = own_ref[g, 1]
-        else:
-            for g in range(groups):
-                for src, part in ((mine_ref, core), (other_ref, 1 - core)):
-                    r = rows_of(g, part)
-                    lhs[r, :cols] = src[g, left_at + core, 0]
-                    lhs[r, cols:] = src[g, left_at + core, 1]
+        for g in range(groups):
+            for src, part, entry in ((mine_ref, core, 0), (other_ref, 1 - core, 1)):
+                at = left_at + core if left_at is not None else mine_ref.shape[1] - 2 + entry
+                r = rows_of(g, part)
+                lhs[r, :cols] = src[g, at, 0]
+                lhs[r, cols:] = src[g, at, 1]
 
     @pl.when(chunk == 0)
     def _():
@@ -195,13 +189,13 @@
                 copies_ref[k, 1] = im.astype(bf16)
 
 
-def couplings(core, green, own, mine, other, first, left_at, name):
+def couplings(core, green, mine, other, first, left_at):
     tiles, _, unk, _ = green.shape
     cols = mine.shape[4]
     rows = 256
     copies = 8
     whole = lambda x: pl.BlockSpec(x.shape, lambda t, m: (0,) * x.ndim)
-    args = ([own] if left_at is None else []) + [mine, other]
+    args = [mine, other]
     out_shape = [jax.ShapeDtypeStruct((2, cols, tiles * cols), f32)]
     out_specs = [pl.BlockSpec((2, cols, cols), lambda t, m: (0, 0, t))]
     if left_at is None:
@@ -219,12 +213,11 @@
             pltpu.VMEM((unk, 2 * cols), bf16),
             pltpu.VMEM((2 * cols, 2 * cols), f32),
         ],
-        compiler_params=pltpu.CompilerParams(vmem_limit_bytes=24 * MB),
+        compiler_params=pltpu.CompilerParams(vmem_limit_bytes=12 * MB),
         cost_estimate=pl.CostEstimate(
             flops=tiles * unk * unk * 2048, transcendentals=0, bytes_accessed=tiles * unk * unk * 4
         ),
-        name=name,
-    )(core, green, *args)
+    )(core, pltpu.with_memory_space_constraint(green, pltpu.HBM), *args)
 
 
 SIZE = 64
@@ -306,6 +299,7 @@
         in_specs=[SMEM, VMEM, VMEM],
         out_specs=VMEM,
         scratch_shapes=[pltpu.VMEM((order // SIZE, order, 2 * SIZE), f32)],
+        compiler_params=pltpu.CompilerParams(vmem_limit_bytes=12 * MB),
         cost_estimate=pl.CostEstimate(flops=int(12e9), transcendentals=0, bytes_accessed=1 << 20),
         name="pivot_inverse",
     )(core, mine, other)
@@ -319,7 +313,7 @@
     return hi, mid, low
 
 
-def schur_kernel(info, inv_ref, mine_ref, other_ref, c0_ref, c1_ref, r_ref, out_ref):
+def schur_kernel(info, inv_ref, mine_ref, other_ref, c_ref, r_ref, out_ref):
     core = info[0]
     funcs = mine_ref.shape[2]
     b = []
@@ -335,8 +329,8 @@
     cols = w.shape[1] // 2
     w_hi = w.astype(bf16)
     w_lo = (w - w_hi.astype(f32)).astype(bf16)
-    cr = jnp.concatenate([c0_ref[0, 0], c1_ref[0, 0]], 1)
-    ci = jnp.concatenate([c0_ref[0, 1], c1_ref[0, 1]], 1)
+    cr = jnp.concatenate([c_ref[0, 0], c_ref[1, 0]], 1)
+    ci = jnp.concatenate([c_ref[0, 1], c_ref[1, 1]], 1)
     left = jnp.concatenate([cr, ci], 0)
     prod = jnp.dot(left, w_hi, preferred_element_type=f32) + jnp.dot(left, w_lo, preferred_element_type=f32)
     rows = cr.shape[0]
@@ -345,30 +339,14 @@
 
 
 def schur_tile(info, inv, mine, other, column, reduced):
-    funcs = mine.shape[2]
-    whole = lambda x: pl.BlockSpec(x.shape, lambda i, s: (0,) * x.ndim)
-
-    def at(p):
-        return lambda i, s: (s[3 + p], 0, 0, s[5 + p])
-
     return pl.pallas_call(
         schur_kernel,
         out_shape=jax.ShapeDtypeStruct(reduced.shape, f32),
-        grid_spec=pltpu.PrefetchScalarGridSpec(
-            num_scalar_prefetch=1,
-            grid=(1,),
-            in_specs=[
-                whole(inv),
-                whole(mine),
-                whole(other),
-                pl.BlockSpec((1, 2, funcs, funcs), at(0)),
-                pl.BlockSpec((1, 2, funcs, funcs), at(1)),
-                whole(reduced),
-            ],
-            out_specs=whole(reduced),
-        ),
+        in_specs=[SMEM] + [VMEM] * 5,
+        out_specs=VMEM,
+        compiler_params=pltpu.CompilerParams(vmem_limit_bytes=12 * MB),
         name="schur",
-    )(info, inv, mine, other, column, column, reduced)
+    )(info, inv, mine, other, column, reduced)
 
 
 def on_device(inverse, excite, coordinates, block_of_slot, panel_order):
@@ -377,6 +355,7 @@
     slot, grp = lax.axis_index("blk"), lax.axis_index("grp")
     core = slot % 2
     slabs = blocks // grp_size
+    cols = excite.shape[3]
     swap = [(i, i ^ 1) for i in range(blk_size)]
     same_core = [list(range(c, blk_size, 2)) for c in range(2)]
     core1 = core.reshape(1)
@@ -390,37 +369,50 @@
     pivots = panel_order[:PANELS]
     feat_left, feat_right = features(coordinates)
 
-    own8, keep, send = basis_rows(core1, inverse, excite, grp_size)
-    own_full = spread(own8, "grp")
+    keep, send = basis_rows(core1, inverse, excite)
     got = lax.ppermute(send, "blk", swap)
-    pair = jnp.broadcast_to(jnp.stack([keep, got])[None], (blk_size // 2, 2, *keep.shape))
+    pair1 = jnp.stack([keep, got])
+    pair = jnp.broadcast_to(pair1[None], (blk_size // 2, *pair1.shape))
     sliced = spread(pair, "blk", same_core)
     sliced = sliced.reshape(blk_size, *keep.shape)
 
     green_main = green_tiles(
-        jnp.broadcast_to(own_id, (slabs,)), grp * slabs + jnp.arange(slabs, dtype=i32), feat_left, feat_right, "green_main"
+        jnp.broadcast_to(own_id, (slabs,)), grp * slabs + jnp.arange(slabs, dtype=i32), feat_left, feat_right
     )
     pivot_mine = jnp.sum(jnp.where(jnp.arange(PANELS) == core, pivots, 0))
-    green_pivot = green_tiles(jnp.broadcast_to(pivot_mine, (PANELS,)), pivots, feat_left, feat_right, "green_pivot")
+    green_pivot = green_tiles(jnp.broadcast_to(pivot_mine, (PANELS,)), pivots, feat_left, feat_right)
 
     wanted = jnp.concatenate(
         [order.reshape(grp_size, slabs), jnp.broadcast_to(pivots[None], (grp_size, PANELS))], axis=1
     )
     from_slot = jnp.sum(jnp.where(wanted[:, :, None] == order, slot_of, 0), axis=2)
+    pair_slots = jnp.stack([slot, slot + 1 - 2 * core])
+    from_slot = jnp.concatenate([from_slot, jnp.broadcast_to(pair_slots[None], (grp_size, 2))], axis=1)
     place = (from_slot // 2) * 2 + (from_slot % 2 + core) % 2
-    mine = spread(jnp.take(sliced, place.reshape(-1), axis=0).reshape(*place.shape, *keep.shape), "grp")
+    picked = sliced.at[place.reshape(-1)].get(mode="promise_in_bounds").reshape(*place.shape, *keep.shape)
+    mine = spread(picked, "grp")
     other = lax.ppermute(mine, "blk", swap)
 
-    reduced, copies = couplings(core1, green_main, own_full, mine, other, 0, None, "main")
-    (pivot_rows,) = couplings(core1, green_pivot, None, mine, other, slabs, slabs, "pivot")
-
-    column = spread(copies, "grp")
+    reduced, copies = couplings(core1, green_main, mine, other, 0, None)
+    (pivot_rows,) = couplings(core1, green_pivot, mine, other, slabs, slabs)
+
+    column_at = pivots // slabs
+    mine_of = jnp.stack(
+        [lax.dynamic_slice_in_dim(copies[0], (pivots[p] % slabs) * cols, cols, 2) for p in range(PANELS)]
+    )
+    bit = 1
+    while bit < grp_size:
+        came = lax.ppermute(mine_of, "grp", [(g, g ^ bit) for g in range(grp_size)])
+        take = ((grp ^ column_at) & bit) != 0
+        mine_of = jnp.where(take[:, None, None, None], came, mine_of)
+        bit *= 2
+    column = mine_of
     rows = spread(copies, "blk", same_core)
     pivot_slot = jnp.sum(jnp.where(pivots[:, None] == order, slot_of, 0), axis=1)
     row_mine = jnp.stack([lax.dynamic_index_in_dim(rows, pivot_slot[p] // 2, 0, keepdims=False) for p in range(PANELS)])
     row_other = lax.ppermute(row_mine, "blk", swap)
     inv = pivot_inverse(core1, pivot_rows, lax.ppermute(pivot_rows, "blk", swap))
-    info = jnp.concatenate([core1, pivot_slot % 2, pivots // slabs, pivots % slabs]).astype(i32)
+    info = jnp.concatenate([core1, pivot_slot % 2]).astype(i32)
     schur = schur_tile(info, inv, row_mine, row_other, column, reduced)
     return (reduced, schur)
 

time: 173 us -> 160 us (0.925)
  local copies, waits for them, and re-layouts: 21.9 us -> 9.77 us
  starting transfers between devices: 21.6 us -> 14.1 us
  blocking collectives: 23.3 us -> 29 us
  between operations: 6.04 us -> 9.93 us
  Pallas kernels: 82.6 us -> 80.6 us
    unnamed x22 -> x14, local copies, waits for them, and re-layouts: 14.9 us -> 2.1 us
    all_to_all x4 -> x2, starting transfers between devices: 20.5 us -> 9.82 us  [spread(): lax.all_to_all(x, axis, split_axis=0, concat_axis=0, tiled=True, axis_ind...]
    all_to_all x1, blocking collectives: 23.3 us -> 29 us  [spread(): lax.all_to_all(x, axis, split_axis=0, concat_axis=0, tiled=True, axis_ind...]
    ppermute x0 -> x3, starting transfers between devices: none -> 3.74 us  [on_device(): came = lax.ppermute(mine_of, 'grp', [(g, g ^ bit) for g in range(grp_size)])]
    pallas_call x2, Pallas kernels: 18.2 us -> 20.7 us  [couplings(): pl.pallas_call(functools.partial(coupling_kernel, first, left_at), out_sh...]
    pallas_call x1, Pallas kernels: 31.8 us -> 29.9 us  [pivot_inverse(): pl.pallas_call(inverse_kernel, out_shape=jax.ShapeDtypeStruct((2, order,...]
    all_to_all x4 -> x2, waiting for transfers between devices: 9.86 us -> 9.81 us  [spread(): lax.all_to_all(x, axis, split_axis=0, concat_axis=0, tiled=True, axis_ind...]
  transfers between devices with their start and end apart: 8 -> 9, of which waited for: 1 -> 1; matrix products, arithmetic and copies ran while one was open for 6% -> 6% of each run, Pallas kernels for 39% -> 43%
where the time goes in v2:
time: 160 us; the launch traced here: 157 us
  Pallas kernels  80.6 us (50%)
  blocking collectives  29 us (18%)
  starting transfers between devices  14.1 us (9%)
  between operations  9.93 us (6%)
  waiting for transfers between devices  9.82 us (6%)
  local copies, waits for them, and re-layouts  9.77 us (6%)
  other arithmetic  4.14 us (3%)
    pallas_call x1, Pallas kernels, pivot_inverse(): pl.pallas_call(inverse_kernel, out_shape=jax.ShapeDtypeStruct((2, order,...  29.9 us
    all_to_all x1, blocking collectives, spread(): lax.all_to_all(x, axis, split_axis=0, concat_axis=0, tiled=True, axis_ind...  29 us
    pallas_call x2, Pallas kernels, green_tiles(): pl.pallas_call(green_kernel, out_shape=pltpu.HBM((tiles, 2, unk, unk), bf...  27.4 us
    pallas_call x2, Pallas kernels, couplings(): pl.pallas_call(functools.partial(coupling_kernel, first, left_at), out_sh...  20.7 us
    all_to_all x2, starting transfers between devices, spread(): lax.all_to_all(x, axis, split_axis=0, concat_axis=0, tiled=True, axis_ind...  9.82 us
    all_to_all x2, waiting for transfers between devices, spread(): lax.all_to_all(x, axis, split_axis=0, concat_axis=0, tiled=True, axis_ind...  9.81 us
    ppermute x3, starting transfers between devices, on_device(): came = lax.ppermute(mine_of, 'grp', [(g, g ^ bit) for g in range(grp_size)])  3.74 us
  transfers between devices with their start and end apart: 9, of which 1 were waited for; matrix products, arithmetic and copies ran while one was open for 6% of the time, Pallas kernels for 43%

profile of v2, /device:TPU:0, one launch (start us, length us, event | category | flops | bytes accessed | tf_op | source)
XLA Modules:
  0.0 157.5 jit_solution(18226186406649287109)
XLA Ops:
  0.7 1.0 copy-done.1
  1.7 1.0 copy-done.2
  2.7 0.3 basis.1
  3.1 0.1 collective-permute-start
  3.2 0.8 select_reduce_fusion.1
  3.9 1.4 fusion.12
  5.3 0.1 pad.11.clone
  5.4 0.1 pad_add_fusion.1
  5.5 0.2 select_reduce_fusion
  5.7 0.1 pad.7.clone
  5.8 0.9 broadcast_in_dim.89
  6.7 5.5 %all-to-all-start = ((bf16[8,2,2,64,128]{4,3,2,1,0:T(8,128)(2,1)}), bf16[8,2,2,64,128]{4,3,2,1,0:T(8,128)(2,1)S(1)}, u32[]{:S(2)}, u32[]{:S(2)}) async-start(bf16[8,2,2,64,128]{4,3,2,1,0:T(8,128)(2,1)} %broadcast_in_dim.89), calls=%async_computation | async-start | bytes 1048576 | tf_op jit(solution)/shard_map/all_to_all | solution.py:364
  12.2 0.1 pad_add_fusion
  12.3 0.1 copy.49
  12.4 0.1 concatenate.13
  12.5 9.8 %all-to-all-done = bf16[8,2,2,64,128]{4,3,2,1,0:T(8,128)(2,1)S(1)} async-done(((bf16[8,2,2,64,128]{4,3,2,1,0:T(8,128)(2,1)}), bf16[8,2,2,64,128]{4,3,2,1,0:T(8,128)(2,1)S(1)}, u32[]{:S(2)}, u32[]{:S(2)}) %all-to-all-start) | async-done | bytes 524320 | tf_op jit(solution)/shard_map/all_to_all | solution.py:364
  22.3 0.8 gather_fusion
  23.2 29.0 %all_to_all.15.refs_0_ = bf16[8,6,2,64,128]{4,3,2,1,0:T(8,128)(2,1)S(1)} all-to-all(bf16[8,6,2,64,128]{4,3,2,1,0:T(8,128)(2,1)S(1)} %bitcast.27), channel_id=1, replica_groups=mesh['blk'=16,'grp'=8] {'grp'}, dimensions={0} | all-to-all | bytes 3145728 | tf_op jit(solution)/shard_map/all_to_all | solution.py:364
  52.2 0.6 fusion.18
  56.7 0.1 copy.48
  56.8 0.1 copy.43
  56.8 0.1 copy.44
  56.9 0.1 copy.45
  57.1 0.3 fusion.7
  57.5 0.8 stack.44.fr_ref
  58.3 0.8 stack.43.fl_ref
  59.2 0.6 fusion.10
  59.8 0.6 broadcast_in_dim.88.left_ids
  60.5 13.6 %shard_map.68.g_ref = bf16[2,2,1024,1024]{3,2,1,0:T(8,128)(2,1)} custom-call(s32[2]{0:T(128)S(1)} %broadcast_in_dim.88.left_ids, s32[2]{0:T(128)S(1)} %iota_add_fusion.right_ids, bf16[16,16,1024]{2,1,0:T(8,128)(2,1)S(1)} %stack.43.fl_ref, bf16[16,16,1024]{2,1,0:T(8,128)(2,1)S(1)} %stack.44.fr_ref), custom_call_target="tpu_custom_call" | custom-call | flops 62914560 | bytes 8388608 | tf_op jit(solution)/shard_map/pallas_call | solution.py:102
  74.1 0.2 fusion.8
  74.3 10.7 %shard_map.69 = (f32[2,128,256]{2,1,0:T(8,128)}, bf16[8,2,128,256]{3,2,1,0:T(8,128)(2,1)S(1)}) custom-call(s32[1]{0:T(128)} %bitcast.core_ref, bf16[2,2,1024,1024]{3,2,1,0:T(8,128)(2,1)} %shard_map.68.g_ref, bf16[8,6,2,64,128]{4,3,2,1,0:T(8,128)(2,1)S(1)} %all_to_all.15.refs_0_, bf16[8,6,2,64,128]{4,3,2,1,0:T(8,128)(2,1)} %collective-permute-done.1.refs_1_), custom_call_target="tpu_custom_call" | custom-call | flops 4294967296 | bytes 8388608 | tf_op jit(solution)/shard_map/pallas_call | solution.py:204
  85.1 0.9 collective-permute-start.4
  86.1 0.6 fusion.19
  86.7 4.3 %all-to-all-start.2 = ((bf16[8,2,128,256]{3,2,1,0:T(8,128)(2,1)}), bf16[8,2,128,256]{3,2,1,0:T(8,128)(2,1)}, u32[]{:S(2)}, u32[]{:S(2)}) async-start(bf16[8,2,128,256]{3,2,1,0:T(8,128)(2,1)} %copy-done), calls=%async_computation.2 | async-start | bytes 2097152 | tf_op jit(solution)/shard_map/all_to_all | solution.py:364
  91.0 0.1 pad_add_fusion.3.info
  96.2 0.6 broadcast_in_dim.98.left_ids
  96.8 13.8 %shard_map.70.g_ref = bf16[2,2,1024,1024]{3,2,1,0:T(8,128)(2,1)} custom-call(s32[2]{0:T(128)S(1)} %broadcast_in_dim.98.left_ids, s32[2]{0:T(128)S(1)} %get-tuple-element.31.right_ids, bf16[16,16,1024]{2,1,0:T(8,128)(2,1)S(1)} %stack.43.fl_ref, bf16[16,16,1024]{2,1,0:T(8,128)(2,1)S(1)} %stack.44.fr_ref), custom_call_target="tpu_custom_call" | custom-call | flops 62914560 | bytes 8388608 | tf_op jit(solution)/shard_map/pallas_call | solution.py:102
  110.6 0.1 broadcast_select_fusion
  110.7 0.7 collective-permute-start.5
  111.5 9.9 %shard_map.71.mine_ref = f32[2,128,256]{2,1,0:T(8,128)S(1)} custom-call(s32[1]{0:T(128)} %bitcast.core_ref, bf16[2,2,1024,1024]{3,2,1,0:T(8,128)(2,1)} %shard_map.70.g_ref, bf16[8,6,2,64,128]{4,3,2,1,0:T(8,128)(2,1)S(1)} %all_to_all.15.refs_0_, bf16[8,6,2,64,128]{4,3,2,1,0:T(8,128)(2,1)} %collective-permute-done.1.refs_1_), custom_call_target="tpu_custom_call" | custom-call | flops 4294967296 | bytes 8388608 | tf_op jit(solution)/shard_map/pallas_call | solution.py:204
  121.4 0.1 collective-permute-start.2
  121.5 0.1 broadcast_select_fusion.1
  121.6 2.1 %collective-permute-start.6 = (bf16[2,2,128,128]{3,2,1,0:T(8,128)(2,1)S(1)}, bf16[2,2,128,128]{3,2,1,0:T(8,128)(2,1)S(1)}, u32[]{:S(2)}, u32[]{:S(2)}) collective-permute-start(bf16[2,2,128,128]{3,2,1,0:T(8,128)(2,1)S(1)} %broadcast_select_fusion.1), channel_id=1, source_target_pairs={{0,4},{1,5},{2,6},{3,7},{4,0},{5,1},{6,2},{7,3},{8,12},{9,13},{10,... | collective-permute-start | bytes 393224 | tf_op jit(solution)/shard_map/ppermute | solution.py:405
  123.7 1.0 constant_dynamic-slice_fusion.3
  124.7 0.4 collective-permute-start.3
  125.1 29.9 %pivot_inverse.1.inv_ref = f32[2,256,256]{2,1,0:T(8,128)S(1)} custom-call(s32[1]{0:T(128)} %bitcast.core_ref, f32[2,128,256]{2,1,0:T(8,128)S(1)} %shard_map.71.mine_ref, f32[2,128,256]{2,1,0:T(8,128)S(1)} %collective-permute-done.2.other_ref), custom_call_target="tpu_custom_call" | custom-call | flops 12000000000 | bytes 1048576 | tf_op jit(solution)/shard_map/pivot_inverse/pallas_call | solution.py:296
  155.1 0.1 broadcast_select_fusion.2.c_ref
  155.2 2.3 %schur.1 = f32[2,128,256]{2,1,0:T(8,128)} custom-call(s32[3]{0:T(128)S(1)} %pad_add_fusion.3.info, f32[2,256,256]{2,1,0:T(8,128)S(1)} %pivot_inverse.1.inv_ref, bf16[2,2,128,256]{3,2,1,0:T(8,128)(2,1)S(1)} %pad_maximum_fusion.mine_ref, bf16[2,2,128,256]{3,2,1,0:T(8,128)(2,1)S(1)} %collective-permute-done.3.other_ref, ...), custom_call_target="tpu_custom_call" | custom-call | tf_op jit(solution)/shard_map/schur/pallas_call | solution.py:342
  (40 shorter events, 0.5 us)
Async XLA Ops:
  0.6 1.0 copy-start.1
  1.7 1.0 copy-start.2
  3.1 2.7 %collective-permute-start = (bf16[2,64,128]{2,1,0:T(8,128)(2,1)S(1)}, bf16[2,64,128]{2,1,0:T(8,128)(2,1)S(1)}, u32[]{:S(2)}, u32[]{:S(2)}) collective-permute-start(bf16[2,64,128]{2,1,0:T(8,128)(2,1)S(1)} %get-tuple-element.7), channel_id=1, source_target_pairs={{0,8},{8,0},{16,24},{24,16},{32,40},{40,32},{48,56},{56,48},{64,72... | collective-permute-start | bytes 98312 | tf_op jit(solution)/shard_map/ppermute | solution.py:373
  6.7 15.6 %all-to-all-start = ((bf16[8,2,2,64,128]{4,3,2,1,0:T(8,128)(2,1)}), bf16[8,2,2,64,128]{4,3,2,1,0:T(8,128)(2,1)S(1)}, u32[]{:S(2)}, u32[]{:S(2)}) async-start(bf16[8,2,2,64,128]{4,3,2,1,0:T(8,128)(2,1)} %broadcast_in_dim.89), calls=%async_computation | async-start | bytes 1048576 | tf_op jit(solution)/shard_map/all_to_all | solution.py:364
  23.2 29.1 %copy-start.5 = (s32[16]{0:T(128)S(1)}, s32[16]{0:T(128)}, u32[]{:S(2)}) copy-start(s32[16]{0:T(128)} %param.9) | copy-start | bytes 196
  23.2 33.5 %copy-start.4 = (s32[3,16,1024]{2,1,0:T(8,128)S(1)}, s32[3,16,1024]{2,1,0:T(8,128)}, u32[]{:S(2)}) copy-start(s32[3,16,1024]{2,1,0:T(8,128)} %param.7) | copy-start | bytes 589828
  52.2 22.1 %collective-permute-start.1 = (bf16[8,6,2,64,128]{4,3,2,1,0:T(8,128)(2,1)S(1)}, bf16[8,6,2,64,128]{4,3,2,1,0:T(8,128)(2,1)}, u32[]{:S(2)}, u32[]{:S(2)}) collective-permute-start(bf16[8,6,2,64,128]{4,3,2,1,0:T(8,128)(2,1)S(1)} %all_to_all.15.refs_0_), channel_id=1, source_target_pairs={{0,8},{8,0},{16,24},{24,16},{32,40},{40,32},{48,56},{56,48},{64,72... | collective-permute-start | bytes 4718600 | tf_op jit(solution)/shard_map/ppermute | solution.py:394
  57.1 2.1 %copy-start.6 = (s32[16]{0:T(128)S(1)}, s32[16]{0:T(128)}, u32[]{:S(2)}) copy-start(s32[16]{0:T(128)} %param.8) | copy-start | bytes 196
  85.1 1.0 copy-start
  85.1 25.5 %collective-permute-start.4 = (bf16[2,2,128,128]{3,2,1,0:T(8,128)(2,1)S(1)}, bf16[2,2,128,128]{3,2,1,0:T(8,128)(2,1)S(1)}, u32[]{:S(2)}, u32[]{:S(2)}) collective-permute-start(bf16[2,2,128,128]{3,2,1,0:T(8,128)(2,1)S(1)} %pad_maximum_fusion.1), channel_id=1, source_target_pairs={{0,1},{1,0},{2,3},{3,2},{4,5},{5,4},{6,7},{7,6},{8,9},{9,8},{10,11... | collective-permute-start | bytes 393224 | tf_op jit(solution)/shard_map/ppermute | solution.py:405
  86.7 37.0 %all-to-all-start.2 = ((bf16[8,2,128,256]{3,2,1,0:T(8,128)(2,1)}), bf16[8,2,128,256]{3,2,1,0:T(8,128)(2,1)}, u32[]{:S(2)}, u32[]{:S(2)}) async-start(bf16[8,2,128,256]{3,2,1,0:T(8,128)(2,1)} %copy-done), calls=%async_computation.2 | async-start | bytes 2097152 | tf_op jit(solution)/shard_map/all_to_all | solution.py:364
  110.7 10.8 %collective-permute-start.5 = (bf16[2,2,128,128]{3,2,1,0:T(8,128)(2,1)S(1)}, bf16[2,2,128,128]{3,2,1,0:T(8,128)(2,1)S(1)}, u32[]{:S(2)}, u32[]{:S(2)}) collective-permute-start(bf16[2,2,128,128]{3,2,1,0:T(8,128)(2,1)S(1)} %broadcast_select_fusion), channel_id=1, source_target_pairs={{0,2},{1,3},{2,0},{3,1},{4,6},{5,7},{6,4},{7,5},{8,10},{9,11},{10,... | collective-permute-start | bytes 393224 | tf_op jit(solution)/shard_map/ppermute | solution.py:405
  121.4 3.7 %collective-permute-start.2 = (f32[2,128,256]{2,1,0:T(8,128)S(1)}, f32[2,128,256]{2,1,0:T(8,128)S(1)}, u32[]{:S(2)}, u32[]{:S(2)}) collective-permute-start(f32[2,128,256]{2,1,0:T(8,128)S(1)} %shard_map.71.mine_ref), channel_id=1, source_target_pairs={{0,8},{8,0},{16,24},{24,16},{32,40},{40,32},{48,56},{56,48},{64,72... | collective-permute-start | bytes 786440 | tf_op jit(solution)/shard_map/ppermute | solution.py:414
  121.6 33.4 %collective-permute-start.6 = (bf16[2,2,128,128]{3,2,1,0:T(8,128)(2,1)S(1)}, bf16[2,2,128,128]{3,2,1,0:T(8,128)(2,1)S(1)}, u32[]{:S(2)}, u32[]{:S(2)}) collective-permute-start(bf16[2,2,128,128]{3,2,1,0:T(8,128)(2,1)S(1)} %broadcast_select_fusion.1), channel_id=1, source_target_pairs={{0,4},{1,5},{2,6},{3,7},{4,0},{5,1},{6,2},{7,3},{8,12},{9,13},{10,... | collective-permute-start | bytes 393224 | tf_op jit(solution)/shard_map/ppermute | solution.py:405
  124.7 30.5 %copy-start.3 = (f32[2,128,256]{2,1,0:T(8,128)S(1)}, f32[2,128,256]{2,1,0:T(8,128)}, u32[]{:S(2)}) copy-start(f32[2,128,256]{2,1,0:T(8,128)} %get-tuple-element.4.r_ref) | copy-start | bytes 786436
  124.7 30.4 %collective-permute-start.3 = (bf16[2,2,128,256]{3,2,1,0:T(8,128)(2,1)S(1)}, bf16[2,2,128,256]{3,2,1,0:T(8,128)(2,1)S(1)}, u32[]{:S(2)}, u32[]{:S(2)}) collective-permute-start(bf16[2,2,128,256]{3,2,1,0:T(8,128)(2,1)S(1)} %pad_maximum_fusion.mine_ref), channel_id=1, source_target_pairs={{0,8},{8,0},{16,24},{24,16},{32,40},{40,32},{48,56},{56,48},{64,72... | collective-permute-start | bytes 786440 | tf_op jit(solution)/shard_map/ppermute | solution.py:413

commit v3 on v2

v3 whole, which is shorter than its diff:
```python
import functools

import jax
import jax.numpy as jnp
import numpy as np
from jax import lax
from jax.experimental import pallas as pl
from jax.experimental.pallas import tpu as pltpu
from jax.sharding import PartitionSpec as P


PANELS = 2
bf16 = jnp.bfloat16
f32 = jnp.float32
i32 = jnp.int32

SELF_REAL = 6.0
SELF_IMAG = -1.5
TURNS = 1.3 / (2 * np.pi)
SHIFT = float(1.5 * 2**23)
SIN = (4.44288283, -7.30824115, 3.60628896, -0.8457636, 0.10920575)
COS = (-1.4142135, 6.97885099, -5.73946117, 1.88356298, -0.31069819)
VMEM = pl.BlockSpec(memory_space=pltpu.VMEM)
SMEM = pl.BlockSpec(memory_space=pltpu.SMEM)
MB = 1 << 20
COUPLE_ROWS = 512
GREEN_ROWS = 512
STRIPS = 4


def horner(coefs, g):
    r = coefs[-1]
    for k in coefs[-2::-1]:
        r = r * g + k
    return r


def half_green(sq):
    inv_r = lax.rsqrt(sq)
    turns = (sq * inv_r) * TURNS
    f = turns - ((turns + SHIFT) - SHIFT)
    g = f * f
    s = horner(SIN, g) * f
    c = horner(COS, g)
    scaled = s * inv_r
    return inv_r - s * scaled, c * scaled


def basis_kernel(core_ref, inv_ref, exc_ref, own_ref, keep_ref, send_ref, both):
    er, ei = exc_ref[0, 0], exc_ref[1, 0]
    j = jnp.dot(inv_ref[0, 0], jnp.concatenate([er, ei], 1), preferred_element_type=f32)
    j += jnp.dot(inv_ref[1, 0], jnp.concatenate([-ei, er], 1), preferred_element_type=f32)
    rows, cols = j.shape[0], j.shape[1] // 2
    half = rows // 2
    both[...] = j.astype(bf16)
    mine = pl.multiple_of(core_ref[0] * half, half)
    other = pl.multiple_of((1 - core_ref[0]) * half, half)
    for part in range(2):
        own_ref[0, part] = both[:, part * cols : (part + 1) * cols]
        keep_ref[part] = both[pl.ds(mine, half), part * cols : (part + 1) * cols]
        send_ref[part] = both[pl.ds(other, half), part * cols : (part + 1) * cols]


def basis_rows(core, inverse, excite):
    rows, cols = inverse.shape[2], excite.shape[3]
    half = jax.ShapeDtypeStruct((2, rows // 2, cols), bf16)
    return pl.pallas_call(
        basis_kernel,
        out_shape=(jax.ShapeDtypeStruct((1, 2, rows, cols), bf16), half, half),
        in_specs=[SMEM, VMEM, VMEM],
        out_specs=(VMEM, VMEM, VMEM),
        scratch_shapes=[pltpu.VMEM((rows, 2 * cols), bf16)],
        compiler_params=pltpu.CompilerParams(vmem_limit_bytes=8 * MB),
        name="basis",
    )(core, inverse, excite)


def features(coords_ref, block, left):
    x, y, z = [coords_ref[d, pl.ds(block, 1), :] for d in range(3)]
    norm = x * x + y * y + z * z
    low = norm & 63
    high = norm - low
    one, zero = jnp.ones_like(norm), jnp.zeros_like(norm)
    rows = [-2 * x, -2 * y, -2 * z, high, low, one, one] if left else [x, y, z, one, one, high, low]
    return jnp.concatenate([v.astype(f32) for v in rows + [zero]], 0).astype(bf16)


def green_kernel(first, at_ref, blocks_ref, panel_ref, coords_ref, *refs):
    g_ref, fl_ref, fr_ref, sq_ref = refs[-4:]
    rows, _ = sq_ref.shape
    tile, chunk = pl.program_id(0) + first, pl.program_id(1)
    own, grp, core = blocks_ref[at_ref[0]], at_ref[1], at_ref[2]
    main = tile < 2
    left = jnp.where(main, own, panel_ref[core])
    right = jnp.where(main, grp * 2 + tile, panel_ref[jnp.maximum(tile - 2, 0)])

    @pl.when(chunk == 0)
    def _():
        fl_ref[...] = features(coords_ref, left, True)
        fr_ref[...] = features(coords_ref, right, False)

    at = pl.ds(pl.multiple_of(chunk * rows, rows), rows)
    sq_ref[...] = lax.dot_general(
        fl_ref[:, at], fr_ref[...], (((0,), (0,)), ((), ())), preferred_element_type=f32
    )

    def strip(i, _):
        r = pl.ds(pl.multiple_of(i * 8, 8), 8)
        re, im = half_green(sq_ref[r, :])
        g_ref[0, 0, r, :] = re.astype(bf16)
        g_ref[0, 1, r, :] = im.astype(bf16)
        return 0

    lax.fori_loop(0, rows // 8, strip, 0, unroll=STRIPS)

    @pl.when(left == right)
    def _():
        same = lax.broadcasted_iota(i32, (rows, rows), 0) == lax.broadcasted_iota(i32, (rows, rows), 1)
        for part, value in ((0, SELF_REAL), (1, SELF_IMAG)):
            block = g_ref[0, part, :, at].astype(f32)
            g_ref[0, part, :, at] = jnp.where(same, value, block).astype(bf16)


def green_tiles(at, blocks, panel, coordinates, first, count, tiles, held):
    unk = coordinates.shape[2]
    rows = GREEN_ROWS
    return pl.pallas_call(
        functools.partial(green_kernel, first),
        out_shape=pltpu.HBM((tiles, 2, unk, unk), bf16),
        grid=(count, unk // rows),
        in_specs=[SMEM, SMEM, SMEM, pl.BlockSpec(coordinates.shape, lambda t, m: (0, 0, 0))]
        + [pl.BlockSpec(memory_space=pltpu.HBM)] * len(held),
        out_specs=pl.BlockSpec((1, 2, rows, unk), lambda t, m: (t + first, 0, m, 0)),
        scratch_shapes=[pltpu.VMEM((8, unk), bf16), pltpu.VMEM((8, unk), bf16), pltpu.VMEM((rows, unk), f32)],
        input_output_aliases={4: 0} if held else {},
        compiler_params=pltpu.CompilerParams(vmem_limit_bytes=10 * MB),
        cost_estimate=pl.CostEstimate(
            flops=count * unk * unk * 30, transcendentals=count * unk * unk, bytes_accessed=count * unk * unk * 4
        ),
    )(at, blocks, panel, coordinates, *held)


def coupling_kernel(pivot, at_ref, panel_ref, g_ref, mine_ref, other_ref, *refs):
    if pivot:
        out_ref, lhs, stage, top, bottom, acc = refs
    else:
        pieces = refs[:4]
        out_ref, copies_ref, column_ref, lhs, stage, top, bottom, acc = refs[5:]
    tile, chunk = pl.program_id(0), pl.program_id(1)
    chunks = pl.num_programs(1)
    grp, core = at_ref[1], at_ref[2]
    groups, _, _, half, cols = mine_ref.shape
    rows = g_ref.shape[2]
    first = 2 if pivot else 0
    halves = ((mine_ref, core), (other_ref, 1 - core))

    def rows_of(g, part):
        return pl.ds(pl.multiple_of(g * 2 * half + part * half, half), half)

    @pl.when((tile == 0) & (chunk == 0))
    def _():
        if pivot:
            for g in range(groups):
                for src, part in halves:
                    r = rows_of(g, part)
                    stage[r, :cols] = src[g, first + core, 0]
                    stage[r, cols:] = src[g, first + core, 1]
        else:
            step = 0
            for piece in pieces:
                for k in range(piece.shape[0]):
                    r = pl.ds(pl.multiple_of((grp ^ step) * 2 * half, 2 * half), 2 * half)
                    stage[r, :cols] = piece[k, 0]
                    stage[r, cols:] = piece[k, 1]
                    step += 1
        lhs[...] = stage[...].T

    @pl.when(chunk == 0)
    def _():
        acc[...] = jnp.zeros_like(acc)
        for g in range(groups):
            for src, part in halves:
                r = rows_of(g, part)
                jr, ji = src[g, first + tile, 0], src[g, first + tile, 1]
                top[r, :cols] = jr
                top[r, cols:] = ji
                bottom[r, :cols] = -ji
                bottom[r, cols:] = jr

    y = jnp.dot(g_ref[0, 0], top[...], preferred_element_type=f32)
    y += jnp.dot(g_ref[0, 1], bottom[...], preferred_element_type=f32)
    y_hi = y.astype(bf16)
    y_lo = (y - y_hi.astype(f32)).astype(bf16)
    left = lhs[:, pl.ds(pl.multiple_of(chunk * rows, rows), rows)]
    acc[...] += jnp.dot(left, y_hi, preferred_element_type=f32) + jnp.dot(left, y_lo, preferred_element_type=f32)

    @pl.when(chunk == chunks - 1)
    def _():
        both = (2.0 * (acc[:cols, :cols] + acc[cols:, cols:]), 2.0 * (acc[:cols, cols:] - acc[cols:, :cols]))
        for part, value in enumerate(both):
            out_ref[part] = value
            if not pivot:
                for k in range(copies_ref.shape[0]):
                    copies_ref[k, part] = value.astype(bf16)
                for p in range(PANELS):
                    here = panel_ref[p] == grp * 2 + tile

                    @pl.when(here | (tile == 0))
                    def _():
                        column_ref[p, part] = value.astype(bf16)


def couplings(at, panel, green, mine, other, pieces, after, pivot):
    _, _, unk, _ = green.shape
    cols = mine.shape[4]
    tiles = 2
    first = 2 if pivot else 0
    rows = COUPLE_ROWS
    copies = 8
    whole = lambda x: pl.BlockSpec(x.shape, lambda t, m: (0,) * x.ndim)
    out_shape = [jax.ShapeDtypeStruct((2, cols, tiles * cols), f32)]
    out_specs = [pl.BlockSpec((2, cols, cols), lambda t, m: (0, 0, t))]
    if not pivot:
        out_shape.append(jax.ShapeDtypeStruct((copies, 2, cols, tiles * cols), bf16))
        out_specs.append(pl.BlockSpec((copies, 2, cols, cols), lambda t, m: (0, 0, 0, t)))
        out_shape.append(jax.ShapeDtypeStruct((PANELS, 2, cols, cols), bf16))
        out_specs.append(pl.BlockSpec((PANELS, 2, cols, cols), lambda t, m: (0, 0, 0, 0)))
    return pl.pallas_call(
        functools.partial(coupling_kernel, pivot),
        out_shape=out_shape,
        grid=(tiles, unk // rows),
        in_specs=[SMEM, SMEM, pl.BlockSpec((1, 2, rows, unk), lambda t, m: (t + first, 0, m, 0))]
        + [whole(x) for x in (mine, other, *pieces)]
        + [pl.BlockSpec(memory_space=pl.ANY)] * len(after),
        out_specs=out_specs,
        scratch_shapes=[
            pltpu.VMEM((2 * cols, unk), bf16),
            pltpu.VMEM((unk, 2 * cols), bf16),
            pltpu.VMEM((unk, 2 * cols), bf16),
            pltpu.VMEM((unk, 2 * cols), bf16),
            pltpu.VMEM((2 * cols, 2 * cols), f32),
        ],
        compiler_params=pltpu.CompilerParams(vmem_limit_bytes=20 * MB),
        cost_estimate=pl.CostEstimate(
            flops=tiles * unk * unk * 2048, transcendentals=0, bytes_accessed=tiles * unk * unk * 4
        ),
    )(at, panel, pltpu.with_memory_space_constraint(green, pltpu.HBM), mine, other, *pieces, *after)


WIDE = 128
PANEL = 32


def small_exchange(ar, ai, sub):
    ar, ai = list(ar), list(ai)
    for s in range(8):
        row = lambda x: jnp.broadcast_to(x[s : s + 1], x.shape)
        pr, pi = row(ar[s]), row(ai[s])
        scale = 1.0 / (pr * pr + pi * pi)
        qr, qi = pr * scale, pi * scale
        br, bi = ar[s], ai[s]
        for m in range(8):
            if m == s:
                vr, vi = -qr, qi
                xr, xi = br * qr + bi * qi, bi * qr - br * qi
            else:
                cr, ci = row(ar[m]), row(ai[m])
                wr, wi = br * cr - bi * ci, br * ci + bi * cr
                vr, vi = cr * qr + ci * qi, ci * qr - cr * qi
                xr, xi = ar[m] - (wr * qr + wi * qi), ai[m] - (wi * qr - wr * qi)
            ar[m], ai[m] = jnp.where(sub == s, -vr, xr), jnp.where(sub == s, -vi, xi)
    return ar, ai


def times(ar, ai, xr, xi, spread):
    nr = ni = None
    for m in range(8):
        cr, ci = spread(xr[m : m + 1]), spread(xi[m : m + 1])
        r, i = ar[m] * cr - ai[m] * ci, ar[m] * ci + ai[m] * cr
        nr, ni = (r, i) if nr is None else (nr + r, ni + i)
    return nr, ni


def inverse_kernel(kb, at_ref, first_ref, second_ref, re_ref, im_ref, rhs_ref):
    if kb == 0:
        core = at_ref[2]
        rows = first_ref.shape[1]
        for src, part in ((first_ref, core), (second_ref, 1 - core)):
            r = pl.ds(pl.multiple_of(part * rows, rows), rows)
            for h in range(2):
                re_ref[h, r, :] = src[0][:, h * WIDE : (h + 1) * WIDE]
                im_ref[h, r, :] = src[1][:, h * WIDE : (h + 1) * WIDE]
    else:
        re_ref[...] = first_ref[...]
        im_ref[...] = second_ref[...]
    rhs_ref[...] = jnp.zeros_like(rhs_ref)
    lane = lax.broadcasted_iota(i32, (8, WIDE), 1)
    sub = lax.broadcasted_iota(i32, (8, WIDE), 0)
    spread = lambda x: jnp.broadcast_to(x, (8, WIDE))
    groups = PANEL // 8

    order = (kb, 1 - kb)
    for t in range(WIDE // PANEL):
        r = slice(kb * WIDE + t * PANEL, kb * WIDE + (t + 1) * PANEL)
        block = [(re_ref[h, r, :], im_ref[h, r, :]) for h in order]
        tr = [[b[0][8 * g : 8 * g + 8] for g in range(groups)] for b in block]
        ti = [[b[1][8 * g : 8 * g + 8] for g in range(groups)] for b in block]
        for gs in range(groups):
            first = t * PANEL + 8 * gs
            ar = [[spread(x[:, first + m : first + m + 1]) for m in range(8)] for x in tr[0]]
            ai = [[spread(x[:, first + m : first + m + 1]) for m in range(8)] for x in ti[0]]
            dr, di = small_exchange(ar[gs], ai[gs], sub)
            within = (lane >= first) & (lane < first + 8)
            unit = jnp.where(lane == sub + first, -1.0, 0.0)
            xr = [jnp.where(within, unit, tr[0][gs]), tr[1][gs]]
            xi = [jnp.where(within, 0.0, ti[0][gs]), ti[1][gs]]
            for h in range(2):
                nr, ni = times(dr, di, xr[h], xi[h], spread)
                tr[h][gs], ti[h][gs] = -nr, -ni
            for g in range(groups):
                if g == gs:
                    continue
                for h in range(2):
                    nr, ni = times(ar[g], ai[g], tr[h][gs], ti[h][gs], spread)
                    yr, yi = tr[h][g], ti[h][g]
                    if h == 0:
                        yr, yi = jnp.where(within, 0.0, yr), jnp.where(within, 0.0, yi)
                    tr[h][g], ti[h][g] = yr + nr, yi + ni
        pr = jnp.concatenate([jnp.concatenate(tr[h], 0) for h in range(2)], 1)
        pi = jnp.concatenate([jnp.concatenate(ti[h], 0) for h in range(2)], 1)
        top, low = slice(t * PANEL, (t + 1) * PANEL), slice(WIDE + t * PANEL, WIDE + (t + 1) * PANEL)
        rhs_ref[top, :] = jnp.concatenate([pr, pi], 1)
        rhs_ref[low, :] = jnp.concatenate([-pi, pr], 1)
        old = jnp.concatenate([re_ref[kb], im_ref[kb]], 1)
        upd = jnp.dot(old, rhs_ref[...], precision=lax.Precision.HIGHEST, preferred_element_type=f32)
        rhs_ref[top, :] = jnp.zeros((PANEL, 4 * WIDE), f32)
        rhs_ref[low, :] = jnp.zeros((PANEL, 4 * WIDE), f32)
        wide_lane = lax.broadcasted_iota(i32, upd[:, :WIDE].shape, 1)
        gone = (wide_lane >= t * PANEL) & (wide_lane < (t + 1) * PANEL)
        re_ref[kb] = jnp.where(gone, 0.0, re_ref[kb]) + upd[:, :WIDE]
        im_ref[kb] = jnp.where(gone, 0.0, im_ref[kb]) + upd[:, 2 * WIDE : 3 * WIDE]
        re_ref[1 - kb] += upd[:, WIDE : 2 * WIDE]
        im_ref[1 - kb] += upd[:, 3 * WIDE :]
        for n, h in enumerate(order):
            re_ref[h, r, :] = pr[:, n * WIDE : (n + 1) * WIDE]
            im_ref[h, r, :] = pi[:, n * WIDE : (n + 1) * WIDE]


def pivot_exchange(kb, at, first, second):
    order = PANELS * WIDE
    part = jax.ShapeDtypeStruct((2, order, WIDE), f32)
    return pl.pallas_call(
        functools.partial(inverse_kernel, kb),
        out_shape=(part, part),
        in_specs=[SMEM, VMEM, VMEM],
        out_specs=(VMEM, VMEM),
        scratch_shapes=[pltpu.VMEM((2 * WIDE, 4 * WIDE), f32)],
        compiler_params=pltpu.CompilerParams(vmem_limit_bytes=12 * MB),
        cost_estimate=pl.CostEstimate(flops=int(6e9), transcendentals=0, bytes_accessed=1 << 20),
    )(at, first, second)


def split3(x):
    hi = x.astype(bf16)
    rest = x - hi.astype(f32)
    mid = rest.astype(bf16)
    low = (rest - mid.astype(f32)).astype(bf16)
    return hi, mid, low


def schur_kernel(info, re_ref, im_ref, mine_ref, other_ref, c_ref, r_ref, out_ref):
    core = info[0]
    funcs = mine_ref.shape[2]
    b = []
    for p in range(PANELS):
        local = info[1 + p] == core
        b.append([jnp.where(local, mine_ref[p, k].astype(f32), other_ref[p, k].astype(f32)).astype(bf16) for k in range(2)])
    br = jnp.concatenate([b[p][0] for p in range(PANELS)], 0)
    bi = jnp.concatenate([b[p][1] for p in range(PANELS)], 0)
    right = jnp.concatenate([jnp.concatenate([br, bi], 1), jnp.concatenate([-bi, br], 1)], 0)
    w = jnp.zeros((PANELS * funcs, right.shape[1]), f32)
    for x in split3(jnp.concatenate([re_ref[0], re_ref[1], im_ref[0], im_ref[1]], 1)):
        w += jnp.dot(x, right, preferred_element_type=f32)
    cols = w.shape[1] // 2
    w_hi = w.astype(bf16)
    w_lo = (w - w_hi.astype(f32)).astype(bf16)
    cr = jnp.concatenate([c_ref[0, 0], c_ref[1, 0]], 1)
    ci = jnp.concatenate([c_ref[0, 1], c_ref[1, 1]], 1)
    left = jnp.concatenate([cr, ci], 0)
    prod = jnp.dot(left, w_hi, preferred_element_type=f32) + jnp.dot(left, w_lo, preferred_element_type=f32)
    rows = cr.shape[0]
    out_ref[0] = r_ref[0] - (prod[:rows, :cols] - prod[rows:, cols:])
    out_ref[1] = r_ref[1] - (prod[:rows, cols:] + prod[rows:, :cols])


def schur_tile(info, re, im, mine, other, column, reduced):
    return pl.pallas_call(
        schur_kernel,
        out_shape=jax.ShapeDtypeStruct(reduced.shape, f32),
        in_specs=[SMEM] + [VMEM] * 6,
        out_specs=VMEM,
        compiler_params=pltpu.CompilerParams(vmem_limit_bytes=12 * MB),
        name="schur",
    )(info, re, im, mine, other, column, reduced)


def on_device(inverse, excite, coordinates, block_of_slot, panel_order):
    blk_size, grp_size = lax.axis_size("blk"), lax.axis_size("grp")
    blocks = block_of_slot.shape[0]
    slot, grp = lax.axis_index("blk").astype(i32), lax.axis_index("grp").astype(i32)
    core = slot % 2
    slabs = blocks // grp_size
    swap = [(i, i ^ 1) for i in range(blk_size)]
    same_core = [list(range(c, blk_size, 2)) for c in range(2)]
    at = jnp.stack([slot, grp, core])

    def spread(x, axis, groups=None):
        return lax.all_to_all(x, axis, split_axis=0, concat_axis=0, tiled=True, axis_index_groups=groups)

    order = jnp.arange(blocks, dtype=i32)
    slot_of = jnp.sum(jnp.where(block_of_slot[None, :] == order[:, None], order[None, :], 0), axis=1)
    pivots = panel_order[:PANELS]

    own, keep, send = basis_rows(core.reshape(1), inverse, excite)
    got = lax.ppermute(send, "blk", swap)
    pair = jnp.stack([keep, got])
    pair = jnp.broadcast_to(pair[None], (blk_size // 2, *pair.shape))
    sliced = spread(pair, "blk", same_core)
    sliced = sliced.reshape(blk_size, *keep.shape)

    pieces, held, bit = [own], own, 1
    while bit < grp_size:
        pieces.append(lax.ppermute(held, "grp", [(g, g ^ bit) for g in range(grp_size)]))
        bit *= 2
        if bit < grp_size:
            held = jnp.concatenate([held, pieces[-1]], 0)

    green = green_tiles(at, block_of_slot, panel_order, coordinates, 0, 1, 2 + PANELS, [])
    green = green_tiles(at, block_of_slot, panel_order, coordinates, 1, 1, 2 + PANELS, [green])
    green = green_tiles(at, block_of_slot, panel_order, coordinates, 2, PANELS, 2 + PANELS, [green])

    wanted = jnp.concatenate(
        [order.reshape(grp_size, slabs), jnp.broadcast_to(pivots[None], (grp_size, PANELS))], axis=1
    )
    from_slot = jnp.sum(jnp.where(wanted[:, :, None] == order, slot_of, 0), axis=2)
    place = (from_slot // 2) * 2 + (from_slot % 2 + core) % 2
    picked = sliced.at[place.reshape(-1)].get(mode="promise_in_bounds").reshape(*place.shape, *keep.shape)
    mine = spread(picked, "grp")
    other = lax.ppermute(mine, "blk", swap)

    (pivot_rows,) = couplings(at, panel_order, green, mine, other, [], [], True)
    pivot_other = lax.ppermute(pivot_rows, "blk", swap)
    reduced, copies, column = couplings(at, panel_order, green, mine, other, pieces, [pivot_rows], False)

    rows = spread(copies, "blk", same_core)
    column_at = pivots // slabs
    bit = 1
    while bit < grp_size:
        came = lax.ppermute(column, "grp", [(g, g ^ bit) for g in range(grp_size)])
        take = ((grp ^ column_at) & bit) != 0
        column = jnp.where(take[:, None, None, None], came, column)
        bit *= 2
    pivot_slot = jnp.sum(jnp.where(pivots[:, None] == order, slot_of, 0), axis=1)
    row_mine = jnp.stack([lax.dynamic_index_in_dim(rows, pivot_slot[p] // 2, 0, keepdims=False) for p in range(PANELS)])
    row_other = lax.ppermute(row_mine, "blk", swap)
    core1 = core.reshape(1)
    re, im = pivot_exchange(0, at, pivot_rows, pivot_other)
    re, im = pivot_exchange(1, at, re, im)
    info = jnp.concatenate([core1, pivot_slot % 2]).astype(i32)
    schur = schur_tile(info, re, im, row_mine, row_other, column, reduced)
    return (reduced, schur)


def solution(mesh):
    placed = (P(None, "blk", "grp", None), P(None, "blk", None, None), P(), P(), P())
    return jax.shard_map(
        on_device,
        mesh=mesh,
        in_specs=placed,
        out_specs=(P(None, "blk", "grp"), P(None, "blk", "grp")),
        check_vma=False,
    )
```

time: 160 us -> 142 us (0.89)
  blocking collectives: 29 us -> 0 us
  waiting for transfers between devices: 9.82 us -> 31 us
  Pallas kernels: 80.6 us -> 66.2 us
  starting transfers between devices: 14.1 us -> 25.8 us
  between operations: 9.93 us -> 5.98 us
  other arithmetic: 4.14 us -> 1.79 us
    all_to_all x1 -> x0, blocking collectives: 29 us -> none  [spread(): lax.all_to_all(x, axis, split_axis=0, concat_axis=0, tiled=True, axis_ind...]
    pallas_call x6 -> x8, Pallas kernels: 78.3 us -> 63.9 us  [the longest x3 27.9 us: green_tiles(): pl.pallas_call(functools.partial(green_kernel, first), out_shape=pltpu.HB...]
    all_to_all x2 -> x3, waiting for transfers between devices: 9.81 us -> 23.7 us  [spread(): lax.all_to_all(x, axis, split_axis=0, concat_axis=0, tiled=True, axis_ind...]
    all_to_all x2 -> x3, starting transfers between devices: 9.82 us -> 17.4 us  [spread(): lax.all_to_all(x, axis, split_axis=0, concat_axis=0, tiled=True, axis_ind...]
    ppermute x4 -> x7, waiting for transfers between devices: 0.01 us -> 6.91 us  [the longest x3 6.9 us: on_device(): lax.ppermute(held, 'grp', [(g, g ^ bit) for g in range(grp_size)])]
    ppermute x4 -> x7, starting transfers between devices: 3.82 us -> 7.94 us  [the longest x3 4.55 us: on_device(): lax.ppermute(held, 'grp', [(g, g ^ bit) for g in range(grp_size)])]
    unnamed x14, local copies, waits for them, and re-layouts: 2.1 us -> 4.32 us
    reduce_sum x3 -> x0, other arithmetic: 2.06 us -> none  [the longest x1 1.41 us: on_device(): pivot_mine = jnp.sum(jnp.where(jnp.arange(PANELS) == core, pivots, 0))]
  transfers between devices with their start and end apart: 9 -> 13, of which waited for: 1 -> 6; matrix products, arithmetic and copies ran while one was open for 6% -> 2% of each run, Pallas kernels for 43% -> 39%
where the time goes in v3:
time: 142 us; the launch traced here: 139 us
  Pallas kernels  66.2 us (47%)
  waiting for transfers between devices  31 us (22%)
  starting transfers between devices  25.8 us (18%)
  local copies, waits for them, and re-layouts  8.46 us (6%)
  between operations  5.98 us (4%)
  other arithmetic  1.79 us (1%)
    pallas_call x3, Pallas kernels, green_tiles(): pl.pallas_call(functools.partial(green_kernel, first), out_shape=pltpu.HB...  27.9 us
    all_to_all x3, waiting for transfers between devices, spread(): lax.all_to_all(x, axis, split_axis=0, concat_axis=0, tiled=True, axis_ind...  23.7 us
    pallas_call x2, Pallas kernels, pivot_exchange(): pl.pallas_call(functools.partial(inverse_kernel, kb), out_shape=(part, pa...  19.6 us
    all_to_all x3, starting transfers between devices, spread(): lax.all_to_all(x, axis, split_axis=0, concat_axis=0, tiled=True, axis_ind...  17.4 us
    pallas_call x2, Pallas kernels, couplings(): pl.pallas_call(functools.partial(coupling_kernel, pivot), out_shape=out_s...  16.1 us
    ppermute x3, waiting for transfers between devices, on_device(): lax.ppermute(held, 'grp', [(g, g ^ bit) for g in range(grp_size)])  6.9 us
    ppermute x3, starting transfers between devices, on_device(): lax.ppermute(held, 'grp', [(g, g ^ bit) for g in range(grp_size)])  4.55 us
    unnamed x14, local copies, waits for them, and re-layouts  4.32 us
  transfers between devices with their start and end apart: 13, of which 6 were waited for; matrix products, arithmetic and copies ran while one was open for 2% of the time, Pallas kernels for 39%

profile of v3, /device:TPU:0, one launch (start us, length us, event | category | flops | bytes accessed | tf_op | source)
XLA Modules:
  0.0 139.2 jit_solution(3186058491042724963)
XLA Ops:
  0.7 1.0 copy-done.1
  1.7 1.0 copy-done.2
  2.7 0.3 basis.1
  3.1 0.1 collective-permute-start
  3.2 0.7 pad.10.clone
  3.9 0.1 pad_add_fusion
  4.0 0.4 collective-permute-done
  4.4 0.9 broadcast_in_dim.69
  5.3 5.5 %all-to-all-start = ((bf16[8,2,2,64,128]{4,3,2,1,0:T(8,128)(2,1)}), bf16[8,2,2,64,128]{4,3,2,1,0:T(8,128)(2,1)S(1)}, u32[]{:S(2)}, u32[]{:S(2)}) async-start(bf16[8,2,2,64,128]{4,3,2,1,0:T(8,128)(2,1)} %broadcast_in_dim.69), calls=%async_computation | async-start | bytes 1048576 | tf_op jit(solution)/shard_map/all_to_all | solution.py:418
  10.8 0.8 select_reduce_fusion.1
  11.6 0.2 select_reduce_fusion
  11.8 0.1 copy.9
  11.9 0.1 reduce_sum.31
  12.0 8.6 %all-to-all-done = bf16[8,2,2,64,128]{4,3,2,1,0:T(8,128)(2,1)S(1)} async-done(((bf16[8,2,2,64,128]{4,3,2,1,0:T(8,128)(2,1)}), bf16[8,2,2,64,128]{4,3,2,1,0:T(8,128)(2,1)S(1)}, u32[]{:S(2)}, u32[]{:S(2)}) %all-to-all-start) | async-done | bytes 524320 | tf_op jit(solution)/shard_map/all_to_all | solution.py:418
  20.6 1.7 %gather_fusion = bf16[32,2,64,128]{3,2,1,0:T(8,128)(2,1)} fusion(bf16[16,2,64,128]{3,2,1,0:T(8,128)(2,1)S(1)} %bitcast.15, s32[1024]{0:T(1024)S(1)} %pad_clamp_fusion), kind=kCustom, calls=%fused_computation | custom fusion | bytes 2097280 | tf_op jit(solution)/shard_map/gather | solution.py:447
  22.2 7.5 %all-to-all-start.1 = ((bf16[8,4,2,64,128]{4,3,2,1,0:T(8,128)(2,1)}), bf16[8,4,2,64,128]{4,3,2,1,0:T(8,128)(2,1)S(1)}, u32[]{:S(2)}, u32[]{:S(2)}) async-start(bf16[8,4,2,64,128]{4,3,2,1,0:T(8,128)(2,1)} %bitcast.7), calls=%async_computation.1 | async-start | bytes 2097152 | tf_op jit(solution)/shard_map/all_to_all | solution.py:418
  29.7 3.5 %collective-permute-start.2 = (bf16[1,2,128,128]{3,2,1,0:T(8,128)(2,1)S(1)}, bf16[1,2,128,128]{3,2,1,0:T(8,128)(2,1)S(1)}, u32[]{:S(2)}, u32[]{:S(2)}) collective-permute-start(bf16[1,2,128,128]{3,2,1,0:T(8,128)(2,1)S(1)} %get-tuple-element.14.refs_0_), channel_id=1, source_target_pairs={{0,1},{1,0},{2,3},{3,2},{4,5},{5,4},{6,7},{7,6},{8,9},{9,8},{10,11... | collective-permute-start | bytes 196616 | tf_op jit(solution)/shard_map/ppermute | solution.py:433
  33.2 12.9 %all-to-all-done.1.mine_ref = bf16[8,4,2,64,128]{4,3,2,1,0:T(8,128)(2,1)S(1)} async-done(((bf16[8,4,2,64,128]{4,3,2,1,0:T(8,128)(2,1)}), bf16[8,4,2,64,128]{4,3,2,1,0:T(8,128)(2,1)S(1)}, u32[]{:S(2)}, u32[]{:S(2)}) %all-to-all-start.1) | async-done | bytes 1048608 | tf_op jit(solution)/shard_map/all_to_all | solution.py:418
  46.2 0.0 collective-permute-start.1
  46.2 0.1 pad_add_fusion.1.at_ref
  46.2 0.9 copy-done
  47.2 0.7 copy-done.4
  47.8 0.7 copy-done.6
  48.5 7.3 %shard_map.68.refs_0_ = bf16[4,2,1024,1024]{3,2,1,0:T(8,128)(2,1)} custom-call(s32[3]{0:T(128)S(1)} %pad_add_fusion.1.at_ref, s32[16]{0:T(128)S(1)} %copy-done.6, s32[16]{0:T(128)S(1)} %copy-done.4, s32[3,16,1024]{2,1,0:T(8,128)S(1)} %copy-done), custom_call_target="tpu_custom_call" | custom-call | flops 31457280 | bytes 4194304 | tf_op jit(solution)/shard_map/pallas_call | solution.py:127
  55.8 7.4 %shard_map.69.refs_0_ = bf16[4,2,1024,1024]{3,2,1,0:T(8,128)(2,1)} custom-call(s32[3]{0:T(128)S(1)} %pad_add_fusion.1.at_ref, s32[16]{0:T(128)S(1)} %copy-done.6, s32[16]{0:T(128)S(1)} %copy-done.4, s32[3,16,1024]{2,1,0:T(8,128)S(1)} %copy-done, bf16[4,2,1024,1024]{3,2,1,0:T(8,128)(2,1)} %shard_map.68.refs_0_), custom_call_target="tpu_custom_call", output_to_operand_aliasing={{}: (4, {})} | custom-call | flops 31457280 | bytes 4194304 | tf_op jit(solution)/shard_map/pallas_call | solution.py:127
  63.2 13.1 %shard_map.70.g_ref = bf16[4,2,1024,1024]{3,2,1,0:T(8,128)(2,1)} custom-call(s32[3]{0:T(128)S(1)} %pad_add_fusion.1.at_ref, s32[16]{0:T(128)S(1)} %copy-done.6, s32[16]{0:T(128)S(1)} %copy-done.4, s32[3,16,1024]{2,1,0:T(8,128)S(1)} %copy-done, bf16[4,2,1024,1024]{3,2,1,0:T(8,128)(2,1)} %shard_map.69.refs_0_), custom_call_target="tpu_custom_call", output_to_operand_aliasing={{}: (4, {})} | custom-call | flops 62914560 | bytes 8388608 | tf_op jit(solution)/shard_map/pallas_call | solution.py:127
  76.4 0.2 fusion
  76.6 0.1 collective-permute-start.3
  76.7 5.9 %collective-permute-done.3.refs_2_ = bf16[2,2,128,128]{3,2,1,0:T(8,128)(2,1)S(1)} collective-permute-done((bf16[2,2,128,128]{3,2,1,0:T(8,128)(2,1)S(1)}, bf16[2,2,128,128]{3,2,1,0:T(8,128)(2,1)S(1)}, u32[]{:S(2)}, u32[]{:S(2)}) %collective-permute-start.3) | collective-permute-done | bytes 131104 | tf_op jit(solution)/shard_map/ppermute | solution.py:433
  82.6 0.9 collective-permute-start.4
  83.5 7.5 %shard_map.71.refs_4_.first_ref = f32[2,128,256]{2,1,0:T(8,128)S(1)} custom-call(s32[3]{0:T(128)S(1)} %pad_add_fusion.1.at_ref, s32[16]{0:T(128)S(1)} %copy-done.5, bf16[4,2,1024,1024]{3,2,1,0:T(8,128)(2,1)} %shard_map.70.g_ref, bf16[8,4,2,64,128]{4,3,2,1,0:T(8,128)(2,1)S(1)} %all-to-all-done.1.mine_ref, ...), custom_call_target="tpu_custom_call" | custom-call | flops 4294967296 | bytes 8388608 | tf_op jit(solution)/shard_map/pallas_call | solution.py:228
  91.0 1.0 collective-permute-done.4.refs_3_
  92.0 8.6 %shard_map.72 = (f32[2,128,256]{2,1,0:T(8,128)}, bf16[8,2,128,256]{3,2,1,0:T(8,128)(2,1)}, bf16[2,2,128,128]{3,2,1,0:T(8,128)(2,1)S(1)}) custom-call(s32[3]{0:T(128)S(1)} %pad_add_fusion.1.at_ref, s32[16]{0:T(128)S(1)} %copy-done.5, bf16[4,2,1024,1024]{3,2,1,0:T(8,128)(2,1)} %shard_map.70.g_ref, bf16[8,4,2,64,128]{4,3,2,1,0:T(8,128)(2,1)S(1)} %all-to-all-done.1.mine_ref, ...), custom_call_target="tpu_custom_call" | custom-call | flops 4294967296 | bytes 8388608 | tf_op jit(solution)/shard_map/pallas_call | solution.py:228
  100.6 0.2 collective-permute-start.7
  100.8 0.6 fusion.8
  101.4 0.1 pad_add_fusion.2.info
  106.6 4.4 %all-to-all-start.2 = ((bf16[8,2,128,256]{3,2,1,0:T(8,128)(2,1)}), bf16[8,2,128,256]{3,2,1,0:T(8,128)(2,1)S(1)}, u32[]{:S(2)}, u32[]{:S(2)}) async-start(bf16[8,2,128,256]{3,2,1,0:T(8,128)(2,1)} %get-tuple-element.20), calls=%async_computation.2 | async-start | bytes 2097152 | tf_op jit(solution)/shard_map/all_to_all | solution.py:418
  111.1 0.1 broadcast_select_fusion
  111.2 0.7 collective-permute-start.8
  111.9 9.8 %shard_map.73 = (f32[2,256,128]{2,1,0:T(8,128)S(1)}, f32[2,256,128]{2,1,0:T(8,128)S(1)}) custom-call(s32[3]{0:T(128)S(1)} %pad_add_fusion.1.at_ref, f32[2,128,256]{2,1,0:T(8,128)S(1)} %shard_map.71.refs_4_.first_ref, f32[2,128,256]{2,1,0:T(8,128)S(1)} %collective-permute-done.5.second_ref), custom_call_target="tpu_custom_call" | custom-call | flops 6000000000 | bytes 1048576 | tf_op jit(solution)/shard_map/pallas_call | solution.py:352
  121.7 0.0 copy-start.3
  121.7 0.1 broadcast_select_fusion.1
  121.8 2.5 %collective-permute-start.9 = (bf16[2,2,128,128]{3,2,1,0:T(8,128)(2,1)S(1)}, bf16[2,2,128,128]{3,2,1,0:T(8,128)(2,1)S(1)}, u32[]{:S(2)}, u32[]{:S(2)}) collective-permute-start(bf16[2,2,128,128]{3,2,1,0:T(8,128)(2,1)S(1)} %broadcast_select_fusion.1), channel_id=1, source_target_pairs={{0,4},{1,5},{2,6},{3,7},{4,0},{5,1},{6,2},{7,3},{8,12},{9,13},{10,... | collective-permute-start | bytes 393224 | tf_op jit(solution)/shard_map/ppermute | solution.py:459
  124.3 2.2 %all-to-all-done.2 = bf16[8,2,128,256]{3,2,1,0:T(8,128)(2,1)S(1)} async-done(((bf16[8,2,128,256]{3,2,1,0:T(8,128)(2,1)}), bf16[8,2,128,256]{3,2,1,0:T(8,128)(2,1)S(1)}, u32[]{:S(2)}, u32[]{:S(2)}) %all-to-all-start.2) | async-done | bytes 1048608 | tf_op jit(solution)/shard_map/all_to_all | solution.py:418
  126.6 0.3 collective-permute-start.6
  126.9 9.8 %shard_map.74 = (f32[2,256,128]{2,1,0:T(8,128)S(1)}, f32[2,256,128]{2,1,0:T(8,128)S(1)}) custom-call(s32[3]{0:T(128)S(1)} %pad_add_fusion.1.at_ref, f32[2,256,128]{2,1,0:T(8,128)S(1)} %get-tuple-element.16.first_ref, f32[2,256,128]{2,1,0:T(8,128)S(1)} %get-tuple-element.17.second_ref), custom_call_target="tpu_custom_call" | custom-call | flops 6000000000 | bytes 1048576 | tf_op jit(solution)/shard_map/pallas_call | solution.py:352
  136.8 0.1 broadcast_select_fusion.2.c_ref
  136.9 2.3 %schur.1 = f32[2,128,256]{2,1,0:T(8,128)} custom-call(s32[3]{0:T(128)S(1)} %pad_add_fusion.2.info, f32[2,256,128]{2,1,0:T(8,128)S(1)} %get-tuple-element.18.re_ref, f32[2,256,128]{2,1,0:T(8,128)S(1)} %get-tuple-element.19.im_ref, bf16[2,2,128,256]{3,2,1,0:T(8,128)(2,1)S(1)} %pad_maximum_fusion.1.mine_ref, ...), custom_call_target="tpu_custom_call" | custom-call | tf_op jit(solution)/shard_map/schur/pallas_call | solution.py:397
  (27 shorter events, 0.2 us)
Async XLA Ops:
  0.6 1.0 copy-start.1
  1.7 1.0 copy-start.2
  3.1 1.3 collective-permute-start
  5.3 15.3 %all-to-all-start = ((bf16[8,2,2,64,128]{4,3,2,1,0:T(8,128)(2,1)}), bf16[8,2,2,64,128]{4,3,2,1,0:T(8,128)(2,1)S(1)}, u32[]{:S(2)}, u32[]{:S(2)}) async-start(bf16[8,2,2,64,128]{4,3,2,1,0:T(8,128)(2,1)} %broadcast_in_dim.69), calls=%async_computation | async-start | bytes 1048576 | tf_op jit(solution)/shard_map/all_to_all | solution.py:418
  22.2 23.9 %all-to-all-start.1 = ((bf16[8,4,2,64,128]{4,3,2,1,0:T(8,128)(2,1)}), bf16[8,4,2,64,128]{4,3,2,1,0:T(8,128)(2,1)S(1)}, u32[]{:S(2)}, u32[]{:S(2)}) async-start(bf16[8,4,2,64,128]{4,3,2,1,0:T(8,128)(2,1)} %bitcast.7), calls=%async_computation.1 | async-start | bytes 2097152 | tf_op jit(solution)/shard_map/all_to_all | solution.py:418
  29.7 46.8 %collective-permute-start.2 = (bf16[1,2,128,128]{3,2,1,0:T(8,128)(2,1)S(1)}, bf16[1,2,128,128]{3,2,1,0:T(8,128)(2,1)S(1)}, u32[]{:S(2)}, u32[]{:S(2)}) collective-permute-start(bf16[1,2,128,128]{3,2,1,0:T(8,128)(2,1)S(1)} %get-tuple-element.14.refs_0_), channel_id=1, source_target_pairs={{0,1},{1,0},{2,3},{3,2},{4,5},{5,4},{6,7},{7,6},{8,9},{9,8},{10,11... | collective-permute-start | bytes 196616 | tf_op jit(solution)/shard_map/ppermute | solution.py:433
  46.2 37.4 %collective-permute-start.1 = (bf16[8,4,2,64,128]{4,3,2,1,0:T(8,128)(2,1)S(1)}, bf16[8,4,2,64,128]{4,3,2,1,0:T(8,128)(2,1)S(1)}, u32[]{:S(2)}, u32[]{:S(2)}) collective-permute-start(bf16[8,4,2,64,128]{4,3,2,1,0:T(8,128)(2,1)S(1)} %all-to-all-done.1.mine_ref), channel_id=1, source_target_pairs={{0,8},{8,0},{16,24},{24,16},{32,40},{40,32},{48,56},{56,48},{64,72... | collective-permute-start | bytes 3145736 | tf_op jit(solution)/shard_map/ppermute | solution.py:449
  46.2 0.9 copy-start
  47.2 0.7 copy-start.4
  47.8 0.7 copy-start.6
  63.2 13.1 %copy-start.5 = (s32[16]{0:T(128)S(1)}, s32[16]{0:T(128)}, u32[]{:S(2)}) copy-start(s32[16]{0:T(128)} %panel_ref.9) | copy-start | bytes 196
  76.6 6.0 %collective-permute-start.3 = (bf16[2,2,128,128]{3,2,1,0:T(8,128)(2,1)S(1)}, bf16[2,2,128,128]{3,2,1,0:T(8,128)(2,1)S(1)}, u32[]{:S(2)}, u32[]{:S(2)}) collective-permute-start(bf16[2,2,128,128]{3,2,1,0:T(8,128)(2,1)S(1)} %pad_maximum_fusion.2), channel_id=1, source_target_pairs={{0,2},{1,3},{2,0},{3,1},{4,6},{5,7},{6,4},{7,5},{8,10},{9,11},{10,... | collective-permute-start | bytes 393224 | tf_op jit(solution)/shard_map/ppermute | solution.py:433
  82.6 9.4 %collective-permute-start.4 = (bf16[4,2,128,128]{3,2,1,0:T(8,128)(2,1)S(1)}, bf16[4,2,128,128]{3,2,1,0:T(8,128)(2,1)S(1)}, u32[]{:S(2)}, u32[]{:S(2)}) collective-permute-start(bf16[4,2,128,128]{3,2,1,0:T(8,128)(2,1)S(1)} %pad_maximum_fusion), channel_id=1, source_target_pairs={{0,4},{1,5},{2,6},{3,7},{4,0},{5,1},{6,2},{7,3},{8,12},{9,13},{10,... | collective-permute-start | bytes 786440 | tf_op jit(solution)/shard_map/ppermute | solution.py:433
  100.6 10.4 %collective-permute-start.7 = (bf16[2,2,128,128]{3,2,1,0:T(8,128)(2,1)S(1)}, bf16[2,2,128,128]{3,2,1,0:T(8,128)(2,1)S(1)}, u32[]{:S(2)}, u32[]{:S(2)}) collective-permute-start(bf16[2,2,128,128]{3,2,1,0:T(8,128)(2,1)S(1)} %get-tuple-element.21), channel_id=1, source_target_pairs={{0,1},{1,0},{2,3},{3,2},{4,5},{5,4},{6,7},{7,6},{8,9},{9,8},{10,11... | collective-permute-start | bytes 393224 | tf_op jit(solution)/shard_map/ppermute | solution.py:459
  101.4 10.5 %collective-permute-start.5 = (f32[2,128,256]{2,1,0:T(8,128)S(1)}, f32[2,128,256]{2,1,0:T(8,128)S(1)}, u32[]{:S(2)}, u32[]{:S(2)}) collective-permute-start(f32[2,128,256]{2,1,0:T(8,128)S(1)} %shard_map.71.refs_4_.first_ref), channel_id=1, source_target_pairs={{0,8},{8,0},{16,24},{24,16},{32,40},{40,32},{48,56},{56,48},{64,72... | collective-permute-start | bytes 786440 | tf_op jit(solution)/shard_map/ppermute | solution.py:452
  106.6 19.9 %all-to-all-start.2 = ((bf16[8,2,128,256]{3,2,1,0:T(8,128)(2,1)}), bf16[8,2,128,256]{3,2,1,0:T(8,128)(2,1)S(1)}, u32[]{:S(2)}, u32[]{:S(2)}) async-start(bf16[8,2,128,256]{3,2,1,0:T(8,128)(2,1)} %get-tuple-element.20), calls=%async_computation.2 | async-start | bytes 2097152 | tf_op jit(solution)/shard_map/all_to_all | solution.py:418
  111.2 10.5 %collective-permute-start.8 = (bf16[2,2,128,128]{3,2,1,0:T(8,128)(2,1)S(1)}, bf16[2,2,128,128]{3,2,1,0:T(8,128)(2,1)S(1)}, u32[]{:S(2)}, u32[]{:S(2)}) collective-permute-start(bf16[2,2,128,128]{3,2,1,0:T(8,128)(2,1)S(1)} %broadcast_select_fusion), channel_id=1, source_target_pairs={{0,2},{1,3},{2,0},{3,1},{4,6},{5,7},{6,4},{7,5},{8,10},{9,11},{10,... | collective-permute-start | bytes 393224 | tf_op jit(solution)/shard_map/ppermute | solution.py:459
  121.7 15.2 %copy-start.3 = (f32[2,128,256]{2,1,0:T(8,128)S(1)}, f32[2,128,256]{2,1,0:T(8,128)}, u32[]{:S(2)}) copy-start(f32[2,128,256]{2,1,0:T(8,128)} %get-tuple-element.10.r_ref) | copy-start | bytes 786436
  121.8 15.0 %collective-permute-start.9 = (bf16[2,2,128,128]{3,2,1,0:T(8,128)(2,1)S(1)}, bf16[2,2,128,128]{3,2,1,0:T(8,128)(2,1)S(1)}, u32[]{:S(2)}, u32[]{:S(2)}) collective-permute-start(bf16[2,2,128,128]{3,2,1,0:T(8,128)(2,1)S(1)} %broadcast_select_fusion.1), channel_id=1, source_target_pairs={{0,4},{1,5},{2,6},{3,7},{4,0},{5,1},{6,2},{7,3},{8,12},{9,13},{10,... | collective-permute-start | bytes 393224 | tf_op jit(solution)/shard_map/ppermute | solution.py:459
  126.6 10.3 %collective-permute-start.6 = (bf16[2,2,128,256]{3,2,1,0:T(8,128)(2,1)S(1)}, bf16[2,2,128,256]{3,2,1,0:T(8,128)(2,1)S(1)}, u32[]{:S(2)}, u32[]{:S(2)}) collective-permute-start(bf16[2,2,128,256]{3,2,1,0:T(8,128)(2,1)S(1)} %pad_maximum_fusion.1.mine_ref), channel_id=1, source_target_pairs={{0,8},{8,0},{16,24},{24,16},{32,40},{40,32},{48,56},{56,48},{64,72... | collective-permute-start | bytes 786440 | tf_op jit(solution)/shard_map/ppermute | solution.py:465

commit v4 on v3

--- a/solution.py
+++ b/solution.py
@@ -46,33 +46,31 @@
     return inv_r - s * scaled, c * scaled
 
 
-def basis_kernel(core_ref, inv_ref, exc_ref, own_ref, keep_ref, send_ref, both):
+def basis_kernel(inv_ref, exc_ref, own_ref, halves_ref):
     er, ei = exc_ref[0, 0], exc_ref[1, 0]
     j = jnp.dot(inv_ref[0, 0], jnp.concatenate([er, ei], 1), preferred_element_type=f32)
     j += jnp.dot(inv_ref[1, 0], jnp.concatenate([-ei, er], 1), preferred_element_type=f32)
-    rows, cols = j.shape[0], j.shape[1] // 2
-    half = rows // 2
-    both[...] = j.astype(bf16)
-    mine = pl.multiple_of(core_ref[0] * half, half)
-    other = pl.multiple_of((1 - core_ref[0]) * half, half)
+    cols, half = j.shape[1] // 2, j.shape[0] // 2
+    jb = j.astype(bf16)
     for part in range(2):
-        own_ref[0, part] = both[:, part * cols : (part + 1) * cols]
-        keep_ref[part] = both[pl.ds(mine, half), part * cols : (part + 1) * cols]
-        send_ref[part] = both[pl.ds(other, half), part * cols : (part + 1) * cols]
-
-
-def basis_rows(core, inverse, excite):
+        own_ref[0, part] = jb[:, part * cols : (part + 1) * cols]
+        for k in range(halves_ref.shape[0]):
+            halves_ref[k, part] = jb[(k % 2) * half : (k % 2 + 1) * half, part * cols : (part + 1) * cols]
+
+
+def basis_rows(inverse, excite, devices):
     rows, cols = inverse.shape[2], excite.shape[3]
-    half = jax.ShapeDtypeStruct((2, rows // 2, cols), bf16)
     return pl.pallas_call(
         basis_kernel,
-        out_shape=(jax.ShapeDtypeStruct((1, 2, rows, cols), bf16), half, half),
-        in_specs=[SMEM, VMEM, VMEM],
-        out_specs=(VMEM, VMEM, VMEM),
-        scratch_shapes=[pltpu.VMEM((rows, 2 * cols), bf16)],
+        out_shape=(
+            jax.ShapeDtypeStruct((1, 2, rows, cols), bf16),
+            jax.ShapeDtypeStruct((devices, 2, rows // 2, cols), bf16),
+        ),
+        in_specs=[VMEM, VMEM],
+        out_specs=(VMEM, VMEM),
         compiler_params=pltpu.CompilerParams(vmem_limit_bytes=8 * MB),
         name="basis",
-    )(core, inverse, excite)
+    )(inverse, excite)
 
 
 def features(coords_ref, block, left):
@@ -85,14 +83,15 @@
     return jnp.concatenate([v.astype(f32) for v in rows + [zero]], 0).astype(bf16)
 
 
-def green_kernel(first, at_ref, blocks_ref, panel_ref, coords_ref, *refs):
+def green_kernel(tiles, at_ref, coords_ref, *refs):
     g_ref, fl_ref, fr_ref, sq_ref = refs[-4:]
     rows, _ = sq_ref.shape
-    tile, chunk = pl.program_id(0) + first, pl.program_id(1)
-    own, grp, core = blocks_ref[at_ref[0]], at_ref[1], at_ref[2]
+    tile, chunk = pl.program_id(0) + tiles, pl.program_id(1)
+    blocks = coords_ref.shape[1]
+    own, grp, core = at_ref[3 + at_ref[0]], at_ref[1], at_ref[2]
     main = tile < 2
-    left = jnp.where(main, own, panel_ref[core])
-    right = jnp.where(main, grp * 2 + tile, panel_ref[jnp.maximum(tile - 2, 0)])
+    left = jnp.where(main, own, at_ref[3 + blocks + core])
+    right = jnp.where(main, grp * 2 + tile, at_ref[3 + blocks + jnp.maximum(tile - 2, 0)])
 
     @pl.when(chunk == 0)
     def _():
@@ -121,26 +120,26 @@
             g_ref[0, part, :, at] = jnp.where(same, value, block).astype(bf16)
 
 
-def green_tiles(at, blocks, panel, coordinates, first, count, tiles, held):
+def green_tiles(at, coordinates, first, count, tiles, held):
     unk = coordinates.shape[2]
     rows = GREEN_ROWS
     return pl.pallas_call(
         functools.partial(green_kernel, first),
         out_shape=pltpu.HBM((tiles, 2, unk, unk), bf16),
         grid=(count, unk // rows),
-        in_specs=[SMEM, SMEM, SMEM, pl.BlockSpec(coordinates.shape, lambda t, m: (0, 0, 0))]
+        in_specs=[SMEM, pl.BlockSpec(coordinates.shape, lambda t, m: (0, 0, 0))]
         + [pl.BlockSpec(memory_space=pltpu.HBM)] * len(held),
         out_specs=pl.BlockSpec((1, 2, rows, unk), lambda t, m: (t + first, 0, m, 0)),
         scratch_shapes=[pltpu.VMEM((8, unk), bf16), pltpu.VMEM((8, unk), bf16), pltpu.VMEM((rows, unk), f32)],
-        input_output_aliases={4: 0} if held else {},
+        input_output_aliases={2: 0} if held else {},
         compiler_params=pltpu.CompilerParams(vmem_limit_bytes=10 * MB),
         cost_estimate=pl.CostEstimate(
             flops=count * unk * unk * 30, transcendentals=count * unk * unk, bytes_accessed=count * unk * unk * 4
         ),
-    )(at, blocks, panel, coordinates, *held)
-
-
-def coupling_kernel(pivot, at_ref, panel_ref, g_ref, mine_ref, other_ref, *refs):
+    )(at, pltpu.with_memory_space_constraint(coordinates, pltpu.HBM), *held)
+
+
+def coupling_kernel(pivot, panel_at, at_ref, g_ref, mine_ref, other_ref, *refs):
     if pivot:
         out_ref, lhs, stage, top, bottom, acc = refs
     else:
@@ -203,14 +202,14 @@
                 for k in range(copies_ref.shape[0]):
                     copies_ref[k, part] = value.astype(bf16)
                 for p in range(PANELS):
-                    here = panel_ref[p] == grp * 2 + tile
+                    here = at_ref[panel_at + p] == grp * 2 + tile
 
                     @pl.when(here | (tile == 0))
                     def _():
                         column_ref[p, part] = value.astype(bf16)
 
 
-def couplings(at, panel, green, mine, other, pieces, after, pivot):
+def couplings(at, blocks, green, mine, other, pieces, after, pivot):
     _, _, unk, _ = green.shape
     cols = mine.shape[4]
     tiles = 2
@@ -226,10 +225,10 @@
         out_shape.append(jax.ShapeDtypeStruct((PANELS, 2, cols, cols), bf16))
         out_specs.append(pl.BlockSpec((PANELS, 2, cols, cols), lambda t, m: (0, 0, 0, 0)))
     return pl.pallas_call(
-        functools.partial(coupling_kernel, pivot),
+        functools.partial(coupling_kernel, pivot, 3 + blocks),
         out_shape=out_shape,
         grid=(tiles, unk // rows),
-        in_specs=[SMEM, SMEM, pl.BlockSpec((1, 2, rows, unk), lambda t, m: (t + first, 0, m, 0))]
+        in_specs=[SMEM, pl.BlockSpec((1, 2, rows, unk), lambda t, m: (t + first, 0, m, 0))]
         + [whole(x) for x in (mine, other, *pieces)]
         + [pl.BlockSpec(memory_space=pl.ANY)] * len(after),
         out_specs=out_specs,
@@ -244,7 +243,7 @@
         cost_estimate=pl.CostEstimate(
             flops=tiles * unk * unk * 2048, transcendentals=0, bytes_accessed=tiles * unk * unk * 4
         ),
-    )(at, panel, pltpu.with_memory_space_constraint(green, pltpu.HBM), mine, other, *pieces, *after)
+    )(at, pltpu.with_memory_space_constraint(green, pltpu.HBM), mine, other, *pieces, *after)
 
 
 WIDE = 128
@@ -412,7 +411,7 @@
     slabs = blocks // grp_size
     swap = [(i, i ^ 1) for i in range(blk_size)]
     same_core = [list(range(c, blk_size, 2)) for c in range(2)]
-    at = jnp.stack([slot, grp, core])
+    at = jnp.concatenate([jnp.stack([slot, grp, core]), block_of_slot, panel_order])
 
     def spread(x, axis, groups=None):
         return lax.all_to_all(x, axis, split_axis=0, concat_axis=0, tiled=True, axis_index_groups=groups)
@@ -421,12 +420,8 @@
     slot_of = jnp.sum(jnp.where(block_of_slot[None, :] == order[:, None], order[None, :], 0), axis=1)
     pivots = panel_order[:PANELS]
 
-    own, keep, send = basis_rows(core.reshape(1), inverse, excite)
-    got = lax.ppermute(send, "blk", swap)
-    pair = jnp.stack([keep, got])
-    pair = jnp.broadcast_to(pair[None], (blk_size // 2, *pair.shape))
-    sliced = spread(pair, "blk", same_core)
-    sliced = sliced.reshape(blk_size, *keep.shape)
+    own, halves = basis_rows(inverse, excite, blk_size)
+    sliced = spread(halves, "blk")
 
     pieces, held, bit = [own], own, 1
     while bit < grp_size:
@@ -435,22 +430,23 @@
         if bit < grp_size:
             held = jnp.concatenate([held, pieces[-1]], 0)
 
-    green = green_tiles(at, block_of_slot, panel_order, coordinates, 0, 1, 2 + PANELS, [])
-    green = green_tiles(at, block_of_slot, panel_order, coordinates, 1, 1, 2 + PANELS, [green])
-    green = green_tiles(at, block_of_slot, panel_order, coordinates, 2, PANELS, 2 + PANELS, [green])
+    tiles = slabs + PANELS
+    green = green_tiles(at, coordinates, 0, 1, tiles, [])
+    green = green_tiles(at, coordinates, 2, PANELS, tiles, [green])
+    green = green_tiles(at, coordinates, 1, 1, tiles, [green])
 
     wanted = jnp.concatenate(
         [order.reshape(grp_size, slabs), jnp.broadcast_to(pivots[None], (grp_size, PANELS))], axis=1
     )
     from_slot = jnp.sum(jnp.where(wanted[:, :, None] == order, slot_of, 0), axis=2)
-    place = (from_slot // 2) * 2 + (from_slot % 2 + core) % 2
-    picked = sliced.at[place.reshape(-1)].get(mode="promise_in_bounds").reshape(*place.shape, *keep.shape)
+    picked = sliced.at[from_slot.reshape(-1)].get(mode="promise_in_bounds")
+    picked = picked.reshape(*from_slot.shape, *sliced.shape[1:])
     mine = spread(picked, "grp")
     other = lax.ppermute(mine, "blk", swap)
 
-    (pivot_rows,) = couplings(at, panel_order, green, mine, other, [], [], True)
+    (pivot_rows,) = couplings(at, blocks, green, mine, other, [], [], True)
     pivot_other = lax.ppermute(pivot_rows, "blk", swap)
-    reduced, copies, column = couplings(at, panel_order, green, mine, other, pieces, [pivot_rows], False)
+    reduced, copies, column = couplings(at, blocks, green, mine, other, pieces, [pivot_rows], False)
 
     rows = spread(copies, "blk", same_core)
     column_at = pivots // slabs

time: 142 us -> 142 us (level)
  blocking collectives: 0 us -> 23.9 us
  waiting for transfers between devices: 31 us -> 17.1 us
  starting transfers between devices: 25.8 us -> 17.8 us
  local copies, waits for them, and re-layouts: 8.46 us -> 5.1 us
  Pallas kernels: 66.2 us -> 68.2 us
    all_to_all x0 -> x1, blocking collectives: none -> 23.9 us  [spread(): lax.all_to_all(x, axis, split_axis=0, concat_axis=0, tiled=True, axis_ind...]
    all_to_all x3 -> x2, waiting for transfers between devices: 23.7 us -> 11.3 us  [spread(): lax.all_to_all(x, axis, split_axis=0, concat_axis=0, tiled=True, axis_ind...]
    all_to_all x3 -> x2, starting transfers between devices: 17.4 us -> 9.18 us  [spread(): lax.all_to_all(x, axis, split_axis=0, concat_axis=0, tiled=True, axis_ind...]
    ppermute x3, starting transfers between devices: 3.39 us -> 5.87 us  [on_device(): came = lax.ppermute(column, 'grp', [(g, g ^ bit) for g in range(grp_size)])]
    unnamed x14 -> x8, local copies, waits for them, and re-layouts: 4.32 us -> 2.09 us
    ppermute x3, starting transfers between devices: 4.55 us -> 2.48 us  [on_device(): lax.ppermute(held, 'grp', [(g, g ^ bit) for g in range(grp_size)])]
  transfers between devices with their start and end apart: 13 -> 11, of which waited for: 6 -> 4; matrix products, arithmetic and copies ran while one was open for 2% -> 3% of each run, Pallas kernels for 39% -> 40%
where the time goes in v4:
time: 142 us; the launch traced here: 140 us
  Pallas kernels  68.2 us (48%)
  blocking collectives  23.9 us (17%)
  starting transfers between devices  17.8 us (13%)
  waiting for transfers between devices  17.1 us (12%)
  between operations  5.99 us (4%)
  local copies, waits for them, and re-layouts  5.1 us (4%)
  other arithmetic  1.69 us (1%)
    pallas_call x3, Pallas kernels, green_tiles(): pl.pallas_call(functools.partial(green_kernel, first), out_shape=pltpu.HB...  29 us
    all_to_all x1, blocking collectives, spread(): lax.all_to_all(x, axis, split_axis=0, concat_axis=0, tiled=True, axis_ind...  23.9 us
    pallas_call x2, Pallas kernels, pivot_exchange(): pl.pallas_call(functools.partial(inverse_kernel, kb), out_shape=(part, pa...  19.6 us
    pallas_call x2, Pallas kernels, couplings(): pl.pallas_call(functools.partial(coupling_kernel, pivot, 3 + blocks), out...  16 us
    all_to_all x2, waiting for transfers between devices, spread(): lax.all_to_all(x, axis, split_axis=0, concat_axis=0, tiled=True, axis_ind...  11.3 us
    all_to_all x2, starting transfers between devices, spread(): lax.all_to_all(x, axis, split_axis=0, concat_axis=0, tiled=True, axis_ind...  9.18 us
    ppermute x3, starting transfers between devices, on_device(): came = lax.ppermute(column, 'grp', [(g, g ^ bit) for g in range(grp_size)])  5.87 us
    ppermute x3, waiting for transfers between devices, on_device(): lax.ppermute(held, 'grp', [(g, g ^ bit) for g in range(grp_size)])  5.77 us
  transfers between devices with their start and end apart: 11, of which 4 were waited for; matrix products, arithmetic and copies ran while one was open for 3% of the time, Pallas kernels for 40%

profile of v4, /device:TPU:0, one launch (start us, length us, event | category | flops | bytes accessed | tf_op | source)
XLA Modules:
  0.0 139.7 jit_solution(4830244472433165168)
XLA Ops:
  0.6 1.0 copy-done
  1.7 1.0 copy-done.1
  2.7 1.1 basis.1
  3.8 5.6 %all-to-all-start = ((bf16[16,2,64,128]{3,2,1,0:T(8,128)(2,1)}), bf16[16,2,64,128]{3,2,1,0:T(8,128)(2,1)S(1)}, u32[]{:S(2)}, u32[]{:S(2)}) async-start(bf16[16,2,64,128]{3,2,1,0:T(8,128)(2,1)} %get-tuple-element.11), calls=%async_computation | async-start | bytes 1048576 | tf_op jit(solution)/shard_map/all_to_all | solution.py:417
  9.5 0.7 pad.10.clone
  10.2 0.1 pad_add_fusion
  10.3 0.8 select_reduce_fusion.1
  11.1 0.2 select_reduce_fusion
  11.3 0.1 copy.9
  11.4 0.1 reshape.56
  11.5 8.8 %all-to-all-done = bf16[16,2,64,128]{3,2,1,0:T(8,128)(2,1)S(1)} async-done(((bf16[16,2,64,128]{3,2,1,0:T(8,128)(2,1)}), bf16[16,2,64,128]{3,2,1,0:T(8,128)(2,1)S(1)}, u32[]{:S(2)}, u32[]{:S(2)}) %all-to-all-start) | async-done | bytes 524320 | tf_op jit(solution)/shard_map/all_to_all | solution.py:417
  20.3 0.7 gather_fusion
  21.1 23.9 %all_to_all.15.mine_ref = bf16[8,4,2,64,128]{4,3,2,1,0:T(8,128)(2,1)S(1)} all-to-all(bf16[8,4,2,64,128]{4,3,2,1,0:T(8,128)(2,1)S(1)} %bitcast.9), channel_id=1, replica_groups=mesh['blk'=16,'grp'=8] {'grp'}, dimensions={0} | all-to-all | bytes 2097152 | tf_op jit(solution)/shard_map/all_to_all | solution.py:417
  44.9 0.0 collective-permute-start
  44.9 0.9 collective-permute-start.1
  45.8 0.7 concatenate.16.at_ref
  46.6 7.8 %shard_map.68.refs_0_ = bf16[4,2,1024,1024]{3,2,1,0:T(8,128)(2,1)} custom-call(s32[35]{0:T(128)S(1)} %concatenate.16.at_ref, s32[3,16,1024]{2,1,0:T(8,128)} %coords_ref.5), custom_call_target="tpu_custom_call" | custom-call | flops 31457280 | bytes 4194304 | tf_op jit(solution)/shard_map/pallas_call | solution.py:126
  54.3 13.5 %shard_map.69.refs_0_ = bf16[4,2,1024,1024]{3,2,1,0:T(8,128)(2,1)} custom-call(s32[35]{0:T(128)S(1)} %concatenate.16.at_ref, s32[3,16,1024]{2,1,0:T(8,128)} %coords_ref.5, bf16[4,2,1024,1024]{3,2,1,0:T(8,128)(2,1)} %shard_map.68.refs_0_), custom_call_target="tpu_custom_call", output_to_operand_aliasing={{}: (2, {})} | custom-call | flops 62914560 | bytes 8388608 | tf_op jit(solution)/shard_map/pallas_call | solution.py:126
  67.8 7.8 %shard_map.70.g_ref = bf16[4,2,1024,1024]{3,2,1,0:T(8,128)(2,1)} custom-call(s32[35]{0:T(128)S(1)} %concatenate.16.at_ref, s32[3,16,1024]{2,1,0:T(8,128)} %coords_ref.5, bf16[4,2,1024,1024]{3,2,1,0:T(8,128)(2,1)} %shard_map.69.refs_0_), custom_call_target="tpu_custom_call", output_to_operand_aliasing={{}: (2, {})} | custom-call | flops 31457280 | bytes 4194304 | tf_op jit(solution)/shard_map/pallas_call | solution.py:126
  75.6 0.2 fusion
  75.8 0.0 collective-permute-done.1.refs_1_
  75.8 0.6 collective-permute-start.2
  76.5 5.1 %collective-permute-done.2.refs_2_ = bf16[2,2,128,128]{3,2,1,0:T(8,128)(2,1)S(1)} collective-permute-done((bf16[2,2,128,128]{3,2,1,0:T(8,128)(2,1)S(1)}, bf16[2,2,128,128]{3,2,1,0:T(8,128)(2,1)S(1)}, u32[]{:S(2)}, u32[]{:S(2)}) %collective-permute-start.2) | collective-permute-done | bytes 131104 | tf_op jit(solution)/shard_map/ppermute | solution.py:428
  81.6 1.0 collective-permute-start.3
  82.5 0.0 collective-permute-done.other_ref
  82.5 7.5 %shard_map.71.refs_4_.first_ref = f32[2,128,256]{2,1,0:T(8,128)S(1)} custom-call(s32[35]{0:T(128)S(1)} %concatenate.16.at_ref, bf16[4,2,1024,1024]{3,2,1,0:T(8,128)(2,1)} %shard_map.70.g_ref, bf16[8,4,2,64,128]{4,3,2,1,0:T(8,128)(2,1)S(1)} %all_to_all.15.mine_ref, bf16[8,4,2,64,128]{4,3,2,1,0:T(8,128)(2,1)S(1)} %collective-permute-done.other_ref), custom_call_target="tpu_custom_call" | custom-call | flops 4294967296 | bytes 8388608 | tf_op jit(solution)/shard_map/pallas_call | solution.py:227
  90.0 0.7 collective-permute-done.3.refs_3_
  90.7 8.6 %shard_map.72 = (f32[2,128,256]{2,1,0:T(8,128)}, bf16[8,2,128,256]{3,2,1,0:T(8,128)(2,1)}, bf16[2,2,128,128]{3,2,1,0:T(8,128)(2,1)S(1)}) custom-call(s32[35]{0:T(128)S(1)} %concatenate.16.at_ref, bf16[4,2,1024,1024]{3,2,1,0:T(8,128)(2,1)} %shard_map.70.g_ref, bf16[8,4,2,64,128]{4,3,2,1,0:T(8,128)(2,1)S(1)} %all_to_all.15.mine_ref, ...), custom_call_target="tpu_custom_call" | custom-call | flops 4294967296 | bytes 8388608 | tf_op jit(solution)/shard_map/pallas_call | solution.py:227
  99.3 2.7 %collective-permute-start.6 = (bf16[2,2,128,128]{3,2,1,0:T(8,128)(2,1)S(1)}, bf16[2,2,128,128]{3,2,1,0:T(8,128)(2,1)S(1)}, u32[]{:S(2)}, u32[]{:S(2)}) collective-permute-start(bf16[2,2,128,128]{3,2,1,0:T(8,128)(2,1)S(1)} %get-tuple-element.19), channel_id=1, source_target_pairs={{0,1},{1,0},{2,3},{3,2},{4,5},{5,4},{6,7},{7,6},{8,9},{9,8},{10,11... | collective-permute-start | bytes 393224 | tf_op jit(solution)/shard_map/ppermute | solution.py:455
  102.0 0.6 fusion.5
  102.6 0.0 collective-permute-start.4
  102.6 0.1 pad_add_fusion.1.info
  107.8 3.6 %all-to-all-start.2 = ((bf16[8,2,128,256]{3,2,1,0:T(8,128)(2,1)}), bf16[8,2,128,256]{3,2,1,0:T(8,128)(2,1)S(1)}, u32[]{:S(2)}, u32[]{:S(2)}) async-start(bf16[8,2,128,256]{3,2,1,0:T(8,128)(2,1)} %get-tuple-element.18), calls=%async_computation.2 | async-start | bytes 2097152 | tf_op jit(solution)/shard_map/all_to_all | solution.py:417
  111.4 0.0 collective-permute-done.6
  111.4 0.1 broadcast_select_fusion
  111.5 0.6 collective-permute-start.7
  112.2 0.0 collective-permute-done.4.second_ref
  112.2 9.8 %shard_map.73 = (f32[2,256,128]{2,1,0:T(8,128)S(1)}, f32[2,256,128]{2,1,0:T(8,128)S(1)}) custom-call(s32[35]{0:T(128)S(1)} %concatenate.16.at_ref, f32[2,128,256]{2,1,0:T(8,128)S(1)} %shard_map.71.refs_4_.first_ref, f32[2,128,256]{2,1,0:T(8,128)S(1)} %collective-permute-done.4.second_ref), custom_call_target="tpu_custom_call" | custom-call | flops 6000000000 | bytes 1048576 | tf_op jit(solution)/shard_map/pallas_call | solution.py:351
  121.9 0.0 copy-start.2
  122.0 0.0 collective-permute-done.7
  122.0 0.1 broadcast_select_fusion.1
  122.1 2.6 %collective-permute-start.8 = (bf16[2,2,128,128]{3,2,1,0:T(8,128)(2,1)S(1)}, bf16[2,2,128,128]{3,2,1,0:T(8,128)(2,1)S(1)}, u32[]{:S(2)}, u32[]{:S(2)}) collective-permute-start(bf16[2,2,128,128]{3,2,1,0:T(8,128)(2,1)S(1)} %broadcast_select_fusion.1), channel_id=1, source_target_pairs={{0,4},{1,5},{2,6},{3,7},{4,0},{5,1},{6,2},{7,3},{8,12},{9,13},{10,... | collective-permute-start | bytes 393224 | tf_op jit(solution)/shard_map/ppermute | solution.py:455
  124.6 2.5 %all-to-all-done.2 = bf16[8,2,128,256]{3,2,1,0:T(8,128)(2,1)S(1)} async-done(((bf16[8,2,128,256]{3,2,1,0:T(8,128)(2,1)}), bf16[8,2,128,256]{3,2,1,0:T(8,128)(2,1)S(1)}, u32[]{:S(2)}, u32[]{:S(2)}) %all-to-all-start.2) | async-done | bytes 1048608 | tf_op jit(solution)/shard_map/all_to_all | solution.py:417
  127.1 0.3 collective-permute-start.5
  127.4 9.9 %shard_map.74 = (f32[2,256,128]{2,1,0:T(8,128)S(1)}, f32[2,256,128]{2,1,0:T(8,128)S(1)}) custom-call(s32[35]{0:T(128)S(1)} %concatenate.16.at_ref, f32[2,256,128]{2,1,0:T(8,128)S(1)} %get-tuple-element.14.first_ref, f32[2,256,128]{2,1,0:T(8,128)S(1)} %get-tuple-element.15.second_ref), custom_call_target="tpu_custom_call" | custom-call | flops 6000000000 | bytes 1048576 | tf_op jit(solution)/shard_map/pallas_call | solution.py:351
  137.3 0.0 collective-permute-done.8
  137.3 0.1 broadcast_select_fusion.2.c_ref
  137.4 2.3 %schur.1 = f32[2,128,256]{2,1,0:T(8,128)} custom-call(s32[3]{0:T(128)S(1)} %pad_add_fusion.1.info, f32[2,256,128]{2,1,0:T(8,128)S(1)} %get-tuple-element.16.re_ref, f32[2,256,128]{2,1,0:T(8,128)S(1)} %get-tuple-element.17.im_ref, bf16[2,2,128,256]{3,2,1,0:T(8,128)(2,1)S(1)} %pad_maximum_fusion.1.mine_ref, ...), custom_call_target="tpu_custom_call" | custom-call | tf_op jit(solution)/shard_map/schur/pallas_call | solution.py:396
  (16 shorter events, 0.1 us)
Async XLA Ops:
  0.6 1.0 copy-start
  1.7 1.0 copy-start.1
  3.8 16.4 %all-to-all-start = ((bf16[16,2,64,128]{3,2,1,0:T(8,128)(2,1)}), bf16[16,2,64,128]{3,2,1,0:T(8,128)(2,1)S(1)}, u32[]{:S(2)}, u32[]{:S(2)}) async-start(bf16[16,2,64,128]{3,2,1,0:T(8,128)(2,1)} %get-tuple-element.11), calls=%async_computation | async-start | bytes 1048576 | tf_op jit(solution)/shard_map/all_to_all | solution.py:417
  44.9 37.6 %collective-permute-start = (bf16[8,4,2,64,128]{4,3,2,1,0:T(8,128)(2,1)S(1)}, bf16[8,4,2,64,128]{4,3,2,1,0:T(8,128)(2,1)S(1)}, u32[]{:S(2)}, u32[]{:S(2)}) collective-permute-start(bf16[8,4,2,64,128]{4,3,2,1,0:T(8,128)(2,1)S(1)} %all_to_all.15.mine_ref), channel_id=1, source_target_pairs={{0,8},{8,0},{16,24},{24,16},{32,40},{40,32},{48,56},{56,48},{64,72... | collective-permute-start | bytes 3145736 | tf_op jit(solution)/shard_map/ppermute | solution.py:445
  44.9 30.9 %collective-permute-start.1 = (bf16[1,2,128,128]{3,2,1,0:T(8,128)(2,1)S(1)}, bf16[1,2,128,128]{3,2,1,0:T(8,128)(2,1)S(1)}, u32[]{:S(2)}, u32[]{:S(2)}) collective-permute-start(bf16[1,2,128,128]{3,2,1,0:T(8,128)(2,1)S(1)} %get-tuple-element.12.refs_0_), channel_id=1, source_target_pairs={{0,1},{1,0},{2,3},{3,2},{4,5},{5,4},{6,7},{7,6},{8,9},{9,8},{10,11... | collective-permute-start | bytes 196616 | tf_op jit(solution)/shard_map/ppermute | solution.py:428
  67.8 7.8 %copy-start.3 = (s32[16]{0:T(128)S(1)}, s32[16]{0:T(128)}, u32[]{:S(2)}) copy-start(s32[16]{0:T(128)} %param.9) | copy-start | bytes 196
  75.8 5.7 %collective-permute-start.2 = (bf16[2,2,128,128]{3,2,1,0:T(8,128)(2,1)S(1)}, bf16[2,2,128,128]{3,2,1,0:T(8,128)(2,1)S(1)}, u32[]{:S(2)}, u32[]{:S(2)}) collective-permute-start(bf16[2,2,128,128]{3,2,1,0:T(8,128)(2,1)S(1)} %pad_maximum_fusion.2), channel_id=1, source_target_pairs={{0,2},{1,3},{2,0},{3,1},{4,6},{5,7},{6,4},{7,5},{8,10},{9,11},{10,... | collective-permute-start | bytes 393224 | tf_op jit(solution)/shard_map/ppermute | solution.py:428
  81.6 9.2 %collective-permute-start.3 = (bf16[4,2,128,128]{3,2,1,0:T(8,128)(2,1)S(1)}, bf16[4,2,128,128]{3,2,1,0:T(8,128)(2,1)S(1)}, u32[]{:S(2)}, u32[]{:S(2)}) collective-permute-start(bf16[4,2,128,128]{3,2,1,0:T(8,128)(2,1)S(1)} %pad_maximum_fusion), channel_id=1, source_target_pairs={{0,4},{1,5},{2,6},{3,7},{4,0},{5,1},{6,2},{7,3},{8,12},{9,13},{10,... | collective-permute-start | bytes 786440 | tf_op jit(solution)/shard_map/ppermute | solution.py:428
  99.3 12.1 %collective-permute-start.6 = (bf16[2,2,128,128]{3,2,1,0:T(8,128)(2,1)S(1)}, bf16[2,2,128,128]{3,2,1,0:T(8,128)(2,1)S(1)}, u32[]{:S(2)}, u32[]{:S(2)}) collective-permute-start(bf16[2,2,128,128]{3,2,1,0:T(8,128)(2,1)S(1)} %get-tuple-element.19), channel_id=1, source_target_pairs={{0,1},{1,0},{2,3},{3,2},{4,5},{5,4},{6,7},{7,6},{8,9},{9,8},{10,11... | collective-permute-start | bytes 393224 | tf_op jit(solution)/shard_map/ppermute | solution.py:455
  102.6 9.6 %collective-permute-start.4 = (f32[2,128,256]{2,1,0:T(8,128)S(1)}, f32[2,128,256]{2,1,0:T(8,128)S(1)}, u32[]{:S(2)}, u32[]{:S(2)}) collective-permute-start(f32[2,128,256]{2,1,0:T(8,128)S(1)} %shard_map.71.refs_4_.first_ref), channel_id=1, source_target_pairs={{0,8},{8,0},{16,24},{24,16},{32,40},{40,32},{48,56},{56,48},{64,72... | collective-permute-start | bytes 786440 | tf_op jit(solution)/shard_map/ppermute | solution.py:448
  107.8 19.2 %all-to-all-start.2 = ((bf16[8,2,128,256]{3,2,1,0:T(8,128)(2,1)}), bf16[8,2,128,256]{3,2,1,0:T(8,128)(2,1)S(1)}, u32[]{:S(2)}, u32[]{:S(2)}) async-start(bf16[8,2,128,256]{3,2,1,0:T(8,128)(2,1)} %get-tuple-element.18), calls=%async_computation.2 | async-start | bytes 2097152 | tf_op jit(solution)/shard_map/all_to_all | solution.py:417
  111.5 10.4 %collective-permute-start.7 = (bf16[2,2,128,128]{3,2,1,0:T(8,128)(2,1)S(1)}, bf16[2,2,128,128]{3,2,1,0:T(8,128)(2,1)S(1)}, u32[]{:S(2)}, u32[]{:S(2)}) collective-permute-start(bf16[2,2,128,128]{3,2,1,0:T(8,128)(2,1)S(1)} %broadcast_select_fusion), channel_id=1, source_target_pairs={{0,2},{1,3},{2,0},{3,1},{4,6},{5,7},{6,4},{7,5},{8,10},{9,11},{10,... | collective-permute-start | bytes 393224 | tf_op jit(solution)/shard_map/ppermute | solution.py:455
  121.9 15.5 %copy-start.2 = (f32[2,128,256]{2,1,0:T(8,128)S(1)}, f32[2,128,256]{2,1,0:T(8,128)}, u32[]{:S(2)}) copy-start(f32[2,128,256]{2,1,0:T(8,128)} %get-tuple-element.9.r_ref) | copy-start | bytes 786436
  122.1 15.3 %collective-permute-start.8 = (bf16[2,2,128,128]{3,2,1,0:T(8,128)(2,1)S(1)}, bf16[2,2,128,128]{3,2,1,0:T(8,128)(2,1)S(1)}, u32[]{:S(2)}, u32[]{:S(2)}) collective-permute-start(bf16[2,2,128,128]{3,2,1,0:T(8,128)(2,1)S(1)} %broadcast_select_fusion.1), channel_id=1, source_target_pairs={{0,4},{1,5},{2,6},{3,7},{4,0},{5,1},{6,2},{7,3},{8,12},{9,13},{10,... | collective-permute-start | bytes 393224 | tf_op jit(solution)/shard_map/ppermute | solution.py:455
  127.1 10.3 %collective-permute-start.5 = (bf16[2,2,128,256]{3,2,1,0:T(8,128)(2,1)S(1)}, bf16[2,2,128,256]{3,2,1,0:T(8,128)(2,1)S(1)}, u32[]{:S(2)}, u32[]{:S(2)}) collective-permute-start(bf16[2,2,128,256]{3,2,1,0:T(8,128)(2,1)S(1)} %pad_maximum_fusion.1.mine_ref), channel_id=1, source_target_pairs={{0,8},{8,0},{16,24},{24,16},{32,40},{40,32},{48,56},{56,48},{64,72... | collective-permute-start | bytes 786440 | tf_op jit(solution)/shard_map/ppermute | solution.py:461

commit v5 on v4

--- a/solution.py
+++ b/solution.py
@@ -71,6 +71,60 @@
         compiler_params=pltpu.CompilerParams(vmem_limit_bytes=8 * MB),
         name="basis",
     )(inverse, excite)
+
+
+def slot_with(at, block, blocks):
+    slot = 0
+    for s in range(blocks):
+        slot = slot + jnp.where(at[3 + s] == block, s, 0)
+    return slot
+
+
+def gather_kernel(at_ref, rows_ref, out_ref, slot_ref):
+    blocks = rows_ref.shape[0]
+    for s in range(blocks):
+        slot_ref[at_ref[3 + s]] = s
+    groups, entries = out_ref.shape[:2]
+    slabs = entries - PANELS
+    for p in range(PANELS):
+        value = rows_ref[slot_ref[at_ref[3 + blocks + p]]]
+        for g in range(groups):
+            out_ref[g, slabs + p] = value
+    for g in range(groups):
+        for e in range(slabs):
+            out_ref[g, e] = rows_ref[slot_ref[g * slabs + e]]
+
+
+def gathered(at, rows, groups, slabs):
+    return pl.pallas_call(
+        gather_kernel,
+        out_shape=jax.ShapeDtypeStruct((groups, slabs + PANELS, *rows.shape[1:]), rows.dtype),
+        in_specs=[SMEM, VMEM],
+        out_specs=VMEM,
+        scratch_shapes=[pltpu.SMEM((rows.shape[0],), i32)],
+        compiler_params=pltpu.CompilerParams(vmem_limit_bytes=8 * MB),
+        name="gathered",
+    )(at, rows)
+
+
+def pick_kernel(at_ref, row_ref, out_ref):
+    out_ref[...] = row_ref[...]
+
+
+def pivot_tiles(at, rows, blocks):
+    shape = (1, *rows.shape[1:])
+    return pl.pallas_call(
+        pick_kernel,
+        out_shape=jax.ShapeDtypeStruct((PANELS, *rows.shape[1:]), rows.dtype),
+        grid_spec=pltpu.PrefetchScalarGridSpec(
+            num_scalar_prefetch=1,
+            grid=(PANELS,),
+            in_specs=[pl.BlockSpec(shape, lambda p, at: (slot_with(at, at[3 + blocks + p], blocks) // 2, 0, 0, 0))],
+            out_specs=pl.BlockSpec(shape, lambda p, at: (p, 0, 0, 0)),
+        ),
+        compiler_params=pltpu.CompilerParams(vmem_limit_bytes=8 * MB),
+        name="pivot_tiles",
+    )(at, rows)
 
 
 def features(coords_ref, block, left):
@@ -367,12 +421,12 @@
     return hi, mid, low
 
 
-def schur_kernel(info, re_ref, im_ref, mine_ref, other_ref, c_ref, r_ref, out_ref):
-    core = info[0]
+def schur_kernel(blocks, at, re_ref, im_ref, mine_ref, other_ref, c_ref, r_ref, out_ref):
+    core = at[2]
     funcs = mine_ref.shape[2]
     b = []
     for p in range(PANELS):
-        local = info[1 + p] == core
+        local = slot_with(at, at[3 + blocks + p], blocks) % 2 == core
         b.append([jnp.where(local, mine_ref[p, k].astype(f32), other_ref[p, k].astype(f32)).astype(bf16) for k in range(2)])
     br = jnp.concatenate([b[p][0] for p in range(PANELS)], 0)
     bi = jnp.concatenate([b[p][1] for p in range(PANELS)], 0)
@@ -392,15 +446,15 @@
     out_ref[1] = r_ref[1] - (prod[:rows, cols:] + prod[rows:, :cols])
 
 
-def schur_tile(info, re, im, mine, other, column, reduced):
-    return pl.pallas_call(
-        schur_kernel,
+def schur_tile(at, blocks, re, im, mine, other, column, reduced):
+    return pl.pallas_call(
+        functools.partial(schur_kernel, blocks),
         out_shape=jax.ShapeDtypeStruct(reduced.shape, f32),
         in_specs=[SMEM] + [VMEM] * 6,
         out_specs=VMEM,
         compiler_params=pltpu.CompilerParams(vmem_limit_bytes=12 * MB),
         name="schur",
-    )(info, re, im, mine, other, column, reduced)
+    )(at, re, im, mine, other, column, reduced)
 
 
 def on_device(inverse, excite, coordinates, block_of_slot, panel_order):
@@ -416,8 +470,6 @@
     def spread(x, axis, groups=None):
         return lax.all_to_all(x, axis, split_axis=0, concat_axis=0, tiled=True, axis_index_groups=groups)
 
-    order = jnp.arange(blocks, dtype=i32)
-    slot_of = jnp.sum(jnp.where(block_of_slot[None, :] == order[:, None], order[None, :], 0), axis=1)
     pivots = panel_order[:PANELS]
 
     own, halves = basis_rows(inverse, excite, blk_size)
@@ -435,12 +487,7 @@
     green = green_tiles(at, coordinates, 2, PANELS, tiles, [green])
     green = green_tiles(at, coordinates, 1, 1, tiles, [green])
 
-    wanted = jnp.concatenate(
-        [order.reshape(grp_size, slabs), jnp.broadcast_to(pivots[None], (grp_size, PANELS))], axis=1
-    )
-    from_slot = jnp.sum(jnp.where(wanted[:, :, None] == order, slot_of, 0), axis=2)
-    picked = sliced.at[from_slot.reshape(-1)].get(mode="promise_in_bounds")
-    picked = picked.reshape(*from_slot.shape, *sliced.shape[1:])
+    picked = gathered(at, sliced, grp_size, slabs)
     mine = spread(picked, "grp")
     other = lax.ppermute(mine, "blk", swap)
 
@@ -456,14 +503,11 @@
         take = ((grp ^ column_at) & bit) != 0
         column = jnp.where(take[:, None, None, None], came, column)
         bit *= 2
-    pivot_slot = jnp.sum(jnp.where(pivots[:, None] == order, slot_of, 0), axis=1)
-    row_mine = jnp.stack([lax.dynamic_index_in_dim(rows, pivot_slot[p] // 2, 0, keepdims=False) for p in range(PANELS)])
+    row_mine = pivot_tiles(at, rows, blocks)
     row_other = lax.ppermute(row_mine, "blk", swap)
-    core1 = core.reshape(1)
     re, im = pivot_exchange(0, at, pivot_rows, pivot_other)
     re, im = pivot_exchange(1, at, re, im)
-    info = jnp.concatenate([core1, pivot_slot % 2]).astype(i32)
-    schur = schur_tile(info, re, im, row_mine, row_other, column, reduced)
+    schur = schur_tile(at, blocks, re, im, row_mine, row_other, column, reduced)
     return (reduced, schur)
 
 

time: 142 us -> 135 us (0.951)
  between operations: 5.99 us -> 0.79 us
  local copies, waits for them, and re-layouts: 5.1 us -> 2.83 us
    pallas_call x1 -> x3, Pallas kernels: 2.29 us -> 3.66 us  [the longest x1 2.34 us: schur_tile(): pl.pallas_call(functools.partial(schur_kernel, blocks), out_shape=jax.Sha...]
  transfers between devices with their start and end apart: 11 -> 11, of which waited for: 4 -> 5; matrix products, arithmetic and copies ran while one was open for 3% -> 1% of each run, Pallas kernels for 40% -> 49%
where the time goes in v5:
time: 135 us; the launch traced here: 133 us
  Pallas kernels  69.6 us (52%)
  blocking collectives  23.9 us (18%)
  starting transfers between devices  18.9 us (14%)
  waiting for transfers between devices  16.5 us (12%)
  local copies, waits for them, and re-layouts  2.83 us (2%)
    pallas_call x3, Pallas kernels, green_tiles(): pl.pallas_call(functools.partial(green_kernel, first), out_shape=pltpu.HB...  29 us
    all_to_all x1, blocking collectives, spread(): lax.all_to_all(x, axis, split_axis=0, concat_axis=0, tiled=True, axis_ind...  23.9 us
    pallas_call x2, Pallas kernels, pivot_exchange(): pl.pallas_call(functools.partial(inverse_kernel, kb), out_shape=(part, pa...  19.7 us
    pallas_call x2, Pallas kernels, couplings(): pl.pallas_call(functools.partial(coupling_kernel, pivot, 3 + blocks), out...  16.1 us
    all_to_all x2, waiting for transfers between devices, spread(): lax.all_to_all(x, axis, split_axis=0, concat_axis=0, tiled=True, axis_ind...  10.3 us
    all_to_all x2, starting transfers between devices, spread(): lax.all_to_all(x, axis, split_axis=0, concat_axis=0, tiled=True, axis_ind...  9.17 us
    ppermute x3, starting transfers between devices, on_device(): came = lax.ppermute(column, 'grp', [(g, g ^ bit) for g in range(grp_size)])  6.84 us
    ppermute x3, waiting for transfers between devices, on_device(): lax.ppermute(held, 'grp', [(g, g ^ bit) for g in range(grp_size)])  5.68 us
  transfers between devices with their start and end apart: 11, of which 5 were waited for; matrix products, arithmetic and copies ran while one was open for 1% of the time, Pallas kernels for 49%

profile of v5, /device:TPU:0, one launch (start us, length us, event | category | flops | bytes accessed | tf_op | source)
XLA Modules:
  0.0 132.8 jit_solution(18241380459866945769)
XLA Ops:
  0.6 0.0 copy-start
  0.6 1.0 copy-done
  1.7 0.0 copy-start.1
  1.7 1.0 copy-done.1
  2.7 1.1 basis.1
  3.9 5.6 %all-to-all-start = ((bf16[16,2,64,128]{3,2,1,0:T(8,128)(2,1)}), bf16[16,2,64,128]{3,2,1,0:T(8,128)(2,1)S(1)}, u32[]{:S(2)}, u32[]{:S(2)}) async-start(bf16[16,2,64,128]{3,2,1,0:T(8,128)(2,1)} %get-tuple-element.11), calls=%async_computation | async-start | bytes 1048576 | tf_op jit(solution)/shard_map/all_to_all | solution.py:471
  9.5 0.7 concatenate.10.at_ref.at
  10.2 10.1 %all-to-all-done.rows_ref = bf16[16,2,64,128]{3,2,1,0:T(8,128)(2,1)S(1)} async-done(((bf16[16,2,64,128]{3,2,1,0:T(8,128)(2,1)}), bf16[16,2,64,128]{3,2,1,0:T(8,128)(2,1)S(1)}, u32[]{:S(2)}, u32[]{:S(2)}) %all-to-all-start) | async-done | bytes 524320 | tf_op jit(solution)/shard_map/all_to_all | solution.py:471
  20.3 0.7 gathered.1
  21.0 23.9 %all_to_all.15.mine_ref = bf16[8,4,2,64,128]{4,3,2,1,0:T(8,128)(2,1)S(1)} all-to-all(bf16[8,4,2,64,128]{4,3,2,1,0:T(8,128)(2,1)S(1)} %gathered.1), channel_id=1, replica_groups=mesh['blk'=16,'grp'=8] {'grp'}, dimensions={0} | all-to-all | bytes 2097152 | tf_op jit(solution)/shard_map/all_to_all | solution.py:471
  44.9 0.0 collective-permute-start
  44.9 0.9 collective-permute-start.1
  45.7 7.7 %shard_map.68.refs_0_ = bf16[4,2,1024,1024]{3,2,1,0:T(8,128)(2,1)} custom-call(s32[35]{0:T(128)S(1)} %concatenate.10.at_ref.at, s32[3,16,1024]{2,1,0:T(8,128)} %coords_ref.5), custom_call_target="tpu_custom_call" | custom-call | flops 31457280 | bytes 4194304 | tf_op jit(solution)/shard_map/pallas_call | solution.py:180
  53.5 13.5 %shard_map.69.refs_0_ = bf16[4,2,1024,1024]{3,2,1,0:T(8,128)(2,1)} custom-call(s32[35]{0:T(128)S(1)} %concatenate.10.at_ref.at, s32[3,16,1024]{2,1,0:T(8,128)} %coords_ref.5, bf16[4,2,1024,1024]{3,2,1,0:T(8,128)(2,1)} %shard_map.68.refs_0_), custom_call_target="tpu_custom_call", output_to_operand_aliasing={{}: (2, {})} | custom-call | flops 62914560 | bytes 8388608 | tf_op jit(solution)/shard_map/pallas_call | solution.py:180
  67.0 0.0 copy-start.3
  67.0 7.8 %shard_map.70.g_ref = bf16[4,2,1024,1024]{3,2,1,0:T(8,128)(2,1)} custom-call(s32[35]{0:T(128)S(1)} %concatenate.10.at_ref.at, s32[3,16,1024]{2,1,0:T(8,128)} %coords_ref.5, bf16[4,2,1024,1024]{3,2,1,0:T(8,128)(2,1)} %shard_map.69.refs_0_), custom_call_target="tpu_custom_call", output_to_operand_aliasing={{}: (2, {})} | custom-call | flops 31457280 | bytes 4194304 | tf_op jit(solution)/shard_map/pallas_call | solution.py:180
  74.8 0.0 collective-permute-done.1.refs_1_
  74.8 0.6 collective-permute-start.2
  75.4 0.0 copy-done.3
  75.4 5.1 %collective-permute-done.2.refs_2_ = bf16[2,2,128,128]{3,2,1,0:T(8,128)(2,1)S(1)} collective-permute-done((bf16[2,2,128,128]{3,2,1,0:T(8,128)(2,1)S(1)}, bf16[2,2,128,128]{3,2,1,0:T(8,128)(2,1)S(1)}, u32[]{:S(2)}, u32[]{:S(2)}) %collective-permute-start.2) | collective-permute-done | bytes 131104 | tf_op jit(solution)/shard_map/ppermute | solution.py:480
  80.5 1.0 collective-permute-start.3
  81.5 0.0 collective-permute-done.other_ref
  81.5 7.5 %shard_map.71.refs_4_.first_ref = f32[2,128,256]{2,1,0:T(8,128)S(1)} custom-call(s32[35]{0:T(128)S(1)} %concatenate.10.at_ref.at, bf16[4,2,1024,1024]{3,2,1,0:T(8,128)(2,1)} %shard_map.70.g_ref, bf16[8,4,2,64,128]{4,3,2,1,0:T(8,128)(2,1)S(1)} %all_to_all.15.mine_ref, bf16[8,4,2,64,128]{4,3,2,1,0:T(8,128)(2,1)S(1)} %collective-permute-done.other_ref), custom_call_target="tpu_custom_call" | custom-call | flops 4294967296 | bytes 8388608 | tf_op jit(solution)/shard_map/pallas_call | solution.py:281
  89.0 0.1 collective-permute-start.4
  89.1 0.6 collective-permute-done.3.refs_3_
  89.7 8.6 %shard_map.72 = (f32[2,128,256]{2,1,0:T(8,128)}, bf16[8,2,128,256]{3,2,1,0:T(8,128)(2,1)}, bf16[2,2,128,128]{3,2,1,0:T(8,128)(2,1)S(1)}) custom-call(s32[35]{0:T(128)S(1)} %concatenate.10.at_ref.at, bf16[4,2,1024,1024]{3,2,1,0:T(8,128)(2,1)} %shard_map.70.g_ref, bf16[8,4,2,64,128]{4,3,2,1,0:T(8,128)(2,1)S(1)} %all_to_all.15.mine_ref, ...), custom_call_target="tpu_custom_call" | custom-call | flops 4294967296 | bytes 8388608 | tf_op jit(solution)/shard_map/pallas_call | solution.py:281
  98.3 2.7 %collective-permute-start.6 = (bf16[2,2,128,128]{3,2,1,0:T(8,128)(2,1)S(1)}, bf16[2,2,128,128]{3,2,1,0:T(8,128)(2,1)S(1)}, u32[]{:S(2)}, u32[]{:S(2)}) collective-permute-start(bf16[2,2,128,128]{3,2,1,0:T(8,128)(2,1)S(1)} %get-tuple-element.19), channel_id=1, source_target_pairs={{0,1},{1,0},{2,3},{3,2},{4,5},{5,4},{6,7},{7,6},{8,9},{9,8},{10,11... | collective-permute-start | bytes 393224 | tf_op jit(solution)/shard_map/ppermute | solution.py:502
  101.0 3.6 %all-to-all-start.2 = ((bf16[8,2,128,256]{3,2,1,0:T(8,128)(2,1)}), bf16[8,2,128,256]{3,2,1,0:T(8,128)(2,1)S(1)}, u32[]{:S(2)}, u32[]{:S(2)}) async-start(bf16[8,2,128,256]{3,2,1,0:T(8,128)(2,1)} %get-tuple-element.18), calls=%async_computation.2 | async-start | bytes 2097152 | tf_op jit(solution)/shard_map/all_to_all | solution.py:471
  104.5 0.5 collective-permute-done.6
  105.1 0.1 broadcast_select_fusion
  105.1 1.4 %collective-permute-start.7 = (bf16[2,2,128,128]{3,2,1,0:T(8,128)(2,1)S(1)}, bf16[2,2,128,128]{3,2,1,0:T(8,128)(2,1)S(1)}, u32[]{:S(2)}, u32[]{:S(2)}) collective-permute-start(bf16[2,2,128,128]{3,2,1,0:T(8,128)(2,1)S(1)} %broadcast_select_fusion), channel_id=1, source_target_pairs={{0,2},{1,3},{2,0},{3,1},{4,6},{5,7},{6,4},{7,5},{8,10},{9,11},{10,... | collective-permute-start | bytes 393224 | tf_op jit(solution)/shard_map/ppermute | solution.py:502
  106.5 0.0 collective-permute-done.4.second_ref
  106.5 9.8 %shard_map.73 = (f32[2,256,128]{2,1,0:T(8,128)S(1)}, f32[2,256,128]{2,1,0:T(8,128)S(1)}) custom-call(s32[35]{0:T(128)S(1)} %concatenate.10.at_ref.at, f32[2,128,256]{2,1,0:T(8,128)S(1)} %shard_map.71.refs_4_.first_ref, f32[2,128,256]{2,1,0:T(8,128)S(1)} %collective-permute-done.4.second_ref), custom_call_target="tpu_custom_call" | custom-call | flops 6000000000 | bytes 1048576 | tf_op jit(solution)/shard_map/pallas_call | solution.py:405
  116.4 0.0 copy-start.2
  116.4 0.0 collective-permute-done.7
  116.4 0.1 broadcast_select_fusion.1
  116.5 2.8 %collective-permute-start.8 = (bf16[2,2,128,128]{3,2,1,0:T(8,128)(2,1)S(1)}, bf16[2,2,128,128]{3,2,1,0:T(8,128)(2,1)S(1)}, u32[]{:S(2)}, u32[]{:S(2)}) collective-permute-start(bf16[2,2,128,128]{3,2,1,0:T(8,128)(2,1)S(1)} %broadcast_select_fusion.1), channel_id=1, source_target_pairs={{0,4},{1,5},{2,6},{3,7},{4,0},{5,1},{6,2},{7,3},{8,12},{9,13},{10,... | collective-permute-start | bytes 393224 | tf_op jit(solution)/shard_map/ppermute | solution.py:502
  119.2 0.3 all-to-all-done.2.row_ref
  119.5 0.7 pivot_tiles.1.mine_ref
  120.2 0.3 collective-permute-start.5
  120.5 9.9 %shard_map.74 = (f32[2,256,128]{2,1,0:T(8,128)S(1)}, f32[2,256,128]{2,1,0:T(8,128)S(1)}) custom-call(s32[35]{0:T(128)S(1)} %concatenate.10.at_ref.at, f32[2,256,128]{2,1,0:T(8,128)S(1)} %get-tuple-element.14.first_ref, f32[2,256,128]{2,1,0:T(8,128)S(1)} %get-tuple-element.15.second_ref), custom_call_target="tpu_custom_call" | custom-call | flops 6000000000 | bytes 1048576 | tf_op jit(solution)/shard_map/pallas_call | solution.py:405
  130.3 0.0 collective-permute-done.8
  130.3 0.1 broadcast_select_fusion.2.c_ref
  130.4 0.0 collective-permute-done.5.other_ref
  130.4 0.0 copy-done.2
  130.5 2.3 %schur.1 = f32[2,128,256]{2,1,0:T(8,128)} custom-call(s32[35]{0:T(128)S(1)} %concatenate.10.at_ref.at, f32[2,256,128]{2,1,0:T(8,128)S(1)} %get-tuple-element.16.re_ref, f32[2,256,128]{2,1,0:T(8,128)S(1)} %get-tuple-element.17.im_ref, bf16[2,2,128,256]{3,2,1,0:T(8,128)(2,1)S(1)} %pivot_tiles.1.mine_ref, ...), custom_call_target="tpu_custom_call" | custom-call | tf_op jit(solution)/shard_map/schur/pallas_call | solution.py:450
  (4 shorter events, 0.1 us)
Async XLA Ops:
  0.6 1.0 copy-start
  1.7 1.0 copy-start.1
  3.9 16.4 %all-to-all-start = ((bf16[16,2,64,128]{3,2,1,0:T(8,128)(2,1)}), bf16[16,2,64,128]{3,2,1,0:T(8,128)(2,1)S(1)}, u32[]{:S(2)}, u32[]{:S(2)}) async-start(bf16[16,2,64,128]{3,2,1,0:T(8,128)(2,1)} %get-tuple-element.11), calls=%async_computation | async-start | bytes 1048576 | tf_op jit(solution)/shard_map/all_to_all | solution.py:471
  44.9 36.6 %collective-permute-start = (bf16[8,4,2,64,128]{4,3,2,1,0:T(8,128)(2,1)S(1)}, bf16[8,4,2,64,128]{4,3,2,1,0:T(8,128)(2,1)S(1)}, u32[]{:S(2)}, u32[]{:S(2)}) collective-permute-start(bf16[8,4,2,64,128]{4,3,2,1,0:T(8,128)(2,1)S(1)} %all_to_all.15.mine_ref), channel_id=1, source_target_pairs={{0,8},{8,0},{16,24},{24,16},{32,40},{40,32},{48,56},{56,48},{64,72... | collective-permute-start | bytes 3145736 | tf_op jit(solution)/shard_map/ppermute | solution.py:492
  44.9 29.9 %collective-permute-start.1 = (bf16[1,2,128,128]{3,2,1,0:T(8,128)(2,1)S(1)}, bf16[1,2,128,128]{3,2,1,0:T(8,128)(2,1)S(1)}, u32[]{:S(2)}, u32[]{:S(2)}) collective-permute-start(bf16[1,2,128,128]{3,2,1,0:T(8,128)(2,1)S(1)} %get-tuple-element.12.refs_0_), channel_id=1, source_target_pairs={{0,1},{1,0},{2,3},{3,2},{4,5},{5,4},{6,7},{7,6},{8,9},{9,8},{10,11... | collective-permute-start | bytes 196616 | tf_op jit(solution)/shard_map/ppermute | solution.py:480
  67.0 8.5 %copy-start.3 = (s32[16]{0:T(128)S(1)}, s32[16]{0:T(128)}, u32[]{:S(2)}) copy-start(s32[16]{0:T(128)} %param.9) | copy-start | bytes 196
  74.8 5.7 %collective-permute-start.2 = (bf16[2,2,128,128]{3,2,1,0:T(8,128)(2,1)S(1)}, bf16[2,2,128,128]{3,2,1,0:T(8,128)(2,1)S(1)}, u32[]{:S(2)}, u32[]{:S(2)}) collective-permute-start(bf16[2,2,128,128]{3,2,1,0:T(8,128)(2,1)S(1)} %pad_maximum_fusion.1), channel_id=1, source_target_pairs={{0,2},{1,3},{2,0},{3,1},{4,6},{5,7},{6,4},{7,5},{8,10},{9,11},{10,... | collective-permute-start | bytes 393224 | tf_op jit(solution)/shard_map/ppermute | solution.py:480
  80.5 9.2 %collective-permute-start.3 = (bf16[4,2,128,128]{3,2,1,0:T(8,128)(2,1)S(1)}, bf16[4,2,128,128]{3,2,1,0:T(8,128)(2,1)S(1)}, u32[]{:S(2)}, u32[]{:S(2)}) collective-permute-start(bf16[4,2,128,128]{3,2,1,0:T(8,128)(2,1)S(1)} %pad_maximum_fusion), channel_id=1, source_target_pairs={{0,4},{1,5},{2,6},{3,7},{4,0},{5,1},{6,2},{7,3},{8,12},{9,13},{10,... | collective-permute-start | bytes 786440 | tf_op jit(solution)/shard_map/ppermute | solution.py:480
  89.0 17.6 %collective-permute-start.4 = (f32[2,128,256]{2,1,0:T(8,128)S(1)}, f32[2,128,256]{2,1,0:T(8,128)S(1)}, u32[]{:S(2)}, u32[]{:S(2)}) collective-permute-start(f32[2,128,256]{2,1,0:T(8,128)S(1)} %shard_map.71.refs_4_.first_ref), channel_id=1, source_target_pairs={{0,8},{8,0},{16,24},{24,16},{32,40},{40,32},{48,56},{56,48},{64,72... | collective-permute-start | bytes 786440 | tf_op jit(solution)/shard_map/ppermute | solution.py:495
  98.3 6.8 %collective-permute-start.6 = (bf16[2,2,128,128]{3,2,1,0:T(8,128)(2,1)S(1)}, bf16[2,2,128,128]{3,2,1,0:T(8,128)(2,1)S(1)}, u32[]{:S(2)}, u32[]{:S(2)}) collective-permute-start(bf16[2,2,128,128]{3,2,1,0:T(8,128)(2,1)S(1)} %get-tuple-element.19), channel_id=1, source_target_pairs={{0,1},{1,0},{2,3},{3,2},{4,5},{5,4},{6,7},{7,6},{8,9},{9,8},{10,11... | collective-permute-start | bytes 393224 | tf_op jit(solution)/shard_map/ppermute | solution.py:502
  101.0 18.5 %all-to-all-start.2 = ((bf16[8,2,128,256]{3,2,1,0:T(8,128)(2,1)}), bf16[8,2,128,256]{3,2,1,0:T(8,128)(2,1)S(1)}, u32[]{:S(2)}, u32[]{:S(2)}) async-start(bf16[8,2,128,256]{3,2,1,0:T(8,128)(2,1)} %get-tuple-element.18), calls=%async_computation.2 | async-start | bytes 2097152 | tf_op jit(solution)/shard_map/all_to_all | solution.py:471
  105.1 11.2 %collective-permute-start.7 = (bf16[2,2,128,128]{3,2,1,0:T(8,128)(2,1)S(1)}, bf16[2,2,128,128]{3,2,1,0:T(8,128)(2,1)S(1)}, u32[]{:S(2)}, u32[]{:S(2)}) collective-permute-start(bf16[2,2,128,128]{3,2,1,0:T(8,128)(2,1)S(1)} %broadcast_select_fusion), channel_id=1, source_target_pairs={{0,2},{1,3},{2,0},{3,1},{4,6},{5,7},{6,4},{7,5},{8,10},{9,11},{10,... | collective-permute-start | bytes 393224 | tf_op jit(solution)/shard_map/ppermute | solution.py:502
  116.4 14.1 %copy-start.2 = (f32[2,128,256]{2,1,0:T(8,128)S(1)}, f32[2,128,256]{2,1,0:T(8,128)}, u32[]{:S(2)}) copy-start(f32[2,128,256]{2,1,0:T(8,128)} %get-tuple-element.9.r_ref) | copy-start | bytes 786436
  116.5 13.9 %collective-permute-start.8 = (bf16[2,2,128,128]{3,2,1,0:T(8,128)(2,1)S(1)}, bf16[2,2,128,128]{3,2,1,0:T(8,128)(2,1)S(1)}, u32[]{:S(2)}, u32[]{:S(2)}) collective-permute-start(bf16[2,2,128,128]{3,2,1,0:T(8,128)(2,1)S(1)} %broadcast_select_fusion.1), channel_id=1, source_target_pairs={{0,4},{1,5},{2,6},{3,7},{4,0},{5,1},{6,2},{7,3},{8,12},{9,13},{10,... | collective-permute-start | bytes 393224 | tf_op jit(solution)/shard_map/ppermute | solution.py:502
  120.2 10.3 %collective-permute-start.5 = (bf16[2,2,128,256]{3,2,1,0:T(8,128)(2,1)S(1)}, bf16[2,2,128,256]{3,2,1,0:T(8,128)(2,1)S(1)}, u32[]{:S(2)}, u32[]{:S(2)}) collective-permute-start(bf16[2,2,128,256]{3,2,1,0:T(8,128)(2,1)S(1)} %pivot_tiles.1.mine_ref), channel_id=1, source_target_pairs={{0,8},{8,0},{16,24},{24,16},{32,40},{40,32},{48,56},{56,48},{64,72... | collective-permute-start | bytes 786440 | tf_op jit(solution)/shard_map/ppermute | solution.py:507

commit v6 on v5

--- a/solution.py
+++ b/solution.py
@@ -23,9 +23,8 @@
 VMEM = pl.BlockSpec(memory_space=pltpu.VMEM)
 SMEM = pl.BlockSpec(memory_space=pltpu.SMEM)
 MB = 1 << 20
-COUPLE_ROWS = 512
-GREEN_ROWS = 512
-STRIPS = 4
+COUPLE_ROWS = 1024
+STRIPS = 8
 
 
 def horner(coefs, g):
@@ -66,11 +65,12 @@
             jax.ShapeDtypeStruct((1, 2, rows, cols), bf16),
             jax.ShapeDtypeStruct((devices, 2, rows // 2, cols), bf16),
         ),
-        in_specs=[VMEM, VMEM],
+        grid=(1,),
+        in_specs=[pl.BlockSpec(x.shape, lambda i: (0, 0, 0, 0)) for x in (inverse, excite)],
         out_specs=(VMEM, VMEM),
         compiler_params=pltpu.CompilerParams(vmem_limit_bytes=8 * MB),
         name="basis",
-    )(inverse, excite)
+    )(*[pltpu.with_memory_space_constraint(x, pltpu.HBM) for x in (inverse, excite)])
 
 
 def slot_with(at, block, blocks):
@@ -137,15 +137,21 @@
     return jnp.concatenate([v.astype(f32) for v in rows + [zero]], 0).astype(bf16)
 
 
-def green_kernel(tiles, at_ref, coords_ref, *refs):
-    g_ref, fl_ref, fr_ref, sq_ref = refs[-4:]
+def green_kernel(first, whole, carried, at_ref, coords_ref, *refs):
+    sources, g_ref, targets = refs[:carried], refs[carried], refs[carried + 1 : 2 * carried + 1]
+    fl_ref, fr_ref, sq_ref, *sems = refs[2 * carried + 1 :]
+    copies = [pltpu.make_async_copy(a, b, sem) for a, b, sem in zip(sources, targets, sems)]
+    for copy in copies:
+        copy.start()
     rows, _ = sq_ref.shape
-    tile, chunk = pl.program_id(0) + tiles, pl.program_id(1)
+    local, chunk = pl.program_id(0), pl.program_id(1)
+    tile = local + first
     blocks = coords_ref.shape[1]
     own, grp, core = at_ref[3 + at_ref[0]], at_ref[1], at_ref[2]
     main = tile < 2
     left = jnp.where(main, own, at_ref[3 + blocks + core])
     right = jnp.where(main, grp * 2 + tile, at_ref[3 + blocks + jnp.maximum(tile - 2, 0)])
+    held, base = (local, chunk * rows) if whole else (0, 0)
 
     @pl.when(chunk == 0)
     def _():
@@ -158,42 +164,58 @@
     )
 
     def strip(i, _):
-        r = pl.ds(pl.multiple_of(i * 8, 8), 8)
-        re, im = half_green(sq_ref[r, :])
-        g_ref[0, 0, r, :] = re.astype(bf16)
-        g_ref[0, 1, r, :] = im.astype(bf16)
+        re, im = half_green(sq_ref[pl.ds(pl.multiple_of(i * 8, 8), 8), :])
+        r = pl.ds(pl.multiple_of(base + i * 8, 8), 8)
+        g_ref[held, 0, r, :] = re.astype(bf16)
+        g_ref[held, 1, r, :] = im.astype(bf16)
         return 0
 
     lax.fori_loop(0, rows // 8, strip, 0, unroll=STRIPS)
 
     @pl.when(left == right)
     def _():
-        same = lax.broadcasted_iota(i32, (rows, rows), 0) == lax.broadcasted_iota(i32, (rows, rows), 1)
-        for part, value in ((0, SELF_REAL), (1, SELF_IMAG)):
-            block = g_ref[0, part, :, at].astype(f32)
-            g_ref[0, part, :, at] = jnp.where(same, value, block).astype(bf16)
-
-
-def green_tiles(at, coordinates, first, count, tiles, held):
+        size = 256
+        same = lax.broadcasted_iota(i32, (size, size), 0) == lax.broadcasted_iota(i32, (size, size), 1)
+        for k in range(rows // size):
+            r = pl.ds(pl.multiple_of(base + k * size, size), size)
+            c = pl.ds(pl.multiple_of(chunk * rows + k * size, size), size)
+            for part, value in ((0, SELF_REAL), (1, SELF_IMAG)):
+                block = g_ref[held, part, r, c].astype(f32)
+                g_ref[held, part, r, c] = jnp.where(same, value, block).astype(bf16)
+
+    for copy in copies:
+        copy.wait()
+
+
+def green_tiles(at, coordinates, first, count, whole, carry=()):
     unk = coordinates.shape[2]
-    rows = GREEN_ROWS
-    return pl.pallas_call(
-        functools.partial(green_kernel, first),
-        out_shape=pltpu.HBM((tiles, 2, unk, unk), bf16),
+    rows = unk if whole else unk // 2
+    shape = (count, 2, unk, unk)
+    return pl.pallas_call(
+        functools.partial(green_kernel, first, whole, len(carry)),
+        out_shape=[(pltpu.VMEM if whole else pltpu.HBM)(shape, bf16)] + [pltpu.VMEM(x.shape, x.dtype) for x in carry],
         grid=(count, unk // rows),
         in_specs=[SMEM, pl.BlockSpec(coordinates.shape, lambda t, m: (0, 0, 0))]
-        + [pl.BlockSpec(memory_space=pltpu.HBM)] * len(held),
-        out_specs=pl.BlockSpec((1, 2, rows, unk), lambda t, m: (t + first, 0, m, 0)),
-        scratch_shapes=[pltpu.VMEM((8, unk), bf16), pltpu.VMEM((8, unk), bf16), pltpu.VMEM((rows, unk), f32)],
-        input_output_aliases={2: 0} if held else {},
+        + [pl.BlockSpec(memory_space=pltpu.HBM)] * len(carry),
+        out_specs=[VMEM if whole else pl.BlockSpec((1, 2, rows, unk), lambda t, m: (t, 0, m, 0))] + [VMEM] * len(carry),
+        scratch_shapes=[pltpu.VMEM((8, unk), bf16), pltpu.VMEM((8, unk), bf16), pltpu.VMEM((rows, unk), f32)]
+        + [pltpu.SemaphoreType.DMA] * len(carry),
         compiler_params=pltpu.CompilerParams(vmem_limit_bytes=10 * MB),
         cost_estimate=pl.CostEstimate(
             flops=count * unk * unk * 30, transcendentals=count * unk * unk, bytes_accessed=count * unk * unk * 4
         ),
-    )(at, pltpu.with_memory_space_constraint(coordinates, pltpu.HBM), *held)
-
-
-def coupling_kernel(pivot, panel_at, at_ref, g_ref, mine_ref, other_ref, *refs):
+    )(at, *[pltpu.with_memory_space_constraint(x, pltpu.HBM) for x in (coordinates, *carry)])
+
+
+def add_tile(y, left, acc):
+    y_hi = y.astype(bf16)
+    y_lo = (y - y_hi.astype(f32)).astype(bf16)
+    acc[...] += jnp.dot(left, y_hi, preferred_element_type=f32) + jnp.dot(left, y_lo, preferred_element_type=f32)
+
+
+def coupling_kernel(pivot, panel_at, greens, at_ref, *refs):
+    g_refs, refs = refs[:greens], refs[greens:]
+    mine_ref, other_ref, refs = refs[0], refs[1], refs[2:]
     if pivot:
         out_ref, lhs, stage, top, bottom, acc = refs
     else:
@@ -203,7 +225,7 @@
     chunks = pl.num_programs(1)
     grp, core = at_ref[1], at_ref[2]
     groups, _, _, half, cols = mine_ref.shape
-    rows = g_ref.shape[2]
+    rows = COUPLE_ROWS
     first = 2 if pivot else 0
     halves = ((mine_ref, core), (other_ref, 1 - core))
 
@@ -240,12 +262,20 @@
                 bottom[r, :cols] = -ji
                 bottom[r, cols:] = jr
 
-    y = jnp.dot(g_ref[0, 0], top[...], preferred_element_type=f32)
-    y += jnp.dot(g_ref[0, 1], bottom[...], preferred_element_type=f32)
-    y_hi = y.astype(bf16)
-    y_lo = (y - y_hi.astype(f32)).astype(bf16)
-    left = lhs[:, pl.ds(pl.multiple_of(chunk * rows, rows), rows)]
-    acc[...] += jnp.dot(left, y_hi, preferred_element_type=f32) + jnp.dot(left, y_lo, preferred_element_type=f32)
+    at_rows = pl.ds(pl.multiple_of(chunk * rows, rows), rows)
+
+    def product(g_ref, held):
+        y = jnp.dot(g_ref[held, 0, at_rows, :], top[...], preferred_element_type=f32)
+        return y + jnp.dot(g_ref[held, 1, at_rows, :], bottom[...], preferred_element_type=f32)
+
+    if greens == 1:
+        add_tile(product(g_refs[0], tile), lhs[:, at_rows], acc)
+    else:
+        for n, g_ref in enumerate(g_refs):
+
+            @pl.when(tile == n)
+            def _():
+                add_tile(product(g_ref, 0), lhs[:, at_rows], acc)
 
     @pl.when(chunk == chunks - 1)
     def _():
@@ -263,11 +293,10 @@
                         column_ref[p, part] = value.astype(bf16)
 
 
-def couplings(at, blocks, green, mine, other, pieces, after, pivot):
-    _, _, unk, _ = green.shape
+def couplings(at, blocks, greens, mine, other, pieces, after, pivot):
+    unk = greens[0].shape[2]
     cols = mine.shape[4]
     tiles = 2
-    first = 2 if pivot else 0
     rows = COUPLE_ROWS
     copies = 8
     whole = lambda x: pl.BlockSpec(x.shape, lambda t, m: (0,) * x.ndim)
@@ -279,10 +308,10 @@
         out_shape.append(jax.ShapeDtypeStruct((PANELS, 2, cols, cols), bf16))
         out_specs.append(pl.BlockSpec((PANELS, 2, cols, cols), lambda t, m: (0, 0, 0, 0)))
     return pl.pallas_call(
-        functools.partial(coupling_kernel, pivot, 3 + blocks),
+        functools.partial(coupling_kernel, pivot, 3 + blocks, len(greens)),
         out_shape=out_shape,
         grid=(tiles, unk // rows),
-        in_specs=[SMEM, pl.BlockSpec((1, 2, rows, unk), lambda t, m: (t + first, 0, m, 0))]
+        in_specs=[SMEM] + [VMEM] * len(greens)
         + [whole(x) for x in (mine, other, *pieces)]
         + [pl.BlockSpec(memory_space=pl.ANY)] * len(after),
         out_specs=out_specs,
@@ -293,11 +322,11 @@
             pltpu.VMEM((unk, 2 * cols), bf16),
             pltpu.VMEM((2 * cols, 2 * cols), f32),
         ],
-        compiler_params=pltpu.CompilerParams(vmem_limit_bytes=20 * MB),
+        compiler_params=pltpu.CompilerParams(vmem_limit_bytes=16 * MB),
         cost_estimate=pl.CostEstimate(
             flops=tiles * unk * unk * 2048, transcendentals=0, bytes_accessed=tiles * unk * unk * 4
         ),
-    )(at, pltpu.with_memory_space_constraint(green, pltpu.HBM), mine, other, *pieces, *after)
+    )(at, *greens, mine, other, *pieces, *after)
 
 
 WIDE = 128
@@ -482,18 +511,17 @@
         if bit < grp_size:
             held = jnp.concatenate([held, pieces[-1]], 0)
 
-    tiles = slabs + PANELS
-    green = green_tiles(at, coordinates, 0, 1, tiles, [])
-    green = green_tiles(at, coordinates, 2, PANELS, tiles, [green])
-    green = green_tiles(at, coordinates, 1, 1, tiles, [green])
+    (green_first,) = green_tiles(at, coordinates, 0, 1, False)
+    (green_pivot,) = green_tiles(at, coordinates, 2, PANELS, False)
+    green_second, green_first, green_pivot = green_tiles(at, coordinates, 1, 1, True, [green_first, green_pivot])
 
     picked = gathered(at, sliced, grp_size, slabs)
     mine = spread(picked, "grp")
     other = lax.ppermute(mine, "blk", swap)
 
-    (pivot_rows,) = couplings(at, blocks, green, mine, other, [], [], True)
+    (pivot_rows,) = couplings(at, blocks, [green_pivot], mine, other, [], [], True)
     pivot_other = lax.ppermute(pivot_rows, "blk", swap)
-    reduced, copies, column = couplings(at, blocks, green, mine, other, pieces, [pivot_rows], False)
+    reduced, copies, column = couplings(at, blocks, [green_first, green_second], mine, other, pieces, [pivot_rows], False)
 
     rows = spread(copies, "blk", same_core)
     column_at = pivots // slabs

time: 135 us -> 128 us (0.948)
  Pallas kernels: 69.6 us -> 64 us
  waiting for transfers between devices: 16.5 us -> 18.6 us
  local copies, waits for them, and re-layouts: 2.83 us -> 0.76 us
  starting transfers between devices: 18.9 us -> 17.5 us
    pallas_call x5, Pallas kernels: 45.1 us -> 38.3 us  [the longest x3 26.9 us: green_tiles(): pl.pallas_call(functools.partial(green_kernel, first, whole, len(carry)),...]
    ppermute x3, waiting for transfers between devices: 5.68 us -> 7.95 us  [on_device(): lax.ppermute(held, 'grp', [(g, g ^ bit) for g in range(grp_size)])]
    unnamed x8 -> x4, local copies, waits for them, and re-layouts: 2.09 us -> 0.01 us
  transfers between devices with their start and end apart: 11 -> 11, of which waited for: 5 -> 5; matrix products, arithmetic and copies ran while one was open for 1% -> 1% of each run, Pallas kernels for 49% -> 47%
where the time goes in v6:
time: 128 us; the launch traced here: 126 us
  Pallas kernels  64 us (50%)
  blocking collectives  23.9 us (19%)
  waiting for transfers between devices  18.6 us (15%)
  starting transfers between devices  17.5 us (14%)
    pallas_call x3, Pallas kernels, green_tiles(): pl.pallas_call(functools.partial(green_kernel, first, whole, len(carry)),...  26.9 us
    all_to_all x1, blocking collectives, spread(): lax.all_to_all(x, axis, split_axis=0, concat_axis=0, tiled=True, axis_ind...  23.9 us
    pallas_call x2, Pallas kernels, pivot_exchange(): pl.pallas_call(functools.partial(inverse_kernel, kb), out_shape=(part, pa...  19.7 us
    pallas_call x2, Pallas kernels, couplings(): pl.pallas_call(functools.partial(coupling_kernel, pivot, 3 + blocks, len(...  11.4 us
    all_to_all x2, waiting for transfers between devices, spread(): lax.all_to_all(x, axis, split_axis=0, concat_axis=0, tiled=True, axis_ind...  10.2 us
    all_to_all x2, starting transfers between devices, spread(): lax.all_to_all(x, axis, split_axis=0, concat_axis=0, tiled=True, axis_ind...  9.17 us
    ppermute x3, waiting for transfers between devices, on_device(): lax.ppermute(held, 'grp', [(g, g ^ bit) for g in range(grp_size)])  7.95 us
    ppermute x3, starting transfers between devices, on_device(): came = lax.ppermute(column, 'grp', [(g, g ^ bit) for g in range(grp_size)])  5.49 us
  transfers between devices with their start and end apart: 11, of which 5 were waited for; matrix products, arithmetic and copies ran while one was open for 1% of the time, Pallas kernels for 47%

profile of v6, /device:TPU:0, one launch (start us, length us, event | category | flops | bytes accessed | tf_op | source)
XLA Modules:
  0.0 125.8 jit_solution(17869399532633280700)
XLA Ops:
  0.6 2.3 %basis.1 = (bf16[1,2,128,128]{3,2,1,0:T(8,128)(2,1)S(1)}, bf16[16,2,64,128]{3,2,1,0:T(8,128)(2,1)}) custom-call(bf16[2,1,128,1024]{3,2,1,0:T(8,128)(2,1)} %inv_ref.1, bf16[2,1,1024,128]{3,2,1,0:T(8,128)(2,1)} %exc_ref.1), custom_call_target="tpu_custom_call" | custom-call | tf_op jit(solution)/shard_map/basis/pallas_call | solution.py:62
  3.0 5.6 %all-to-all-start = ((bf16[16,2,64,128]{3,2,1,0:T(8,128)(2,1)}), bf16[16,2,64,128]{3,2,1,0:T(8,128)(2,1)S(1)}, u32[]{:S(2)}, u32[]{:S(2)}) async-start(bf16[16,2,64,128]{3,2,1,0:T(8,128)(2,1)} %get-tuple-element.16), calls=%async_computation | async-start | bytes 1048576 | tf_op jit(solution)/shard_map/all_to_all | solution.py:500
  8.6 0.7 concatenate.10.at_ref.at
  9.4 10.1 %all-to-all-done.rows_ref = bf16[16,2,64,128]{3,2,1,0:T(8,128)(2,1)S(1)} async-done(((bf16[16,2,64,128]{3,2,1,0:T(8,128)(2,1)}), bf16[16,2,64,128]{3,2,1,0:T(8,128)(2,1)S(1)}, u32[]{:S(2)}, u32[]{:S(2)}) %all-to-all-start) | async-done | bytes 524320 | tf_op jit(solution)/shard_map/all_to_all | solution.py:500
  19.4 0.7 gathered.1
  20.1 23.9 %all_to_all.15.refs_1_.refs_2_ = bf16[8,4,2,64,128]{4,3,2,1,0:T(8,128)(2,1)S(1)} all-to-all(bf16[8,4,2,64,128]{4,3,2,1,0:T(8,128)(2,1)S(1)} %gathered.1), channel_id=1, replica_groups=mesh['blk'=16,'grp'=8] {'grp'}, dimensions={0} | all-to-all | bytes 2097152 | tf_op jit(solution)/shard_map/all_to_all | solution.py:500
  44.0 0.0 collective-permute-start
  44.0 0.9 collective-permute-start.1
  44.8 7.6 %shard_map.68.refs_0_ = bf16[1,2,1024,1024]{3,2,1,0:T(8,128)(2,1)} custom-call(s32[35]{0:T(128)S(1)} %concatenate.10.at_ref.at, s32[3,16,1024]{2,1,0:T(8,128)} %coords_ref.5), custom_call_target="tpu_custom_call" | custom-call | flops 31457280 | bytes 4194304 | tf_op jit(solution)/shard_map/pallas_call | solution.py:194
  52.4 13.3 %shard_map.69.refs_1_ = bf16[2,2,1024,1024]{3,2,1,0:T(8,128)(2,1)} custom-call(s32[35]{0:T(128)S(1)} %concatenate.10.at_ref.at, s32[3,16,1024]{2,1,0:T(8,128)} %coords_ref.5), custom_call_target="tpu_custom_call" | custom-call | flops 62914560 | bytes 8388608 | tf_op jit(solution)/shard_map/pallas_call | solution.py:194
  65.7 0.0 copy-start.1
  65.7 6.1 %shard_map.70 = (bf16[1,2,1024,1024]{3,2,1,0:T(8,128)(2,1)S(1)}, bf16[1,2,1024,1024]{3,2,1,0:T(8,128)(2,1)S(1)}, bf16[2,2,1024,1024]{3,2,1,0:T(8,128)(2,1)S(1)}) custom-call(s32[35]{0:T(128)S(1)} %concatenate.10.at_ref.at, s32[3,16,1024]{2,1,0:T(8,128)} %coords_ref.5, bf16[1,2,1024,1024]{3,2,1,0:T(8,128)(2,1)} %shard_map.68.refs_0_, ...), custom_call_target="tpu_custom_call" | custom-call | flops 31457280 | bytes 4194304 | tf_op jit(solution)/shard_map/pallas_call | solution.py:194
  71.8 0.0 collective-permute-done.1.refs_5_
  71.8 0.6 collective-permute-start.2
  72.5 0.0 copy-done.1
  72.5 5.0 %collective-permute-done.2.refs_6_ = bf16[2,2,128,128]{3,2,1,0:T(8,128)(2,1)S(1)} collective-permute-done((bf16[2,2,128,128]{3,2,1,0:T(8,128)(2,1)S(1)}, bf16[2,2,128,128]{3,2,1,0:T(8,128)(2,1)S(1)}, u32[]{:S(2)}, u32[]{:S(2)}) %collective-permute-start.2) | collective-permute-done | bytes 131104 | tf_op jit(solution)/shard_map/ppermute | solution.py:509
  77.6 1.0 collective-permute-start.3
  78.6 0.0 collective-permute-done.refs_2_.refs_3_
  78.6 5.2 %shard_map.71.refs_8_.first_ref = f32[2,128,256]{2,1,0:T(8,128)S(1)} custom-call(s32[35]{0:T(128)S(1)} %concatenate.10.at_ref.at, bf16[2,2,1024,1024]{3,2,1,0:T(8,128)(2,1)S(1)} %get-tuple-element.18.refs_0_, bf16[8,4,2,64,128]{4,3,2,1,0:T(8,128)(2,1)S(1)} %all_to_all.15.refs_1_.refs_2_, bf16[8,4,2,64,128]{4,3,2,1,0:T(8,128)(2,1)S(1)} %collective-permute-done.refs_2_.refs_3_), custom_call_target="tpu_custom_call" | custom-call | flops 4294967296 | bytes 8388608 | tf_op jit(solution)/shard_map/pallas_call | solution.py:310
  83.8 0.1 collective-permute-start.4
  83.9 2.9 %collective-permute-done.3.refs_7_ = bf16[4,2,128,128]{3,2,1,0:T(8,128)(2,1)S(1)} collective-permute-done((bf16[4,2,128,128]{3,2,1,0:T(8,128)(2,1)S(1)}, bf16[4,2,128,128]{3,2,1,0:T(8,128)(2,1)S(1)}, u32[]{:S(2)}, u32[]{:S(2)}) %collective-permute-start.3) | collective-permute-done | bytes 262176 | tf_op jit(solution)/shard_map/ppermute | solution.py:509
  86.8 6.2 %shard_map.72 = (f32[2,128,256]{2,1,0:T(8,128)}, bf16[8,2,128,256]{3,2,1,0:T(8,128)(2,1)}, bf16[2,2,128,128]{3,2,1,0:T(8,128)(2,1)S(1)}) custom-call(s32[35]{0:T(128)S(1)} %concatenate.10.at_ref.at, bf16[1,2,1024,1024]{3,2,1,0:T(8,128)(2,1)S(1)} %get-tuple-element.14.refs_0_, bf16[1,2,1024,1024]{3,2,1,0:T(8,128)(2,1)S(1)} %get-tuple-element.15.refs_1_, ...), custom_call_target="tpu_custom_call" | custom-call | flops 4294967296 | bytes 8388608 | tf_op jit(solution)/shard_map/pallas_call | solution.py:310
  92.9 2.7 %collective-permute-start.6 = (bf16[2,2,128,128]{3,2,1,0:T(8,128)(2,1)S(1)}, bf16[2,2,128,128]{3,2,1,0:T(8,128)(2,1)S(1)}, u32[]{:S(2)}, u32[]{:S(2)}) collective-permute-start(bf16[2,2,128,128]{3,2,1,0:T(8,128)(2,1)S(1)} %get-tuple-element.25), channel_id=1, source_target_pairs={{0,1},{1,0},{2,3},{3,2},{4,5},{5,4},{6,7},{7,6},{8,9},{9,8},{10,11... | collective-permute-start | bytes 393224 | tf_op jit(solution)/shard_map/ppermute | solution.py:530
  95.6 3.6 %all-to-all-start.2 = ((bf16[8,2,128,256]{3,2,1,0:T(8,128)(2,1)}), bf16[8,2,128,256]{3,2,1,0:T(8,128)(2,1)S(1)}, u32[]{:S(2)}, u32[]{:S(2)}) async-start(bf16[8,2,128,256]{3,2,1,0:T(8,128)(2,1)} %get-tuple-element.24), calls=%async_computation.2 | async-start | bytes 2097152 | tf_op jit(solution)/shard_map/all_to_all | solution.py:500
  99.1 0.4 collective-permute-done.6
  99.5 0.1 broadcast_select_fusion
  99.6 0.7 collective-permute-start.7
  100.3 0.0 collective-permute-done.4.second_ref
  100.3 9.8 %shard_map.73 = (f32[2,256,128]{2,1,0:T(8,128)S(1)}, f32[2,256,128]{2,1,0:T(8,128)S(1)}) custom-call(s32[35]{0:T(128)S(1)} %concatenate.10.at_ref.at, f32[2,128,256]{2,1,0:T(8,128)S(1)} %shard_map.71.refs_8_.first_ref, f32[2,128,256]{2,1,0:T(8,128)S(1)} %collective-permute-done.4.second_ref), custom_call_target="tpu_custom_call" | custom-call | flops 6000000000 | bytes 1048576 | tf_op jit(solution)/shard_map/pallas_call | solution.py:434
  110.1 0.0 collective-permute-done.7
  110.1 0.1 broadcast_select_fusion.1
  110.2 2.2 %collective-permute-start.8 = (bf16[2,2,128,128]{3,2,1,0:T(8,128)(2,1)S(1)}, bf16[2,2,128,128]{3,2,1,0:T(8,128)(2,1)S(1)}, u32[]{:S(2)}, u32[]{:S(2)}) collective-permute-start(bf16[2,2,128,128]{3,2,1,0:T(8,128)(2,1)S(1)} %broadcast_select_fusion.1), channel_id=1, source_target_pairs={{0,4},{1,5},{2,6},{3,7},{4,0},{5,1},{6,2},{7,3},{8,12},{9,13},{10,... | collective-permute-start | bytes 393224 | tf_op jit(solution)/shard_map/ppermute | solution.py:530
  112.4 0.2 all-to-all-done.2.row_ref
  112.5 0.7 pivot_tiles.1.mine_ref
  113.2 0.3 collective-permute-start.5
  113.5 0.0 copy-start
  113.5 9.9 %shard_map.74 = (f32[2,256,128]{2,1,0:T(8,128)S(1)}, f32[2,256,128]{2,1,0:T(8,128)S(1)}) custom-call(s32[35]{0:T(128)S(1)} %concatenate.10.at_ref.at, f32[2,256,128]{2,1,0:T(8,128)S(1)} %get-tuple-element.20.first_ref, f32[2,256,128]{2,1,0:T(8,128)S(1)} %get-tuple-element.21.second_ref), custom_call_target="tpu_custom_call" | custom-call | flops 6000000000 | bytes 1048576 | tf_op jit(solution)/shard_map/pallas_call | solution.py:434
  123.4 0.0 collective-permute-done.8
  123.4 0.1 broadcast_select_fusion.2.c_ref
  123.5 0.0 collective-permute-done.5.other_ref
  123.5 0.0 copy-done
  123.5 2.3 %schur.1 = f32[2,128,256]{2,1,0:T(8,128)} custom-call(s32[35]{0:T(128)S(1)} %concatenate.10.at_ref.at, f32[2,256,128]{2,1,0:T(8,128)S(1)} %get-tuple-element.22.re_ref, f32[2,256,128]{2,1,0:T(8,128)S(1)} %get-tuple-element.23.im_ref, bf16[2,2,128,256]{3,2,1,0:T(8,128)(2,1)S(1)} %pivot_tiles.1.mine_ref, ...), custom_call_target="tpu_custom_call" | custom-call | tf_op jit(solution)/shard_map/schur/pallas_call | solution.py:479
  (4 shorter events, 0.1 us)
Async XLA Ops:
  3.0 16.4 %all-to-all-start = ((bf16[16,2,64,128]{3,2,1,0:T(8,128)(2,1)}), bf16[16,2,64,128]{3,2,1,0:T(8,128)(2,1)S(1)}, u32[]{:S(2)}, u32[]{:S(2)}) async-start(bf16[16,2,64,128]{3,2,1,0:T(8,128)(2,1)} %get-tuple-element.16), calls=%async_computation | async-start | bytes 1048576 | tf_op jit(solution)/shard_map/all_to_all | solution.py:500
  44.0 34.6 %collective-permute-start = (bf16[8,4,2,64,128]{4,3,2,1,0:T(8,128)(2,1)S(1)}, bf16[8,4,2,64,128]{4,3,2,1,0:T(8,128)(2,1)S(1)}, u32[]{:S(2)}, u32[]{:S(2)}) collective-permute-start(bf16[8,4,2,64,128]{4,3,2,1,0:T(8,128)(2,1)S(1)} %all_to_all.15.refs_1_.refs_2_), channel_id=1, source_target_pairs={{0,8},{8,0},{16,24},{24,16},{32,40},{40,32},{48,56},{56,48},{64,72... | collective-permute-start | bytes 3145736 | tf_op jit(solution)/shard_map/ppermute | solution.py:520
  44.0 27.8 %collective-permute-start.1 = (bf16[1,2,128,128]{3,2,1,0:T(8,128)(2,1)S(1)}, bf16[1,2,128,128]{3,2,1,0:T(8,128)(2,1)S(1)}, u32[]{:S(2)}, u32[]{:S(2)}) collective-permute-start(bf16[1,2,128,128]{3,2,1,0:T(8,128)(2,1)S(1)} %get-tuple-element.17.refs_4_), channel_id=1, source_target_pairs={{0,1},{1,0},{2,3},{3,2},{4,5},{5,4},{6,7},{7,6},{8,9},{9,8},{10,11... | collective-permute-start | bytes 196616 | tf_op jit(solution)/shard_map/ppermute | solution.py:509
  65.7 6.8 %copy-start.1 = (s32[16]{0:T(128)S(1)}, s32[16]{0:T(128)}, u32[]{:S(2)}) copy-start(s32[16]{0:T(128)} %param.9) | copy-start | bytes 196
  71.8 5.7 %collective-permute-start.2 = (bf16[2,2,128,128]{3,2,1,0:T(8,128)(2,1)S(1)}, bf16[2,2,128,128]{3,2,1,0:T(8,128)(2,1)S(1)}, u32[]{:S(2)}, u32[]{:S(2)}) collective-permute-start(bf16[2,2,128,128]{3,2,1,0:T(8,128)(2,1)S(1)} %pad_maximum_fusion.1), channel_id=1, source_target_pairs={{0,2},{1,3},{2,0},{3,1},{4,6},{5,7},{6,4},{7,5},{8,10},{9,11},{10,... | collective-permute-start | bytes 393224 | tf_op jit(solution)/shard_map/ppermute | solution.py:509
  77.6 9.2 %collective-permute-start.3 = (bf16[4,2,128,128]{3,2,1,0:T(8,128)(2,1)S(1)}, bf16[4,2,128,128]{3,2,1,0:T(8,128)(2,1)S(1)}, u32[]{:S(2)}, u32[]{:S(2)}) collective-permute-start(bf16[4,2,128,128]{3,2,1,0:T(8,128)(2,1)S(1)} %pad_maximum_fusion), channel_id=1, source_target_pairs={{0,4},{1,5},{2,6},{3,7},{4,0},{5,1},{6,2},{7,3},{8,12},{9,13},{10,... | collective-permute-start | bytes 786440 | tf_op jit(solution)/shard_map/ppermute | solution.py:509
  83.8 16.5 %collective-permute-start.4 = (f32[2,128,256]{2,1,0:T(8,128)S(1)}, f32[2,128,256]{2,1,0:T(8,128)S(1)}, u32[]{:S(2)}, u32[]{:S(2)}) collective-permute-start(f32[2,128,256]{2,1,0:T(8,128)S(1)} %shard_map.71.refs_8_.first_ref), channel_id=1, source_target_pairs={{0,8},{8,0},{16,24},{24,16},{32,40},{40,32},{48,56},{56,48},{64,72... | collective-permute-start | bytes 786440 | tf_op jit(solution)/shard_map/ppermute | solution.py:523
  92.9 6.6 %collective-permute-start.6 = (bf16[2,2,128,128]{3,2,1,0:T(8,128)(2,1)S(1)}, bf16[2,2,128,128]{3,2,1,0:T(8,128)(2,1)S(1)}, u32[]{:S(2)}, u32[]{:S(2)}) collective-permute-start(bf16[2,2,128,128]{3,2,1,0:T(8,128)(2,1)S(1)} %get-tuple-element.25), channel_id=1, source_target_pairs={{0,1},{1,0},{2,3},{3,2},{4,5},{5,4},{6,7},{7,6},{8,9},{9,8},{10,11... | collective-permute-start | bytes 393224 | tf_op jit(solution)/shard_map/ppermute | solution.py:530
  95.6 16.9 %all-to-all-start.2 = ((bf16[8,2,128,256]{3,2,1,0:T(8,128)(2,1)}), bf16[8,2,128,256]{3,2,1,0:T(8,128)(2,1)S(1)}, u32[]{:S(2)}, u32[]{:S(2)}) async-start(bf16[8,2,128,256]{3,2,1,0:T(8,128)(2,1)} %get-tuple-element.24), calls=%async_computation.2 | async-start | bytes 2097152 | tf_op jit(solution)/shard_map/all_to_all | solution.py:500
  99.6 10.5 %collective-permute-start.7 = (bf16[2,2,128,128]{3,2,1,0:T(8,128)(2,1)S(1)}, bf16[2,2,128,128]{3,2,1,0:T(8,128)(2,1)S(1)}, u32[]{:S(2)}, u32[]{:S(2)}) collective-permute-start(bf16[2,2,128,128]{3,2,1,0:T(8,128)(2,1)S(1)} %broadcast_select_fusion), channel_id=1, source_target_pairs={{0,2},{1,3},{2,0},{3,1},{4,6},{5,7},{6,4},{7,5},{8,10},{9,11},{10,... | collective-permute-start | bytes 393224 | tf_op jit(solution)/shard_map/ppermute | solution.py:530
  110.2 13.2 %collective-permute-start.8 = (bf16[2,2,128,128]{3,2,1,0:T(8,128)(2,1)S(1)}, bf16[2,2,128,128]{3,2,1,0:T(8,128)(2,1)S(1)}, u32[]{:S(2)}, u32[]{:S(2)}) collective-permute-start(bf16[2,2,128,128]{3,2,1,0:T(8,128)(2,1)S(1)} %broadcast_select_fusion.1), channel_id=1, source_target_pairs={{0,4},{1,5},{2,6},{3,7},{4,0},{5,1},{6,2},{7,3},{8,12},{9,13},{10,... | collective-permute-start | bytes 393224 | tf_op jit(solution)/shard_map/ppermute | solution.py:530
  113.2 10.3 %collective-permute-start.5 = (bf16[2,2,128,256]{3,2,1,0:T(8,128)(2,1)S(1)}, bf16[2,2,128,256]{3,2,1,0:T(8,128)(2,1)S(1)}, u32[]{:S(2)}, u32[]{:S(2)}) collective-permute-start(bf16[2,2,128,256]{3,2,1,0:T(8,128)(2,1)S(1)} %pivot_tiles.1.mine_ref), channel_id=1, source_target_pairs={{0,8},{8,0},{16,24},{24,16},{32,40},{40,32},{48,56},{56,48},{64,72... | collective-permute-start | bytes 786440 | tf_op jit(solution)/shard_map/ppermute | solution.py:535
  113.5 10.0 %copy-start = (f32[2,128,256]{2,1,0:T(8,128)S(1)}, f32[2,128,256]{2,1,0:T(8,128)}, u32[]{:S(2)}) copy-start(f32[2,128,256]{2,1,0:T(8,128)} %get-tuple-element.12.r_ref) | copy-start | bytes 786436

commit v7 on v6

--- a/solution.py
+++ b/solution.py
@@ -330,7 +330,7 @@
 
 
 WIDE = 128
-PANEL = 32
+PANEL = 64
 
 
 def small_exchange(ar, ai, sub):
@@ -347,9 +347,8 @@
                 xr, xi = br * qr + bi * qi, bi * qr - br * qi
             else:
                 cr, ci = row(ar[m]), row(ai[m])
-                wr, wi = br * cr - bi * ci, br * ci + bi * cr
                 vr, vi = cr * qr + ci * qi, ci * qr - cr * qi
-                xr, xi = ar[m] - (wr * qr + wi * qi), ai[m] - (wi * qr - wr * qi)
+                xr, xi = ar[m] - (br * vr - bi * vi), ai[m] - (br * vi + bi * vr)
             ar[m], ai[m] = jnp.where(sub == s, -vr, xr), jnp.where(sub == s, -vi, xi)
     return ar, ai
 
@@ -450,40 +449,60 @@
     return hi, mid, low
 
 
-def schur_kernel(blocks, at, re_ref, im_ref, mine_ref, other_ref, c_ref, r_ref, out_ref):
+def real_form(re, im):
+    return jnp.concatenate([jnp.concatenate([re, im], 1), jnp.concatenate([-im, re], 1)], 0)
+
+
+def column_kernel(re_ref, im_ref, c_ref, x_ref):
+    left = jnp.concatenate([c_ref[0, 0], c_ref[1, 0], c_ref[0, 1], c_ref[1, 1]], 1)
+    re = split3(jnp.concatenate([re_ref[0], re_ref[1]], 1))
+    im = split3(jnp.concatenate([im_ref[0], im_ref[1]], 1))
+    x = jnp.zeros(x_ref.shape, f32)
+    for r, i in zip(re, im):
+        x += jnp.dot(left, real_form(r, i), preferred_element_type=f32)
+    x_ref[...] = x
+
+
+def pivot_columns(re, im, column):
+    rows = column.shape[2]
+    return pl.pallas_call(
+        column_kernel,
+        out_shape=jax.ShapeDtypeStruct((rows, 2 * PANELS * WIDE), f32),
+        in_specs=[VMEM] * 3,
+        out_specs=VMEM,
+        compiler_params=pltpu.CompilerParams(vmem_limit_bytes=12 * MB),
+        cost_estimate=pl.CostEstimate(flops=int(2e9), transcendentals=0, bytes_accessed=1 << 20),
+        name="pivot_columns",
+    )(re, im, column)
+
+
+def schur_kernel(blocks, at, x_ref, mine_ref, other_ref, r_ref, out_ref):
     core = at[2]
-    funcs = mine_ref.shape[2]
     b = []
     for p in range(PANELS):
         local = slot_with(at, at[3 + blocks + p], blocks) % 2 == core
         b.append([jnp.where(local, mine_ref[p, k].astype(f32), other_ref[p, k].astype(f32)).astype(bf16) for k in range(2)])
     br = jnp.concatenate([b[p][0] for p in range(PANELS)], 0)
     bi = jnp.concatenate([b[p][1] for p in range(PANELS)], 0)
-    right = jnp.concatenate([jnp.concatenate([br, bi], 1), jnp.concatenate([-bi, br], 1)], 0)
-    w = jnp.zeros((PANELS * funcs, right.shape[1]), f32)
-    for x in split3(jnp.concatenate([re_ref[0], re_ref[1], im_ref[0], im_ref[1]], 1)):
-        w += jnp.dot(x, right, preferred_element_type=f32)
-    cols = w.shape[1] // 2
-    w_hi = w.astype(bf16)
-    w_lo = (w - w_hi.astype(f32)).astype(bf16)
-    cr = jnp.concatenate([c_ref[0, 0], c_ref[1, 0]], 1)
-    ci = jnp.concatenate([c_ref[0, 1], c_ref[1, 1]], 1)
-    left = jnp.concatenate([cr, ci], 0)
-    prod = jnp.dot(left, w_hi, preferred_element_type=f32) + jnp.dot(left, w_lo, preferred_element_type=f32)
-    rows = cr.shape[0]
-    out_ref[0] = r_ref[0] - (prod[:rows, :cols] - prod[rows:, cols:])
-    out_ref[1] = r_ref[1] - (prod[:rows, cols:] + prod[rows:, :cols])
-
-
-def schur_tile(at, blocks, re, im, mine, other, column, reduced):
+    right = real_form(br, bi)
+    x = x_ref[...]
+    x_hi = x.astype(bf16)
+    x_lo = (x - x_hi.astype(f32)).astype(bf16)
+    prod = jnp.dot(x_hi, right, preferred_element_type=f32) + jnp.dot(x_lo, right, preferred_element_type=f32)
+    cols = prod.shape[1] // 2
+    out_ref[0] = r_ref[0] - prod[:, :cols]
+    out_ref[1] = r_ref[1] - prod[:, cols:]
+
+
+def schur_tile(at, blocks, x, mine, other, reduced):
     return pl.pallas_call(
         functools.partial(schur_kernel, blocks),
         out_shape=jax.ShapeDtypeStruct(reduced.shape, f32),
-        in_specs=[SMEM] + [VMEM] * 6,
+        in_specs=[SMEM] + [VMEM] * 4,
         out_specs=VMEM,
         compiler_params=pltpu.CompilerParams(vmem_limit_bytes=12 * MB),
         name="schur",
-    )(at, re, im, mine, other, column, reduced)
+    )(at, x, mine, other, reduced)
 
 
 def on_device(inverse, excite, coordinates, block_of_slot, panel_order):
@@ -535,7 +554,8 @@
     row_other = lax.ppermute(row_mine, "blk", swap)
     re, im = pivot_exchange(0, at, pivot_rows, pivot_other)
     re, im = pivot_exchange(1, at, re, im)
-    schur = schur_tile(at, blocks, re, im, row_mine, row_other, column, reduced)
+    x = pivot_columns(re, im, column)
+    schur = schur_tile(at, blocks, x, row_mine, row_other, reduced)
     return (reduced, schur)
 
 

time: 128 us -> 126 us (0.984)
  Pallas kernels: 64 us -> 61.5 us
    pallas_call x2, Pallas kernels: 19.7 us -> 17.5 us  [pivot_exchange(): pl.pallas_call(functools.partial(inverse_kernel, kb), out_shape=(part, pa...]
  transfers between devices with their start and end apart: 11 -> 11, of which waited for: 5 -> 5; matrix products, arithmetic and copies ran while one was open for 1% -> 1% of each run, Pallas kernels for 47% -> 46%
where the time goes in v7:
time: 126 us; the launch traced here: 124 us
  Pallas kernels  61.5 us (49%)
  blocking collectives  23.9 us (19%)
  waiting for transfers between devices  19.4 us (15%)
  starting transfers between devices  17.5 us (14%)
    pallas_call x3, Pallas kernels, green_tiles(): pl.pallas_call(functools.partial(green_kernel, first, whole, len(carry)),...  26.9 us
    all_to_all x1, blocking collectives, spread(): lax.all_to_all(x, axis, split_axis=0, concat_axis=0, tiled=True, axis_ind...  23.9 us
    pallas_call x2, Pallas kernels, pivot_exchange(): pl.pallas_call(functools.partial(inverse_kernel, kb), out_shape=(part, pa...  17.5 us
    pallas_call x2, Pallas kernels, couplings(): pl.pallas_call(functools.partial(coupling_kernel, pivot, 3 + blocks, len(...  11.4 us
    all_to_all x2, waiting for transfers between devices, spread(): lax.all_to_all(x, axis, split_axis=0, concat_axis=0, tiled=True, axis_ind...  10.1 us
    all_to_all x2, starting transfers between devices, spread(): lax.all_to_all(x, axis, split_axis=0, concat_axis=0, tiled=True, axis_ind...  9.17 us
    ppermute x3, waiting for transfers between devices, on_device(): lax.ppermute(held, 'grp', [(g, g ^ bit) for g in range(grp_size)])  7.95 us
    ppermute x3, starting transfers between devices, on_device(): came = lax.ppermute(column, 'grp', [(g, g ^ bit) for g in range(grp_size)])  5.71 us
  transfers between devices with their start and end apart: 11, of which 5 were waited for; matrix products, arithmetic and copies ran while one was open for 1% of the time, Pallas kernels for 46%

profile of v7, /device:TPU:0, one launch (start us, length us, event | category | flops | bytes accessed | tf_op | source)
XLA Modules:
  0.0 124.2 jit_solution(11706151426023619894)
XLA Ops:
  0.6 2.3 %basis.1 = (bf16[1,2,128,128]{3,2,1,0:T(8,128)(2,1)S(1)}, bf16[16,2,64,128]{3,2,1,0:T(8,128)(2,1)}) custom-call(bf16[2,1,128,1024]{3,2,1,0:T(8,128)(2,1)} %inv_ref.1, bf16[2,1,1024,128]{3,2,1,0:T(8,128)(2,1)} %exc_ref.1), custom_call_target="tpu_custom_call" | custom-call | tf_op jit(solution)/shard_map/basis/pallas_call | solution.py:62
  3.0 5.6 %all-to-all-start = ((bf16[16,2,64,128]{3,2,1,0:T(8,128)(2,1)}), bf16[16,2,64,128]{3,2,1,0:T(8,128)(2,1)S(1)}, u32[]{:S(2)}, u32[]{:S(2)}) async-start(bf16[16,2,64,128]{3,2,1,0:T(8,128)(2,1)} %get-tuple-element.16), calls=%async_computation | async-start | bytes 1048576 | tf_op jit(solution)/shard_map/all_to_all | solution.py:519
  8.6 0.7 concatenate.10.at_ref.at
  9.4 10.1 %all-to-all-done.rows_ref = bf16[16,2,64,128]{3,2,1,0:T(8,128)(2,1)S(1)} async-done(((bf16[16,2,64,128]{3,2,1,0:T(8,128)(2,1)}), bf16[16,2,64,128]{3,2,1,0:T(8,128)(2,1)S(1)}, u32[]{:S(2)}, u32[]{:S(2)}) %all-to-all-start) | async-done | bytes 524320 | tf_op jit(solution)/shard_map/all_to_all | solution.py:519
  19.4 0.7 gathered.1
  20.1 23.9 %all_to_all.15.refs_1_.refs_2_ = bf16[8,4,2,64,128]{4,3,2,1,0:T(8,128)(2,1)S(1)} all-to-all(bf16[8,4,2,64,128]{4,3,2,1,0:T(8,128)(2,1)S(1)} %gathered.1), channel_id=1, replica_groups=mesh['blk'=16,'grp'=8] {'grp'}, dimensions={0} | all-to-all | bytes 2097152 | tf_op jit(solution)/shard_map/all_to_all | solution.py:519
  44.0 0.0 collective-permute-start
  44.0 0.9 collective-permute-start.1
  44.8 7.6 %shard_map.68.refs_0_ = bf16[1,2,1024,1024]{3,2,1,0:T(8,128)(2,1)} custom-call(s32[35]{0:T(128)S(1)} %concatenate.10.at_ref.at, s32[3,16,1024]{2,1,0:T(8,128)} %coords_ref.5), custom_call_target="tpu_custom_call" | custom-call | flops 31457280 | bytes 4194304 | tf_op jit(solution)/shard_map/pallas_call | solution.py:194
  52.4 13.3 %shard_map.69.refs_1_ = bf16[2,2,1024,1024]{3,2,1,0:T(8,128)(2,1)} custom-call(s32[35]{0:T(128)S(1)} %concatenate.10.at_ref.at, s32[3,16,1024]{2,1,0:T(8,128)} %coords_ref.5), custom_call_target="tpu_custom_call" | custom-call | flops 62914560 | bytes 8388608 | tf_op jit(solution)/shard_map/pallas_call | solution.py:194
  65.7 0.0 copy-start.1
  65.7 6.1 %shard_map.70 = (bf16[1,2,1024,1024]{3,2,1,0:T(8,128)(2,1)S(1)}, bf16[1,2,1024,1024]{3,2,1,0:T(8,128)(2,1)S(1)}, bf16[2,2,1024,1024]{3,2,1,0:T(8,128)(2,1)S(1)}) custom-call(s32[35]{0:T(128)S(1)} %concatenate.10.at_ref.at, s32[3,16,1024]{2,1,0:T(8,128)} %coords_ref.5, bf16[1,2,1024,1024]{3,2,1,0:T(8,128)(2,1)} %shard_map.68.refs_0_, ...), custom_call_target="tpu_custom_call" | custom-call | flops 31457280 | bytes 4194304 | tf_op jit(solution)/shard_map/pallas_call | solution.py:194
  71.8 0.0 collective-permute-done.1.refs_5_
  71.8 0.6 collective-permute-start.2
  72.5 0.0 copy-done.1
  72.5 5.0 %collective-permute-done.2.refs_6_ = bf16[2,2,128,128]{3,2,1,0:T(8,128)(2,1)S(1)} collective-permute-done((bf16[2,2,128,128]{3,2,1,0:T(8,128)(2,1)S(1)}, bf16[2,2,128,128]{3,2,1,0:T(8,128)(2,1)S(1)}, u32[]{:S(2)}, u32[]{:S(2)}) %collective-permute-start.2) | collective-permute-done | bytes 131104 | tf_op jit(solution)/shard_map/ppermute | solution.py:528
  77.6 1.0 collective-permute-start.3
  78.6 0.0 collective-permute-done.refs_2_.refs_3_
  78.6 5.2 %shard_map.71.refs_8_.first_ref = f32[2,128,256]{2,1,0:T(8,128)S(1)} custom-call(s32[35]{0:T(128)S(1)} %concatenate.10.at_ref.at, bf16[2,2,1024,1024]{3,2,1,0:T(8,128)(2,1)S(1)} %get-tuple-element.18.refs_0_, bf16[8,4,2,64,128]{4,3,2,1,0:T(8,128)(2,1)S(1)} %all_to_all.15.refs_1_.refs_2_, bf16[8,4,2,64,128]{4,3,2,1,0:T(8,128)(2,1)S(1)} %collective-permute-done.refs_2_.refs_3_), custom_call_target="tpu_custom_call" | custom-call | flops 4294967296 | bytes 8388608 | tf_op jit(solution)/shard_map/pallas_call | solution.py:310
  83.8 0.1 collective-permute-start.4
  83.9 2.9 %collective-permute-done.3.refs_7_ = bf16[4,2,128,128]{3,2,1,0:T(8,128)(2,1)S(1)} collective-permute-done((bf16[4,2,128,128]{3,2,1,0:T(8,128)(2,1)S(1)}, bf16[4,2,128,128]{3,2,1,0:T(8,128)(2,1)S(1)}, u32[]{:S(2)}, u32[]{:S(2)}) %collective-permute-start.3) | collective-permute-done | bytes 262176 | tf_op jit(solution)/shard_map/ppermute | solution.py:528
  86.8 6.2 %shard_map.72 = (f32[2,128,256]{2,1,0:T(8,128)}, bf16[8,2,128,256]{3,2,1,0:T(8,128)(2,1)}, bf16[2,2,128,128]{3,2,1,0:T(8,128)(2,1)S(1)}) custom-call(s32[35]{0:T(128)S(1)} %concatenate.10.at_ref.at, bf16[1,2,1024,1024]{3,2,1,0:T(8,128)(2,1)S(1)} %get-tuple-element.14.refs_0_, bf16[1,2,1024,1024]{3,2,1,0:T(8,128)(2,1)S(1)} %get-tuple-element.15.refs_1_, ...), custom_call_target="tpu_custom_call" | custom-call | flops 4294967296 | bytes 8388608 | tf_op jit(solution)/shard_map/pallas_call | solution.py:310
  92.9 2.7 %collective-permute-start.5 = (bf16[2,2,128,128]{3,2,1,0:T(8,128)(2,1)S(1)}, bf16[2,2,128,128]{3,2,1,0:T(8,128)(2,1)S(1)}, u32[]{:S(2)}, u32[]{:S(2)}) collective-permute-start(bf16[2,2,128,128]{3,2,1,0:T(8,128)(2,1)S(1)} %get-tuple-element.24), channel_id=1, source_target_pairs={{0,1},{1,0},{2,3},{3,2},{4,5},{5,4},{6,7},{7,6},{8,9},{9,8},{10,11... | collective-permute-start | bytes 393224 | tf_op jit(solution)/shard_map/ppermute | solution.py:549
  95.6 3.6 %all-to-all-start.2 = ((bf16[8,2,128,256]{3,2,1,0:T(8,128)(2,1)}), bf16[8,2,128,256]{3,2,1,0:T(8,128)(2,1)S(1)}, u32[]{:S(2)}, u32[]{:S(2)}) async-start(bf16[8,2,128,256]{3,2,1,0:T(8,128)(2,1)} %get-tuple-element.25), calls=%async_computation.2 | async-start | bytes 2097152 | tf_op jit(solution)/shard_map/all_to_all | solution.py:519
  99.1 0.4 collective-permute-done.5
  99.5 0.1 broadcast_select_fusion
  99.6 0.7 collective-permute-start.6
  100.3 0.0 collective-permute-done.4.second_ref
  100.3 8.7 %shard_map.73 = (f32[2,256,128]{2,1,0:T(8,128)S(1)}, f32[2,256,128]{2,1,0:T(8,128)S(1)}) custom-call(s32[35]{0:T(128)S(1)} %concatenate.10.at_ref.at, f32[2,128,256]{2,1,0:T(8,128)S(1)} %shard_map.71.refs_8_.first_ref, f32[2,128,256]{2,1,0:T(8,128)S(1)} %collective-permute-done.4.second_ref), custom_call_target="tpu_custom_call" | custom-call | flops 6000000000 | bytes 1048576 | tf_op jit(solution)/shard_map/pallas_call | solution.py:433
  109.0 0.0 collective-permute-done.6
  109.0 0.1 broadcast_select_fusion.1
  109.1 2.4 %collective-permute-start.7 = (bf16[2,2,128,128]{3,2,1,0:T(8,128)(2,1)S(1)}, bf16[2,2,128,128]{3,2,1,0:T(8,128)(2,1)S(1)}, u32[]{:S(2)}, u32[]{:S(2)}) collective-permute-start(bf16[2,2,128,128]{3,2,1,0:T(8,128)(2,1)S(1)} %broadcast_select_fusion.1), channel_id=1, source_target_pairs={{0,4},{1,5},{2,6},{3,7},{4,0},{5,1},{6,2},{7,3},{8,12},{9,13},{10,... | collective-permute-start | bytes 393224 | tf_op jit(solution)/shard_map/ppermute | solution.py:549
  111.5 8.8 %shard_map.74 = (f32[2,256,128]{2,1,0:T(8,128)S(1)}, f32[2,256,128]{2,1,0:T(8,128)S(1)}) custom-call(s32[35]{0:T(128)S(1)} %concatenate.10.at_ref.at, f32[2,256,128]{2,1,0:T(8,128)S(1)} %get-tuple-element.20.first_ref, f32[2,256,128]{2,1,0:T(8,128)S(1)} %get-tuple-element.21.second_ref), custom_call_target="tpu_custom_call" | custom-call | flops 6000000000 | bytes 1048576 | tf_op jit(solution)/shard_map/pallas_call | solution.py:433
  120.3 0.0 all-to-all-done.2.row_ref
  120.3 0.7 pivot_tiles.1.mine_ref
  120.9 0.0 copy-start
  121.0 0.1 collective-permute-start.8
  121.1 0.0 collective-permute-done.7
  121.1 0.1 broadcast_select_fusion.2.c_ref
  121.2 0.4 pivot_columns.1.x_ref
  121.6 1.0 collective-permute-done.8.other_ref
  122.6 0.0 copy-done
  122.6 1.6 %schur.1 = f32[2,128,256]{2,1,0:T(8,128)} custom-call(s32[35]{0:T(128)S(1)} %concatenate.10.at_ref.at, f32[128,512]{1,0:T(8,128)S(1)} %pivot_columns.1.x_ref, bf16[2,2,128,256]{3,2,1,0:T(8,128)(2,1)S(1)} %pivot_tiles.1.mine_ref, bf16[2,2,128,256]{3,2,1,0:T(8,128)(2,1)S(1)} %collective-permute-done.8.other_ref, f32[2,128,256]{2,1,0:T(8,128)S(1)} %copy-done), custom_call_target="tpu_custom_call" | custom-call | tf_op jit(solution)/shard_map/schur/pallas_call | solution.py:498
  (4 shorter events, 0.1 us)
Async XLA Ops:
  3.0 16.4 %all-to-all-start = ((bf16[16,2,64,128]{3,2,1,0:T(8,128)(2,1)}), bf16[16,2,64,128]{3,2,1,0:T(8,128)(2,1)S(1)}, u32[]{:S(2)}, u32[]{:S(2)}) async-start(bf16[16,2,64,128]{3,2,1,0:T(8,128)(2,1)} %get-tuple-element.16), calls=%async_computation | async-start | bytes 1048576 | tf_op jit(solution)/shard_map/all_to_all | solution.py:519
  44.0 34.6 %collective-permute-start = (bf16[8,4,2,64,128]{4,3,2,1,0:T(8,128)(2,1)S(1)}, bf16[8,4,2,64,128]{4,3,2,1,0:T(8,128)(2,1)S(1)}, u32[]{:S(2)}, u32[]{:S(2)}) collective-permute-start(bf16[8,4,2,64,128]{4,3,2,1,0:T(8,128)(2,1)S(1)} %all_to_all.15.refs_1_.refs_2_), channel_id=1, source_target_pairs={{0,8},{8,0},{16,24},{24,16},{32,40},{40,32},{48,56},{56,48},{64,72... | collective-permute-start | bytes 3145736 | tf_op jit(solution)/shard_map/ppermute | solution.py:539
  44.0 27.8 %collective-permute-start.1 = (bf16[1,2,128,128]{3,2,1,0:T(8,128)(2,1)S(1)}, bf16[1,2,128,128]{3,2,1,0:T(8,128)(2,1)S(1)}, u32[]{:S(2)}, u32[]{:S(2)}) collective-permute-start(bf16[1,2,128,128]{3,2,1,0:T(8,128)(2,1)S(1)} %get-tuple-element.17.refs_4_), channel_id=1, source_target_pairs={{0,1},{1,0},{2,3},{3,2},{4,5},{5,4},{6,7},{7,6},{8,9},{9,8},{10,11... | collective-permute-start | bytes 196616 | tf_op jit(solution)/shard_map/ppermute | solution.py:528
  65.7 6.8 %copy-start.1 = (s32[16]{0:T(128)S(1)}, s32[16]{0:T(128)}, u32[]{:S(2)}) copy-start(s32[16]{0:T(128)} %param.9) | copy-start | bytes 196
  71.8 5.7 %collective-permute-start.2 = (bf16[2,2,128,128]{3,2,1,0:T(8,128)(2,1)S(1)}, bf16[2,2,128,128]{3,2,1,0:T(8,128)(2,1)S(1)}, u32[]{:S(2)}, u32[]{:S(2)}) collective-permute-start(bf16[2,2,128,128]{3,2,1,0:T(8,128)(2,1)S(1)} %pad_maximum_fusion.1), channel_id=1, source_target_pairs={{0,2},{1,3},{2,0},{3,1},{4,6},{5,7},{6,4},{7,5},{8,10},{9,11},{10,... | collective-permute-start | bytes 393224 | tf_op jit(solution)/shard_map/ppermute | solution.py:528
  77.6 9.2 %collective-permute-start.3 = (bf16[4,2,128,128]{3,2,1,0:T(8,128)(2,1)S(1)}, bf16[4,2,128,128]{3,2,1,0:T(8,128)(2,1)S(1)}, u32[]{:S(2)}, u32[]{:S(2)}) collective-permute-start(bf16[4,2,128,128]{3,2,1,0:T(8,128)(2,1)S(1)} %pad_maximum_fusion), channel_id=1, source_target_pairs={{0,4},{1,5},{2,6},{3,7},{4,0},{5,1},{6,2},{7,3},{8,12},{9,13},{10,... | collective-permute-start | bytes 786440 | tf_op jit(solution)/shard_map/ppermute | solution.py:528
  83.8 16.5 %collective-permute-start.4 = (f32[2,128,256]{2,1,0:T(8,128)S(1)}, f32[2,128,256]{2,1,0:T(8,128)S(1)}, u32[]{:S(2)}, u32[]{:S(2)}) collective-permute-start(f32[2,128,256]{2,1,0:T(8,128)S(1)} %shard_map.71.refs_8_.first_ref), channel_id=1, source_target_pairs={{0,8},{8,0},{16,24},{24,16},{32,40},{40,32},{48,56},{56,48},{64,72... | collective-permute-start | bytes 786440 | tf_op jit(solution)/shard_map/ppermute | solution.py:542
  92.9 6.6 %collective-permute-start.5 = (bf16[2,2,128,128]{3,2,1,0:T(8,128)(2,1)S(1)}, bf16[2,2,128,128]{3,2,1,0:T(8,128)(2,1)S(1)}, u32[]{:S(2)}, u32[]{:S(2)}) collective-permute-start(bf16[2,2,128,128]{3,2,1,0:T(8,128)(2,1)S(1)} %get-tuple-element.24), channel_id=1, source_target_pairs={{0,1},{1,0},{2,3},{3,2},{4,5},{5,4},{6,7},{7,6},{8,9},{9,8},{10,11... | collective-permute-start | bytes 393224 | tf_op jit(solution)/shard_map/ppermute | solution.py:549
  95.6 24.7 %all-to-all-start.2 = ((bf16[8,2,128,256]{3,2,1,0:T(8,128)(2,1)}), bf16[8,2,128,256]{3,2,1,0:T(8,128)(2,1)S(1)}, u32[]{:S(2)}, u32[]{:S(2)}) async-start(bf16[8,2,128,256]{3,2,1,0:T(8,128)(2,1)} %get-tuple-element.25), calls=%async_computation.2 | async-start | bytes 2097152 | tf_op jit(solution)/shard_map/all_to_all | solution.py:519
  99.6 9.4 %collective-permute-start.6 = (bf16[2,2,128,128]{3,2,1,0:T(8,128)(2,1)S(1)}, bf16[2,2,128,128]{3,2,1,0:T(8,128)(2,1)S(1)}, u32[]{:S(2)}, u32[]{:S(2)}) collective-permute-start(bf16[2,2,128,128]{3,2,1,0:T(8,128)(2,1)S(1)} %broadcast_select_fusion), channel_id=1, source_target_pairs={{0,2},{1,3},{2,0},{3,1},{4,6},{5,7},{6,4},{7,5},{8,10},{9,11},{10,... | collective-permute-start | bytes 393224 | tf_op jit(solution)/shard_map/ppermute | solution.py:549
  109.1 12.0 %collective-permute-start.7 = (bf16[2,2,128,128]{3,2,1,0:T(8,128)(2,1)S(1)}, bf16[2,2,128,128]{3,2,1,0:T(8,128)(2,1)S(1)}, u32[]{:S(2)}, u32[]{:S(2)}) collective-permute-start(bf16[2,2,128,128]{3,2,1,0:T(8,128)(2,1)S(1)} %broadcast_select_fusion.1), channel_id=1, source_target_pairs={{0,4},{1,5},{2,6},{3,7},{4,0},{5,1},{6,2},{7,3},{8,12},{9,13},{10,... | collective-permute-start | bytes 393224 | tf_op jit(solution)/shard_map/ppermute | solution.py:549
  120.9 1.6 %copy-start = (f32[2,128,256]{2,1,0:T(8,128)S(1)}, f32[2,128,256]{2,1,0:T(8,128)}, u32[]{:S(2)}) copy-start(f32[2,128,256]{2,1,0:T(8,128)} %get-tuple-element.12.r_ref) | copy-start | bytes 786436
  121.0 1.6 %collective-permute-start.8 = (bf16[2,2,128,256]{3,2,1,0:T(8,128)(2,1)S(1)}, bf16[2,2,128,256]{3,2,1,0:T(8,128)(2,1)S(1)}, u32[]{:S(2)}, u32[]{:S(2)}) collective-permute-start(bf16[2,2,128,256]{3,2,1,0:T(8,128)(2,1)S(1)} %pivot_tiles.1.mine_ref), channel_id=1, source_target_pairs={{0,8},{8,0},{16,24},{24,16},{32,40},{40,32},{48,56},{56,48},{64,72... | collective-permute-start | bytes 786440 | tf_op jit(solution)/shard_map/ppermute | solution.py:554

commit v8 on v7

--- a/solution.py
+++ b/solution.py
@@ -80,28 +80,31 @@
     return slot
 
 
-def gather_kernel(at_ref, rows_ref, out_ref, slot_ref):
+def gather_kernel(at_ref, rows_ref, out_ref, slot_ref, sems):
     blocks = rows_ref.shape[0]
     for s in range(blocks):
         slot_ref[at_ref[3 + s]] = s
     groups, entries = out_ref.shape[:2]
     slabs = entries - PANELS
-    for p in range(PANELS):
-        value = rows_ref[slot_ref[at_ref[3 + blocks + p]]]
-        for g in range(groups):
-            out_ref[g, slabs + p] = value
+    copies = []
     for g in range(groups):
-        for e in range(slabs):
-            out_ref[g, e] = rows_ref[slot_ref[g * slabs + e]]
+        for e in range(entries):
+            block = g * slabs + e if e < slabs else at_ref[3 + blocks + e - slabs]
+            copy = pltpu.make_async_copy(rows_ref.at[slot_ref[block]], out_ref.at[g, e], sems.at[g, e])
+            copy.start()
+            copies.append(copy)
+    for copy in copies:
+        copy.wait()
 
 
 def gathered(at, rows, groups, slabs):
+    entries = slabs + PANELS
     return pl.pallas_call(
         gather_kernel,
-        out_shape=jax.ShapeDtypeStruct((groups, slabs + PANELS, *rows.shape[1:]), rows.dtype),
+        out_shape=pltpu.HBM((groups, entries, *rows.shape[1:]), rows.dtype),
         in_specs=[SMEM, VMEM],
-        out_specs=VMEM,
-        scratch_shapes=[pltpu.SMEM((rows.shape[0],), i32)],
+        out_specs=pl.BlockSpec(memory_space=pltpu.HBM),
+        scratch_shapes=[pltpu.SMEM((rows.shape[0],), i32), pltpu.SemaphoreType.DMA((groups, entries))],
         compiler_params=pltpu.CompilerParams(vmem_limit_bytes=8 * MB),
         name="gathered",
     )(at, rows)
@@ -213,14 +216,15 @@
     acc[...] += jnp.dot(left, y_hi, preferred_element_type=f32) + jnp.dot(left, y_lo, preferred_element_type=f32)
 
 
-def coupling_kernel(pivot, panel_at, greens, at_ref, *refs):
+def coupling_kernel(pivot, panel_at, greens, bits, at_ref, *refs):
     g_refs, refs = refs[:greens], refs[greens:]
     mine_ref, other_ref, refs = refs[0], refs[1], refs[2:]
     if pivot:
         out_ref, lhs, stage, top, bottom, acc = refs
     else:
-        pieces = refs[:4]
-        out_ref, copies_ref, column_ref, lhs, stage, top, bottom, acc = refs[5:]
+        count = 1 + len(bits)
+        pieces = refs[:count]
+        out_ref, copies_ref, column_ref, lhs, stage, top, bottom, acc = refs[count + 1 :]
     tile, chunk = pl.program_id(0), pl.program_id(1)
     chunks = pl.num_programs(1)
     grp, core = at_ref[1], at_ref[2]
@@ -241,13 +245,14 @@
                     stage[r, :cols] = src[g, first + core, 0]
                     stage[r, cols:] = src[g, first + core, 1]
         else:
-            step = 0
+            away = [0]
+            for bit in bits:
+                away = away + [d ^ bit for d in away]
             for piece in pieces:
                 for k in range(piece.shape[0]):
-                    r = pl.ds(pl.multiple_of((grp ^ step) * 2 * half, 2 * half), 2 * half)
+                    r = pl.ds(pl.multiple_of((grp ^ away.pop(0)) * 2 * half, 2 * half), 2 * half)
                     stage[r, :cols] = piece[k, 0]
                     stage[r, cols:] = piece[k, 1]
-                    step += 1
         lhs[...] = stage[...].T
 
     @pl.when(chunk == 0)
@@ -293,7 +298,7 @@
                         column_ref[p, part] = value.astype(bf16)
 
 
-def couplings(at, blocks, greens, mine, other, pieces, after, pivot):
+def couplings(at, blocks, greens, mine, other, pieces, bits, after, pivot):
     unk = greens[0].shape[2]
     cols = mine.shape[4]
     tiles = 2
@@ -308,7 +313,7 @@
         out_shape.append(jax.ShapeDtypeStruct((PANELS, 2, cols, cols), bf16))
         out_specs.append(pl.BlockSpec((PANELS, 2, cols, cols), lambda t, m: (0, 0, 0, 0)))
     return pl.pallas_call(
-        functools.partial(coupling_kernel, pivot, 3 + blocks, len(greens)),
+        functools.partial(coupling_kernel, pivot, 3 + blocks, len(greens), bits),
         out_shape=out_shape,
         grid=(tiles, unk // rows),
         in_specs=[SMEM] + [VMEM] * len(greens)
@@ -523,11 +528,11 @@
     own, halves = basis_rows(inverse, excite, blk_size)
     sliced = spread(halves, "blk")
 
-    pieces, held, bit = [own], own, 1
-    while bit < grp_size:
+    bits = [1] + [1 << k for k in range(grp_size.bit_length() - 2, 0, -1)]
+    pieces, held = [own], own
+    for n, bit in enumerate(bits):
         pieces.append(lax.ppermute(held, "grp", [(g, g ^ bit) for g in range(grp_size)]))
-        bit *= 2
-        if bit < grp_size:
+        if n + 1 < len(bits):
             held = jnp.concatenate([held, pieces[-1]], 0)
 
     (green_first,) = green_tiles(at, coordinates, 0, 1, False)
@@ -538,18 +543,16 @@
     mine = spread(picked, "grp")
     other = lax.ppermute(mine, "blk", swap)
 
-    (pivot_rows,) = couplings(at, blocks, [green_pivot], mine, other, [], [], True)
+    (pivot_rows,) = couplings(at, blocks, [green_pivot], mine, other, [], [], [], True)
     pivot_other = lax.ppermute(pivot_rows, "blk", swap)
-    reduced, copies, column = couplings(at, blocks, [green_first, green_second], mine, other, pieces, [pivot_rows], False)
+    reduced, copies, column = couplings(at, blocks, [green_first, green_second], mine, other, pieces, bits, [pivot_rows], False)
 
     rows = spread(copies, "blk", same_core)
     column_at = pivots // slabs
-    bit = 1
-    while bit < grp_size:
+    for bit in bits:
         came = lax.ppermute(column, "grp", [(g, g ^ bit) for g in range(grp_size)])
         take = ((grp ^ column_at) & bit) != 0
         column = jnp.where(take[:, None, None, None], came, column)
-        bit *= 2
     row_mine = pivot_tiles(at, rows, blocks)
     row_other = lax.ppermute(row_mine, "blk", swap)
     re, im = pivot_exchange(0, at, pivot_rows, pivot_other)

time: 126 us -> 126 us (level)
  transfers between devices with their start and end apart: 11 -> 11, of which waited for: 5 -> 5; matrix products, arithmetic and copies ran while one was open for 1% -> 1% of each run, Pallas kernels for 46% -> 45%
where the time goes in v8:
time: 126 us; the launch traced here: 125 us
  Pallas kernels  62.7 us (50%)
  blocking collectives  24.1 us (19%)
  waiting for transfers between devices  19.6 us (16%)
  starting transfers between devices  16.8 us (13%)
    pallas_call x3, Pallas kernels, green_tiles(): pl.pallas_call(functools.partial(green_kernel, first, whole, len(carry)),...  27 us
    all_to_all x1, blocking collectives, spread(): lax.all_to_all(x, axis, split_axis=0, concat_axis=0, tiled=True, axis_ind...  24.1 us
    pallas_call x2, Pallas kernels, pivot_exchange(): pl.pallas_call(functools.partial(inverse_kernel, kb), out_shape=(part, pa...  17.5 us
    pallas_call x2, Pallas kernels, couplings(): pl.pallas_call(functools.partial(coupling_kernel, pivot, 3 + blocks, len(...  11.4 us
    all_to_all x2, waiting for transfers between devices, spread(): lax.all_to_all(x, axis, split_axis=0, concat_axis=0, tiled=True, axis_ind...  10.1 us
    all_to_all x2, starting transfers between devices, spread(): lax.all_to_all(x, axis, split_axis=0, concat_axis=0, tiled=True, axis_ind...  9.17 us
    ppermute x3, waiting for transfers between devices, on_device(): lax.ppermute(held, 'grp', [(g, g ^ bit) for g in range(grp_size)])  8.27 us
    ppermute x3, starting transfers between devices, on_device(): came = lax.ppermute(column, 'grp', [(g, g ^ bit) for g in range(grp_size)])  5.32 us
  transfers between devices with their start and end apart: 11, of which 5 were waited for; matrix products, arithmetic and copies ran while one was open for 1% of the time, Pallas kernels for 45%

profile of v8, /device:TPU:0, one launch (start us, length us, event | category | flops | bytes accessed | tf_op | source)
XLA Modules:
  0.0 125.1 jit_solution(12585312147122130091)
XLA Ops:
  0.6 2.3 %basis.1 = (bf16[1,2,128,128]{3,2,1,0:T(8,128)(2,1)S(1)}, bf16[16,2,64,128]{3,2,1,0:T(8,128)(2,1)}) custom-call(bf16[2,1,128,1024]{3,2,1,0:T(8,128)(2,1)} %inv_ref.1, bf16[2,1,1024,128]{3,2,1,0:T(8,128)(2,1)} %exc_ref.1), custom_call_target="tpu_custom_call" | custom-call | tf_op jit(solution)/shard_map/basis/pallas_call | solution.py:62
  3.0 5.6 %all-to-all-start = ((bf16[16,2,64,128]{3,2,1,0:T(8,128)(2,1)}), bf16[16,2,64,128]{3,2,1,0:T(8,128)(2,1)S(1)}, u32[]{:S(2)}, u32[]{:S(2)}) async-start(bf16[16,2,64,128]{3,2,1,0:T(8,128)(2,1)} %get-tuple-element.16), calls=%async_computation | async-start | bytes 1048576 | tf_op jit(solution)/shard_map/all_to_all | solution.py:524
  8.6 0.7 concatenate.10.at_ref.at
  9.4 10.1 %all-to-all-done.rows_ref = bf16[16,2,64,128]{3,2,1,0:T(8,128)(2,1)S(1)} async-done(((bf16[16,2,64,128]{3,2,1,0:T(8,128)(2,1)}), bf16[16,2,64,128]{3,2,1,0:T(8,128)(2,1)S(1)}, u32[]{:S(2)}, u32[]{:S(2)}) %all-to-all-start) | async-done | bytes 524320 | tf_op jit(solution)/shard_map/all_to_all | solution.py:524
  19.4 1.8 %gathered.1 = bf16[8,4,2,64,128]{4,3,2,1,0:T(8,128)(2,1)} custom-call(s32[35]{0:T(128)S(1)} %concatenate.10.at_ref.at, bf16[16,2,64,128]{3,2,1,0:T(8,128)(2,1)S(1)} %all-to-all-done.rows_ref), custom_call_target="tpu_custom_call" | custom-call | tf_op jit(solution)/shard_map/gathered/pallas_call | solution.py:102
  21.3 24.1 %all_to_all.15.refs_1_.refs_2_ = bf16[8,4,2,64,128]{4,3,2,1,0:T(8,128)(2,1)S(1)} all-to-all(bf16[8,4,2,64,128]{4,3,2,1,0:T(8,128)(2,1)} %gathered.1), channel_id=1, replica_groups=mesh['blk'=16,'grp'=8] {'grp'}, dimensions={0} | all-to-all | bytes 2097152 | tf_op jit(solution)/shard_map/all_to_all | solution.py:524
  45.4 0.0 collective-permute-start
  45.4 0.9 collective-permute-start.1
  46.2 7.6 %shard_map.68.refs_0_ = bf16[1,2,1024,1024]{3,2,1,0:T(8,128)(2,1)} custom-call(s32[35]{0:T(128)S(1)} %concatenate.10.at_ref.at, s32[3,16,1024]{2,1,0:T(8,128)} %coords_ref.5), custom_call_target="tpu_custom_call" | custom-call | flops 31457280 | bytes 4194304 | tf_op jit(solution)/shard_map/pallas_call | solution.py:197
  53.8 13.3 %shard_map.69.refs_1_ = bf16[2,2,1024,1024]{3,2,1,0:T(8,128)(2,1)} custom-call(s32[35]{0:T(128)S(1)} %concatenate.10.at_ref.at, s32[3,16,1024]{2,1,0:T(8,128)} %coords_ref.5), custom_call_target="tpu_custom_call" | custom-call | flops 62914560 | bytes 8388608 | tf_op jit(solution)/shard_map/pallas_call | solution.py:197
  67.1 0.0 copy-start.1
  67.1 6.1 %shard_map.70 = (bf16[1,2,1024,1024]{3,2,1,0:T(8,128)(2,1)S(1)}, bf16[1,2,1024,1024]{3,2,1,0:T(8,128)(2,1)S(1)}, bf16[2,2,1024,1024]{3,2,1,0:T(8,128)(2,1)S(1)}) custom-call(s32[35]{0:T(128)S(1)} %concatenate.10.at_ref.at, s32[3,16,1024]{2,1,0:T(8,128)} %coords_ref.5, bf16[1,2,1024,1024]{3,2,1,0:T(8,128)(2,1)} %shard_map.68.refs_0_, ...), custom_call_target="tpu_custom_call" | custom-call | flops 31457280 | bytes 4194304 | tf_op jit(solution)/shard_map/pallas_call | solution.py:197
  73.2 0.0 collective-permute-done.1.refs_5_
  73.2 0.6 collective-permute-start.2
  73.9 0.0 copy-done.1
  73.9 6.6 %collective-permute-done.2.refs_6_ = bf16[2,2,128,128]{3,2,1,0:T(8,128)(2,1)S(1)} collective-permute-done((bf16[2,2,128,128]{3,2,1,0:T(8,128)(2,1)S(1)}, bf16[2,2,128,128]{3,2,1,0:T(8,128)(2,1)S(1)}, u32[]{:S(2)}, u32[]{:S(2)}) %collective-permute-start.2) | collective-permute-done | bytes 131104 | tf_op jit(solution)/shard_map/ppermute | solution.py:534
  80.5 0.6 collective-permute-start.3
  81.1 0.0 collective-permute-done.refs_2_.refs_3_
  81.1 5.2 %shard_map.71.refs_8_.first_ref = f32[2,128,256]{2,1,0:T(8,128)S(1)} custom-call(s32[35]{0:T(128)S(1)} %concatenate.10.at_ref.at, bf16[2,2,1024,1024]{3,2,1,0:T(8,128)(2,1)S(1)} %get-tuple-element.18.refs_0_, bf16[8,4,2,64,128]{4,3,2,1,0:T(8,128)(2,1)S(1)} %all_to_all.15.refs_1_.refs_2_, bf16[8,4,2,64,128]{4,3,2,1,0:T(8,128)(2,1)S(1)} %collective-permute-done.refs_2_.refs_3_), custom_call_target="tpu_custom_call" | custom-call | flops 4294967296 | bytes 8388608 | tf_op jit(solution)/shard_map/pallas_call | solution.py:315
  86.4 0.1 collective-permute-start.4
  86.4 1.7 %collective-permute-done.3.refs_7_ = bf16[4,2,128,128]{3,2,1,0:T(8,128)(2,1)S(1)} collective-permute-done((bf16[4,2,128,128]{3,2,1,0:T(8,128)(2,1)S(1)}, bf16[4,2,128,128]{3,2,1,0:T(8,128)(2,1)S(1)}, u32[]{:S(2)}, u32[]{:S(2)}) %collective-permute-start.3) | collective-permute-done | bytes 262176 | tf_op jit(solution)/shard_map/ppermute | solution.py:534
  88.2 6.2 %shard_map.72 = (f32[2,128,256]{2,1,0:T(8,128)}, bf16[8,2,128,256]{3,2,1,0:T(8,128)(2,1)}, bf16[2,2,128,128]{3,2,1,0:T(8,128)(2,1)S(1)}) custom-call(s32[35]{0:T(128)S(1)} %concatenate.10.at_ref.at, bf16[1,2,1024,1024]{3,2,1,0:T(8,128)(2,1)S(1)} %get-tuple-element.14.refs_0_, bf16[1,2,1024,1024]{3,2,1,0:T(8,128)(2,1)S(1)} %get-tuple-element.15.refs_1_, ...), custom_call_target="tpu_custom_call" | custom-call | flops 4294967296 | bytes 8388608 | tf_op jit(solution)/shard_map/pallas_call | solution.py:315
  94.3 2.7 %collective-permute-start.5 = (bf16[2,2,128,128]{3,2,1,0:T(8,128)(2,1)S(1)}, bf16[2,2,128,128]{3,2,1,0:T(8,128)(2,1)S(1)}, u32[]{:S(2)}, u32[]{:S(2)}) collective-permute-start(bf16[2,2,128,128]{3,2,1,0:T(8,128)(2,1)S(1)} %get-tuple-element.24), channel_id=1, source_target_pairs={{0,1},{1,0},{2,3},{3,2},{4,5},{5,4},{6,7},{7,6},{8,9},{9,8},{10,11... | collective-permute-start | bytes 393224 | tf_op jit(solution)/shard_map/ppermute | solution.py:553
  97.0 3.6 %all-to-all-start.2 = ((bf16[8,2,128,256]{3,2,1,0:T(8,128)(2,1)}), bf16[8,2,128,256]{3,2,1,0:T(8,128)(2,1)S(1)}, u32[]{:S(2)}, u32[]{:S(2)}) async-start(bf16[8,2,128,256]{3,2,1,0:T(8,128)(2,1)} %get-tuple-element.25), calls=%async_computation.2 | async-start | bytes 2097152 | tf_op jit(solution)/shard_map/all_to_all | solution.py:524
  100.6 0.2 collective-permute-done.5
  100.8 0.1 broadcast_select_fusion
  100.9 1.6 %collective-permute-start.6 = (bf16[2,2,128,128]{3,2,1,0:T(8,128)(2,1)S(1)}, bf16[2,2,128,128]{3,2,1,0:T(8,128)(2,1)S(1)}, u32[]{:S(2)}, u32[]{:S(2)}) collective-permute-start(bf16[2,2,128,128]{3,2,1,0:T(8,128)(2,1)S(1)} %broadcast_select_fusion), channel_id=1, source_target_pairs={{0,4},{1,5},{2,6},{3,7},{4,0},{5,1},{6,2},{7,3},{8,12},{9,13},{10,... | collective-permute-start | bytes 393224 | tf_op jit(solution)/shard_map/ppermute | solution.py:553
  102.4 0.0 collective-permute-done.4.second_ref
  102.4 8.7 %shard_map.73 = (f32[2,256,128]{2,1,0:T(8,128)S(1)}, f32[2,256,128]{2,1,0:T(8,128)S(1)}) custom-call(s32[35]{0:T(128)S(1)} %concatenate.10.at_ref.at, f32[2,128,256]{2,1,0:T(8,128)S(1)} %shard_map.71.refs_8_.first_ref, f32[2,128,256]{2,1,0:T(8,128)S(1)} %collective-permute-done.4.second_ref), custom_call_target="tpu_custom_call" | custom-call | flops 6000000000 | bytes 1048576 | tf_op jit(solution)/shard_map/pallas_call | solution.py:438
  111.1 0.0 collective-permute-done.6
  111.1 0.1 broadcast_select_fusion.1
  111.2 1.1 collective-permute-start.7
  112.3 8.8 %shard_map.74 = (f32[2,256,128]{2,1,0:T(8,128)S(1)}, f32[2,256,128]{2,1,0:T(8,128)S(1)}) custom-call(s32[35]{0:T(128)S(1)} %concatenate.10.at_ref.at, f32[2,256,128]{2,1,0:T(8,128)S(1)} %get-tuple-element.20.first_ref, f32[2,256,128]{2,1,0:T(8,128)S(1)} %get-tuple-element.21.second_ref), custom_call_target="tpu_custom_call" | custom-call | flops 6000000000 | bytes 1048576 | tf_op jit(solution)/shard_map/pallas_call | solution.py:438
  121.1 0.0 all-to-all-done.2.row_ref
  121.1 0.7 pivot_tiles.1.mine_ref
  121.8 0.0 copy-start
  121.8 0.1 collective-permute-start.8
  121.9 0.0 collective-permute-done.7
  121.9 0.1 broadcast_select_fusion.2.c_ref
  122.0 0.4 pivot_columns.1.x_ref
  122.4 1.0 collective-permute-done.8.other_ref
  123.4 0.0 copy-done
  123.4 1.6 %schur.1 = f32[2,128,256]{2,1,0:T(8,128)} custom-call(s32[35]{0:T(128)S(1)} %concatenate.10.at_ref.at, f32[128,512]{1,0:T(8,128)S(1)} %pivot_columns.1.x_ref, bf16[2,2,128,256]{3,2,1,0:T(8,128)(2,1)S(1)} %pivot_tiles.1.mine_ref, bf16[2,2,128,256]{3,2,1,0:T(8,128)(2,1)S(1)} %collective-permute-done.8.other_ref, f32[2,128,256]{2,1,0:T(8,128)S(1)} %copy-done), custom_call_target="tpu_custom_call" | custom-call | tf_op jit(solution)/shard_map/schur/pallas_call | solution.py:503
  (4 shorter events, 0.1 us)
Async XLA Ops:
  3.0 16.4 %all-to-all-start = ((bf16[16,2,64,128]{3,2,1,0:T(8,128)(2,1)}), bf16[16,2,64,128]{3,2,1,0:T(8,128)(2,1)S(1)}, u32[]{:S(2)}, u32[]{:S(2)}) async-start(bf16[16,2,64,128]{3,2,1,0:T(8,128)(2,1)} %get-tuple-element.16), calls=%async_computation | async-start | bytes 1048576 | tf_op jit(solution)/shard_map/all_to_all | solution.py:524
  45.4 35.8 %collective-permute-start = (bf16[8,4,2,64,128]{4,3,2,1,0:T(8,128)(2,1)S(1)}, bf16[8,4,2,64,128]{4,3,2,1,0:T(8,128)(2,1)S(1)}, u32[]{:S(2)}, u32[]{:S(2)}) collective-permute-start(bf16[8,4,2,64,128]{4,3,2,1,0:T(8,128)(2,1)S(1)} %all_to_all.15.refs_1_.refs_2_), channel_id=1, source_target_pairs={{0,8},{8,0},{16,24},{24,16},{32,40},{40,32},{48,56},{56,48},{64,72... | collective-permute-start | bytes 3145736 | tf_op jit(solution)/shard_map/ppermute | solution.py:544
  45.4 27.8 %collective-permute-start.1 = (bf16[1,2,128,128]{3,2,1,0:T(8,128)(2,1)S(1)}, bf16[1,2,128,128]{3,2,1,0:T(8,128)(2,1)S(1)}, u32[]{:S(2)}, u32[]{:S(2)}) collective-permute-start(bf16[1,2,128,128]{3,2,1,0:T(8,128)(2,1)S(1)} %get-tuple-element.17.refs_4_), channel_id=1, source_target_pairs={{0,1},{1,0},{2,3},{3,2},{4,5},{5,4},{6,7},{7,6},{8,9},{9,8},{10,11... | collective-permute-start | bytes 196616 | tf_op jit(solution)/shard_map/ppermute | solution.py:534
  67.1 6.8 %copy-start.1 = (s32[16]{0:T(128)S(1)}, s32[16]{0:T(128)}, u32[]{:S(2)}) copy-start(s32[16]{0:T(128)} %param.9) | copy-start | bytes 196
  73.2 7.2 %collective-permute-start.2 = (bf16[2,2,128,128]{3,2,1,0:T(8,128)(2,1)S(1)}, bf16[2,2,128,128]{3,2,1,0:T(8,128)(2,1)S(1)}, u32[]{:S(2)}, u32[]{:S(2)}) collective-permute-start(bf16[2,2,128,128]{3,2,1,0:T(8,128)(2,1)S(1)} %pad_maximum_fusion.1), channel_id=1, source_target_pairs={{0,4},{1,5},{2,6},{3,7},{4,0},{5,1},{6,2},{7,3},{8,12},{9,13},{10,... | collective-permute-start | bytes 393224 | tf_op jit(solution)/shard_map/ppermute | solution.py:534
  80.5 7.7 %collective-permute-start.3 = (bf16[4,2,128,128]{3,2,1,0:T(8,128)(2,1)S(1)}, bf16[4,2,128,128]{3,2,1,0:T(8,128)(2,1)S(1)}, u32[]{:S(2)}, u32[]{:S(2)}) collective-permute-start(bf16[4,2,128,128]{3,2,1,0:T(8,128)(2,1)S(1)} %pad_maximum_fusion), channel_id=1, source_target_pairs={{0,2},{1,3},{2,0},{3,1},{4,6},{5,7},{6,4},{7,5},{8,10},{9,11},{10,... | collective-permute-start | bytes 786440 | tf_op jit(solution)/shard_map/ppermute | solution.py:534
  86.4 16.1 %collective-permute-start.4 = (f32[2,128,256]{2,1,0:T(8,128)S(1)}, f32[2,128,256]{2,1,0:T(8,128)S(1)}, u32[]{:S(2)}, u32[]{:S(2)}) collective-permute-start(f32[2,128,256]{2,1,0:T(8,128)S(1)} %shard_map.71.refs_8_.first_ref), channel_id=1, source_target_pairs={{0,8},{8,0},{16,24},{24,16},{32,40},{40,32},{48,56},{56,48},{64,72... | collective-permute-start | bytes 786440 | tf_op jit(solution)/shard_map/ppermute | solution.py:547
  94.3 6.5 %collective-permute-start.5 = (bf16[2,2,128,128]{3,2,1,0:T(8,128)(2,1)S(1)}, bf16[2,2,128,128]{3,2,1,0:T(8,128)(2,1)S(1)}, u32[]{:S(2)}, u32[]{:S(2)}) collective-permute-start(bf16[2,2,128,128]{3,2,1,0:T(8,128)(2,1)S(1)} %get-tuple-element.24), channel_id=1, source_target_pairs={{0,1},{1,0},{2,3},{3,2},{4,5},{5,4},{6,7},{7,6},{8,9},{9,8},{10,11... | collective-permute-start | bytes 393224 | tf_op jit(solution)/shard_map/ppermute | solution.py:553
  97.0 24.1 %all-to-all-start.2 = ((bf16[8,2,128,256]{3,2,1,0:T(8,128)(2,1)}), bf16[8,2,128,256]{3,2,1,0:T(8,128)(2,1)S(1)}, u32[]{:S(2)}, u32[]{:S(2)}) async-start(bf16[8,2,128,256]{3,2,1,0:T(8,128)(2,1)} %get-tuple-element.25), calls=%async_computation.2 | async-start | bytes 2097152 | tf_op jit(solution)/shard_map/all_to_all | solution.py:524
  100.9 10.3 %collective-permute-start.6 = (bf16[2,2,128,128]{3,2,1,0:T(8,128)(2,1)S(1)}, bf16[2,2,128,128]{3,2,1,0:T(8,128)(2,1)S(1)}, u32[]{:S(2)}, u32[]{:S(2)}) collective-permute-start(bf16[2,2,128,128]{3,2,1,0:T(8,128)(2,1)S(1)} %broadcast_select_fusion), channel_id=1, source_target_pairs={{0,4},{1,5},{2,6},{3,7},{4,0},{5,1},{6,2},{7,3},{8,12},{9,13},{10,... | collective-permute-start | bytes 393224 | tf_op jit(solution)/shard_map/ppermute | solution.py:553
  111.2 10.7 %collective-permute-start.7 = (bf16[2,2,128,128]{3,2,1,0:T(8,128)(2,1)S(1)}, bf16[2,2,128,128]{3,2,1,0:T(8,128)(2,1)S(1)}, u32[]{:S(2)}, u32[]{:S(2)}) collective-permute-start(bf16[2,2,128,128]{3,2,1,0:T(8,128)(2,1)S(1)} %broadcast_select_fusion.1), channel_id=1, source_target_pairs={{0,2},{1,3},{2,0},{3,1},{4,6},{5,7},{6,4},{7,5},{8,10},{9,11},{10,... | collective-permute-start | bytes 393224 | tf_op jit(solution)/shard_map/ppermute | solution.py:553
  121.8 1.6 %copy-start = (f32[2,128,256]{2,1,0:T(8,128)S(1)}, f32[2,128,256]{2,1,0:T(8,128)}, u32[]{:S(2)}) copy-start(f32[2,128,256]{2,1,0:T(8,128)} %get-tuple-element.12.r_ref) | copy-start | bytes 786436
  121.8 1.6 %collective-permute-start.8 = (bf16[2,2,128,256]{3,2,1,0:T(8,128)(2,1)S(1)}, bf16[2,2,128,256]{3,2,1,0:T(8,128)(2,1)S(1)}, u32[]{:S(2)}, u32[]{:S(2)}) collective-permute-start(bf16[2,2,128,256]{3,2,1,0:T(8,128)(2,1)S(1)} %pivot_tiles.1.mine_ref), channel_id=1, source_target_pairs={{0,8},{8,0},{16,24},{24,16},{32,40},{40,32},{48,56},{56,48},{64,72... | collective-permute-start | bytes 786440 | tf_op jit(solution)/shard_map/ppermute | solution.py:557

commit v9 on v8

--- a/solution.py
+++ b/solution.py
@@ -80,31 +80,28 @@
     return slot
 
 
-def gather_kernel(at_ref, rows_ref, out_ref, slot_ref, sems):
+def gather_kernel(at_ref, rows_ref, out_ref, slot_ref):
     blocks = rows_ref.shape[0]
     for s in range(blocks):
         slot_ref[at_ref[3 + s]] = s
     groups, entries = out_ref.shape[:2]
     slabs = entries - PANELS
-    copies = []
+    for p in range(PANELS):
+        value = rows_ref[slot_ref[at_ref[3 + blocks + p]]]
+        for g in range(groups):
+            out_ref[g, slabs + p] = value
     for g in range(groups):
-        for e in range(entries):
-            block = g * slabs + e if e < slabs else at_ref[3 + blocks + e - slabs]
-            copy = pltpu.make_async_copy(rows_ref.at[slot_ref[block]], out_ref.at[g, e], sems.at[g, e])
-            copy.start()
-            copies.append(copy)
-    for copy in copies:
-        copy.wait()
+        for e in range(slabs):
+            out_ref[g, e] = rows_ref[slot_ref[g * slabs + e]]
 
 
 def gathered(at, rows, groups, slabs):
-    entries = slabs + PANELS
     return pl.pallas_call(
         gather_kernel,
-        out_shape=pltpu.HBM((groups, entries, *rows.shape[1:]), rows.dtype),
+        out_shape=jax.ShapeDtypeStruct((groups, slabs + PANELS, *rows.shape[1:]), rows.dtype),
         in_specs=[SMEM, VMEM],
-        out_specs=pl.BlockSpec(memory_space=pltpu.HBM),
-        scratch_shapes=[pltpu.SMEM((rows.shape[0],), i32), pltpu.SemaphoreType.DMA((groups, entries))],
+        out_specs=VMEM,
+        scratch_shapes=[pltpu.SMEM((rows.shape[0],), i32)],
         compiler_params=pltpu.CompilerParams(vmem_limit_bytes=8 * MB),
         name="gathered",
     )(at, rows)

time: 126 us -> 125 us (level)
  transfers between devices with their start and end apart: 11 -> 11, of which waited for: 5 -> 5; matrix products, arithmetic and copies ran while one was open for 1% -> 1% of each run, Pallas kernels for 45% -> 46%
where the time goes in v9:
time: 125 us; the launch traced here: 124 us
  Pallas kernels  61.5 us (49%)
  blocking collectives  23.9 us (19%)
  waiting for transfers between devices  19.6 us (16%)
  starting transfers between devices  16.8 us (13%)
    pallas_call x3, Pallas kernels, green_tiles(): pl.pallas_call(functools.partial(green_kernel, first, whole, len(carry)),...  26.9 us
    all_to_all x1, blocking collectives, spread(): lax.all_to_all(x, axis, split_axis=0, concat_axis=0, tiled=True, axis_ind...  23.9 us
    pallas_call x2, Pallas kernels, pivot_exchange(): pl.pallas_call(functools.partial(inverse_kernel, kb), out_shape=(part, pa...  17.5 us
    pallas_call x2, Pallas kernels, couplings(): pl.pallas_call(functools.partial(coupling_kernel, pivot, 3 + blocks, len(...  11.4 us
    all_to_all x2, waiting for transfers between devices, spread(): lax.all_to_all(x, axis, split_axis=0, concat_axis=0, tiled=True, axis_ind...  10.1 us
    all_to_all x2, starting transfers between devices, spread(): lax.all_to_all(x, axis, split_axis=0, concat_axis=0, tiled=True, axis_ind...  9.17 us
    ppermute x3, waiting for transfers between devices, on_device(): lax.ppermute(held, 'grp', [(g, g ^ bit) for g in range(grp_size)])  8.28 us
    ppermute x3, starting transfers between devices, on_device(): came = lax.ppermute(column, 'grp', [(g, g ^ bit) for g in range(grp_size)])  5.33 us
  transfers between devices with their start and end apart: 11, of which 5 were waited for; matrix products, arithmetic and copies ran while one was open for 1% of the time, Pallas kernels for 46%

profile of v9, /device:TPU:0, one launch (start us, length us, event | category | flops | bytes accessed | tf_op | source)
XLA Modules:
  0.0 123.7 jit_solution(2092486837045451710)
XLA Ops:
  0.6 2.3 %basis.1 = (bf16[1,2,128,128]{3,2,1,0:T(8,128)(2,1)S(1)}, bf16[16,2,64,128]{3,2,1,0:T(8,128)(2,1)}) custom-call(bf16[2,1,128,1024]{3,2,1,0:T(8,128)(2,1)} %inv_ref.1, bf16[2,1,1024,128]{3,2,1,0:T(8,128)(2,1)} %exc_ref.1), custom_call_target="tpu_custom_call" | custom-call | tf_op jit(solution)/shard_map/basis/pallas_call | solution.py:62
  3.0 5.6 %all-to-all-start = ((bf16[16,2,64,128]{3,2,1,0:T(8,128)(2,1)}), bf16[16,2,64,128]{3,2,1,0:T(8,128)(2,1)S(1)}, u32[]{:S(2)}, u32[]{:S(2)}) async-start(bf16[16,2,64,128]{3,2,1,0:T(8,128)(2,1)} %get-tuple-element.16), calls=%async_computation | async-start | bytes 1048576 | tf_op jit(solution)/shard_map/all_to_all | solution.py:521
  8.6 0.7 concatenate.10.at_ref.at
  9.4 10.1 %all-to-all-done.rows_ref = bf16[16,2,64,128]{3,2,1,0:T(8,128)(2,1)S(1)} async-done(((bf16[16,2,64,128]{3,2,1,0:T(8,128)(2,1)}), bf16[16,2,64,128]{3,2,1,0:T(8,128)(2,1)S(1)}, u32[]{:S(2)}, u32[]{:S(2)}) %all-to-all-start) | async-done | bytes 524320 | tf_op jit(solution)/shard_map/all_to_all | solution.py:521
  19.4 0.7 gathered.1
  20.1 23.9 %all_to_all.15.refs_1_.refs_2_ = bf16[8,4,2,64,128]{4,3,2,1,0:T(8,128)(2,1)S(1)} all-to-all(bf16[8,4,2,64,128]{4,3,2,1,0:T(8,128)(2,1)S(1)} %gathered.1), channel_id=1, replica_groups=mesh['blk'=16,'grp'=8] {'grp'}, dimensions={0} | all-to-all | bytes 2097152 | tf_op jit(solution)/shard_map/all_to_all | solution.py:521
  44.0 0.0 collective-permute-start
  44.0 0.9 collective-permute-start.1
  44.8 7.6 %shard_map.68.refs_0_ = bf16[1,2,1024,1024]{3,2,1,0:T(8,128)(2,1)} custom-call(s32[35]{0:T(128)S(1)} %concatenate.10.at_ref.at, s32[3,16,1024]{2,1,0:T(8,128)} %coords_ref.5), custom_call_target="tpu_custom_call" | custom-call | flops 31457280 | bytes 4194304 | tf_op jit(solution)/shard_map/pallas_call | solution.py:194
  52.4 13.3 %shard_map.69.refs_1_ = bf16[2,2,1024,1024]{3,2,1,0:T(8,128)(2,1)} custom-call(s32[35]{0:T(128)S(1)} %concatenate.10.at_ref.at, s32[3,16,1024]{2,1,0:T(8,128)} %coords_ref.5), custom_call_target="tpu_custom_call" | custom-call | flops 62914560 | bytes 8388608 | tf_op jit(solution)/shard_map/pallas_call | solution.py:194
  65.7 0.0 copy-start.1
  65.7 6.1 %shard_map.70 = (bf16[1,2,1024,1024]{3,2,1,0:T(8,128)(2,1)S(1)}, bf16[1,2,1024,1024]{3,2,1,0:T(8,128)(2,1)S(1)}, bf16[2,2,1024,1024]{3,2,1,0:T(8,128)(2,1)S(1)}) custom-call(s32[35]{0:T(128)S(1)} %concatenate.10.at_ref.at, s32[3,16,1024]{2,1,0:T(8,128)} %coords_ref.5, bf16[1,2,1024,1024]{3,2,1,0:T(8,128)(2,1)} %shard_map.68.refs_0_, ...), custom_call_target="tpu_custom_call" | custom-call | flops 31457280 | bytes 4194304 | tf_op jit(solution)/shard_map/pallas_call | solution.py:194
  71.8 0.0 collective-permute-done.1.refs_5_
  71.8 0.6 collective-permute-start.2
  72.5 0.0 copy-done.1
  72.5 6.6 %collective-permute-done.2.refs_6_ = bf16[2,2,128,128]{3,2,1,0:T(8,128)(2,1)S(1)} collective-permute-done((bf16[2,2,128,128]{3,2,1,0:T(8,128)(2,1)S(1)}, bf16[2,2,128,128]{3,2,1,0:T(8,128)(2,1)S(1)}, u32[]{:S(2)}, u32[]{:S(2)}) %collective-permute-start.2) | collective-permute-done | bytes 131104 | tf_op jit(solution)/shard_map/ppermute | solution.py:531
  79.1 0.6 collective-permute-start.3
  79.7 0.0 collective-permute-done.refs_2_.refs_3_
  79.7 5.2 %shard_map.71.refs_8_.first_ref = f32[2,128,256]{2,1,0:T(8,128)S(1)} custom-call(s32[35]{0:T(128)S(1)} %concatenate.10.at_ref.at, bf16[2,2,1024,1024]{3,2,1,0:T(8,128)(2,1)S(1)} %get-tuple-element.18.refs_0_, bf16[8,4,2,64,128]{4,3,2,1,0:T(8,128)(2,1)S(1)} %all_to_all.15.refs_1_.refs_2_, bf16[8,4,2,64,128]{4,3,2,1,0:T(8,128)(2,1)S(1)} %collective-permute-done.refs_2_.refs_3_), custom_call_target="tpu_custom_call" | custom-call | flops 4294967296 | bytes 8388608 | tf_op jit(solution)/shard_map/pallas_call | solution.py:312
  84.9 0.1 collective-permute-start.4
  85.0 1.7 %collective-permute-done.3.refs_7_ = bf16[4,2,128,128]{3,2,1,0:T(8,128)(2,1)S(1)} collective-permute-done((bf16[4,2,128,128]{3,2,1,0:T(8,128)(2,1)S(1)}, bf16[4,2,128,128]{3,2,1,0:T(8,128)(2,1)S(1)}, u32[]{:S(2)}, u32[]{:S(2)}) %collective-permute-start.3) | collective-permute-done | bytes 262176 | tf_op jit(solution)/shard_map/ppermute | solution.py:531
  86.8 6.2 %shard_map.72 = (f32[2,128,256]{2,1,0:T(8,128)}, bf16[8,2,128,256]{3,2,1,0:T(8,128)(2,1)}, bf16[2,2,128,128]{3,2,1,0:T(8,128)(2,1)S(1)}) custom-call(s32[35]{0:T(128)S(1)} %concatenate.10.at_ref.at, bf16[1,2,1024,1024]{3,2,1,0:T(8,128)(2,1)S(1)} %get-tuple-element.14.refs_0_, bf16[1,2,1024,1024]{3,2,1,0:T(8,128)(2,1)S(1)} %get-tuple-element.15.refs_1_, ...), custom_call_target="tpu_custom_call" | custom-call | flops 4294967296 | bytes 8388608 | tf_op jit(solution)/shard_map/pallas_call | solution.py:312
  92.9 2.7 %collective-permute-start.5 = (bf16[2,2,128,128]{3,2,1,0:T(8,128)(2,1)S(1)}, bf16[2,2,128,128]{3,2,1,0:T(8,128)(2,1)S(1)}, u32[]{:S(2)}, u32[]{:S(2)}) collective-permute-start(bf16[2,2,128,128]{3,2,1,0:T(8,128)(2,1)S(1)} %get-tuple-element.24), channel_id=1, source_target_pairs={{0,1},{1,0},{2,3},{3,2},{4,5},{5,4},{6,7},{7,6},{8,9},{9,8},{10,11... | collective-permute-start | bytes 393224 | tf_op jit(solution)/shard_map/ppermute | solution.py:550
  95.6 3.6 %all-to-all-start.2 = ((bf16[8,2,128,256]{3,2,1,0:T(8,128)(2,1)}), bf16[8,2,128,256]{3,2,1,0:T(8,128)(2,1)S(1)}, u32[]{:S(2)}, u32[]{:S(2)}) async-start(bf16[8,2,128,256]{3,2,1,0:T(8,128)(2,1)} %get-tuple-element.25), calls=%async_computation.2 | async-start | bytes 2097152 | tf_op jit(solution)/shard_map/all_to_all | solution.py:521
  99.1 0.2 collective-permute-done.5
  99.4 0.1 broadcast_select_fusion
  99.5 1.5 %collective-permute-start.6 = (bf16[2,2,128,128]{3,2,1,0:T(8,128)(2,1)S(1)}, bf16[2,2,128,128]{3,2,1,0:T(8,128)(2,1)S(1)}, u32[]{:S(2)}, u32[]{:S(2)}) collective-permute-start(bf16[2,2,128,128]{3,2,1,0:T(8,128)(2,1)S(1)} %broadcast_select_fusion), channel_id=1, source_target_pairs={{0,4},{1,5},{2,6},{3,7},{4,0},{5,1},{6,2},{7,3},{8,12},{9,13},{10,... | collective-permute-start | bytes 393224 | tf_op jit(solution)/shard_map/ppermute | solution.py:550
  101.0 0.0 collective-permute-done.4.second_ref
  101.0 8.7 %shard_map.73 = (f32[2,256,128]{2,1,0:T(8,128)S(1)}, f32[2,256,128]{2,1,0:T(8,128)S(1)}) custom-call(s32[35]{0:T(128)S(1)} %concatenate.10.at_ref.at, f32[2,128,256]{2,1,0:T(8,128)S(1)} %shard_map.71.refs_8_.first_ref, f32[2,128,256]{2,1,0:T(8,128)S(1)} %collective-permute-done.4.second_ref), custom_call_target="tpu_custom_call" | custom-call | flops 6000000000 | bytes 1048576 | tf_op jit(solution)/shard_map/pallas_call | solution.py:435
  109.7 0.0 collective-permute-done.6
  109.7 0.1 broadcast_select_fusion.1
  109.8 1.1 collective-permute-start.7
  111.0 8.8 %shard_map.74 = (f32[2,256,128]{2,1,0:T(8,128)S(1)}, f32[2,256,128]{2,1,0:T(8,128)S(1)}) custom-call(s32[35]{0:T(128)S(1)} %concatenate.10.at_ref.at, f32[2,256,128]{2,1,0:T(8,128)S(1)} %get-tuple-element.20.first_ref, f32[2,256,128]{2,1,0:T(8,128)S(1)} %get-tuple-element.21.second_ref), custom_call_target="tpu_custom_call" | custom-call | flops 6000000000 | bytes 1048576 | tf_op jit(solution)/shard_map/pallas_call | solution.py:435
  119.8 0.0 all-to-all-done.2.row_ref
  119.8 0.7 pivot_tiles.1.mine_ref
  120.4 0.0 copy-start
  120.4 0.1 collective-permute-start.8
  120.5 0.0 collective-permute-done.7
  120.5 0.1 broadcast_select_fusion.2.c_ref
  120.6 0.4 pivot_columns.1.x_ref
  121.1 1.0 collective-permute-done.8.other_ref
  122.1 0.0 copy-done
  122.1 1.6 %schur.1 = f32[2,128,256]{2,1,0:T(8,128)} custom-call(s32[35]{0:T(128)S(1)} %concatenate.10.at_ref.at, f32[128,512]{1,0:T(8,128)S(1)} %pivot_columns.1.x_ref, bf16[2,2,128,256]{3,2,1,0:T(8,128)(2,1)S(1)} %pivot_tiles.1.mine_ref, bf16[2,2,128,256]{3,2,1,0:T(8,128)(2,1)S(1)} %collective-permute-done.8.other_ref, f32[2,128,256]{2,1,0:T(8,128)S(1)} %copy-done), custom_call_target="tpu_custom_call" | custom-call | tf_op jit(solution)/shard_map/schur/pallas_call | solution.py:500
  (4 shorter events, 0.1 us)
Async XLA Ops:
  3.0 16.4 %all-to-all-start = ((bf16[16,2,64,128]{3,2,1,0:T(8,128)(2,1)}), bf16[16,2,64,128]{3,2,1,0:T(8,128)(2,1)S(1)}, u32[]{:S(2)}, u32[]{:S(2)}) async-start(bf16[16,2,64,128]{3,2,1,0:T(8,128)(2,1)} %get-tuple-element.16), calls=%async_computation | async-start | bytes 1048576 | tf_op jit(solution)/shard_map/all_to_all | solution.py:521
  44.0 35.7 %collective-permute-start = (bf16[8,4,2,64,128]{4,3,2,1,0:T(8,128)(2,1)S(1)}, bf16[8,4,2,64,128]{4,3,2,1,0:T(8,128)(2,1)S(1)}, u32[]{:S(2)}, u32[]{:S(2)}) collective-permute-start(bf16[8,4,2,64,128]{4,3,2,1,0:T(8,128)(2,1)S(1)} %all_to_all.15.refs_1_.refs_2_), channel_id=1, source_target_pairs={{0,8},{8,0},{16,24},{24,16},{32,40},{40,32},{48,56},{56,48},{64,72... | collective-permute-start | bytes 3145736 | tf_op jit(solution)/shard_map/ppermute | solution.py:541
  44.0 27.8 %collective-permute-start.1 = (bf16[1,2,128,128]{3,2,1,0:T(8,128)(2,1)S(1)}, bf16[1,2,128,128]{3,2,1,0:T(8,128)(2,1)S(1)}, u32[]{:S(2)}, u32[]{:S(2)}) collective-permute-start(bf16[1,2,128,128]{3,2,1,0:T(8,128)(2,1)S(1)} %get-tuple-element.17.refs_4_), channel_id=1, source_target_pairs={{0,1},{1,0},{2,3},{3,2},{4,5},{5,4},{6,7},{7,6},{8,9},{9,8},{10,11... | collective-permute-start | bytes 196616 | tf_op jit(solution)/shard_map/ppermute | solution.py:531
  65.7 6.7 %copy-start.1 = (s32[16]{0:T(128)S(1)}, s32[16]{0:T(128)}, u32[]{:S(2)}) copy-start(s32[16]{0:T(128)} %param.9) | copy-start | bytes 196
  71.8 7.2 %collective-permute-start.2 = (bf16[2,2,128,128]{3,2,1,0:T(8,128)(2,1)S(1)}, bf16[2,2,128,128]{3,2,1,0:T(8,128)(2,1)S(1)}, u32[]{:S(2)}, u32[]{:S(2)}) collective-permute-start(bf16[2,2,128,128]{3,2,1,0:T(8,128)(2,1)S(1)} %pad_maximum_fusion.1), channel_id=1, source_target_pairs={{0,4},{1,5},{2,6},{3,7},{4,0},{5,1},{6,2},{7,3},{8,12},{9,13},{10,... | collective-permute-start | bytes 393224 | tf_op jit(solution)/shard_map/ppermute | solution.py:531
  79.1 7.7 %collective-permute-start.3 = (bf16[4,2,128,128]{3,2,1,0:T(8,128)(2,1)S(1)}, bf16[4,2,128,128]{3,2,1,0:T(8,128)(2,1)S(1)}, u32[]{:S(2)}, u32[]{:S(2)}) collective-permute-start(bf16[4,2,128,128]{3,2,1,0:T(8,128)(2,1)S(1)} %pad_maximum_fusion), channel_id=1, source_target_pairs={{0,2},{1,3},{2,0},{3,1},{4,6},{5,7},{6,4},{7,5},{8,10},{9,11},{10,... | collective-permute-start | bytes 786440 | tf_op jit(solution)/shard_map/ppermute | solution.py:531
  84.9 16.1 %collective-permute-start.4 = (f32[2,128,256]{2,1,0:T(8,128)S(1)}, f32[2,128,256]{2,1,0:T(8,128)S(1)}, u32[]{:S(2)}, u32[]{:S(2)}) collective-permute-start(f32[2,128,256]{2,1,0:T(8,128)S(1)} %shard_map.71.refs_8_.first_ref), channel_id=1, source_target_pairs={{0,8},{8,0},{16,24},{24,16},{32,40},{40,32},{48,56},{56,48},{64,72... | collective-permute-start | bytes 786440 | tf_op jit(solution)/shard_map/ppermute | solution.py:544
  92.9 6.5 %collective-permute-start.5 = (bf16[2,2,128,128]{3,2,1,0:T(8,128)(2,1)S(1)}, bf16[2,2,128,128]{3,2,1,0:T(8,128)(2,1)S(1)}, u32[]{:S(2)}, u32[]{:S(2)}) collective-permute-start(bf16[2,2,128,128]{3,2,1,0:T(8,128)(2,1)S(1)} %get-tuple-element.24), channel_id=1, source_target_pairs={{0,1},{1,0},{2,3},{3,2},{4,5},{5,4},{6,7},{7,6},{8,9},{9,8},{10,11... | collective-permute-start | bytes 393224 | tf_op jit(solution)/shard_map/ppermute | solution.py:550
  95.6 24.2 %all-to-all-start.2 = ((bf16[8,2,128,256]{3,2,1,0:T(8,128)(2,1)}), bf16[8,2,128,256]{3,2,1,0:T(8,128)(2,1)S(1)}, u32[]{:S(2)}, u32[]{:S(2)}) async-start(bf16[8,2,128,256]{3,2,1,0:T(8,128)(2,1)} %get-tuple-element.25), calls=%async_computation.2 | async-start | bytes 2097152 | tf_op jit(solution)/shard_map/all_to_all | solution.py:521
  99.5 10.3 %collective-permute-start.6 = (bf16[2,2,128,128]{3,2,1,0:T(8,128)(2,1)S(1)}, bf16[2,2,128,128]{3,2,1,0:T(8,128)(2,1)S(1)}, u32[]{:S(2)}, u32[]{:S(2)}) collective-permute-start(bf16[2,2,128,128]{3,2,1,0:T(8,128)(2,1)S(1)} %broadcast_select_fusion), channel_id=1, source_target_pairs={{0,4},{1,5},{2,6},{3,7},{4,0},{5,1},{6,2},{7,3},{8,12},{9,13},{10,... | collective-permute-start | bytes 393224 | tf_op jit(solution)/shard_map/ppermute | solution.py:550
  109.8 10.7 %collective-permute-start.7 = (bf16[2,2,128,128]{3,2,1,0:T(8,128)(2,1)S(1)}, bf16[2,2,128,128]{3,2,1,0:T(8,128)(2,1)S(1)}, u32[]{:S(2)}, u32[]{:S(2)}) collective-permute-start(bf16[2,2,128,128]{3,2,1,0:T(8,128)(2,1)S(1)} %broadcast_select_fusion.1), channel_id=1, source_target_pairs={{0,2},{1,3},{2,0},{3,1},{4,6},{5,7},{6,4},{7,5},{8,10},{9,11},{10,... | collective-permute-start | bytes 393224 | tf_op jit(solution)/shard_map/ppermute | solution.py:550
  120.4 1.6 %copy-start = (f32[2,128,256]{2,1,0:T(8,128)S(1)}, f32[2,128,256]{2,1,0:T(8,128)}, u32[]{:S(2)}) copy-start(f32[2,128,256]{2,1,0:T(8,128)} %get-tuple-element.12.r_ref) | copy-start | bytes 786436
  120.4 1.6 %collective-permute-start.8 = (bf16[2,2,128,256]{3,2,1,0:T(8,128)(2,1)S(1)}, bf16[2,2,128,256]{3,2,1,0:T(8,128)(2,1)S(1)}, u32[]{:S(2)}, u32[]{:S(2)}) collective-permute-start(bf16[2,2,128,256]{3,2,1,0:T(8,128)(2,1)S(1)} %pivot_tiles.1.mine_ref), channel_id=1, source_target_pairs={{0,8},{8,0},{16,24},{24,16},{32,40},{40,32},{48,56},{56,48},{64,72... | collective-permute-start | bytes 786440 | tf_op jit(solution)/shard_map/ppermute | solution.py:554
